TPU v7x, 32 devices: a whole 2x2x4 slice. The times are simulated.
32 devices in a mesh: dp: 4 (over z), ctx: 4 (over y, core), tensor: 2 (over x).
Axes of the slice: x: 2, y: 2, z: 4, core: 2. Of those that a mesh axis runs over, the one named last changes fastest.
Arguments:
- tokens: bfloat16 [8192, 4, 1280], P(('ctx', 'tensor'), 'dp'), may hold values from -6 to 6
- segments: int32 [4, 8192], P('dp'), may hold values from 0 to 31, never falling along the last dimension, each value on 1 to 4096 neighbouring positions
- gain_attn: float32 [1280], replicated, may hold values from 0.5 to 1.5
- query_scale: float32 [80], replicated, may hold values from -3 to 3
- w_qkv: bfloat16 [3, 1280, 1280], P(None, ('dp', 'ctx'), 'tensor'), may hold values from -0.15625 to 0.15625
- w_out: bfloat16 [1280, 1280], P('tensor', ('dp', 'ctx')), may hold values from -1 to 1
- gain_mlp: float32 [1280], replicated, may hold values from 0.5 to 1.5
- w_up: bfloat16 [1280, 1280], P(('dp', 'ctx'), 'tensor'), may hold values from -0.15625 to 0.15625
- b_up: float32 [1280], replicated, may hold values from -3 to 3
- w_down: bfloat16 [1280, 1280], P('tensor', ('dp', 'ctx')), may hold values from -0.15625 to 0.15625
- b_down: float32 [1280], replicated, may hold values from -3 to 3
- cotangent: bfloat16 [8192, 4, 1280], P(('ctx', 'tensor'), 'dp'), may hold values from -6 to 6
Outputs:
- outputs: bfloat16 [8192, 4, 1280], P(('ctx', 'tensor'), 'dp')
- grad_inputs: bfloat16 [8192, 4, 1280], P(('ctx', 'tensor'), 'dp')
- grad_w_qkv: float32 [3, 1280, 1280], P(None, ('dp', 'ctx'), 'tensor')
- grad_w_out: float32 [1280, 1280], P('tensor', ('dp', 'ctx'))
- grad_w_up: float32 [1280, 1280], P(('dp', 'ctx'), 'tensor')
- grad_w_down: float32 [1280, 1280], P('tensor', ('dp', 'ctx'))
- grad_gain_attn: float32 [1280], replicated
- grad_query_scale: float32 [80], replicated
- grad_gain_mlp: float32 [1280], replicated
- grad_b_up: float32 [1280], replicated
- grad_b_down: float32 [1280], replicated
Inputs may be any that keep to these rules, and one draw needn't show every extreme that they name: `segments`: along each sequence the ids never fall; a document is a run of equal ids of at most 4096 positions.
All inputs are finite; a program needn't handle non-finite values.
Results may differ from a plain program's by a relative error of at most 0.018.
Values may be sent and summed in bfloat16 or wider, within the bound.
No kernel may reach another device: no remote copies, remote signals or barrier semaphores. Data moves between devices by JAX's collectives and lax.ppermute only.
A program may use at most 768 MiB of HBM per device.

v0:
```python
import math

import jax
import jax.numpy as jnp
from jax import lax
from jax.sharding import PartitionSpec as P

HD = 80
QB = 512


EPSILON = 1e-06
LOG_TWO_E = 1.442695041
NEGATIVE = -1e30


def normalize(values):
    inverse = lax.rsqrt(jnp.mean(values * values, axis=-1, keepdims=True) + EPSILON)
    return (values * inverse, inverse)


def norm_back(grad_norm, unit, inverse, gain):
    grad_unit = grad_norm * gain
    return inverse * (grad_unit - unit * jnp.mean(grad_unit * unit, axis=-1, keepdims=True))


def block_scores(q_block, keys_all, seg_query, seg_all, query_pos):
    raw_scores = jnp.einsum(
        "qshe,kshe->shqk", q_block, keys_all, preferred_element_type=jnp.float32
    )
    key_pos = lax.iota(jnp.int32, keys_all.shape[0])
    allowed = (key_pos[None, None, :] <= query_pos[None, :, None]) & (
        seg_all[:, None, :] == seg_query[:, :, None]
    )
    return jnp.where(allowed[:, None], raw_scores, NEGATIVE)


def attend(queries, keys_all, values_all, segments, offset):
    number = queries.shape[0] // QB

    def one_block(index):
        first = index * QB
        q_block = lax.dynamic_slice_in_dim(queries, first, QB, 0)
        query_pos = offset + first + lax.iota(jnp.int32, QB)
        seg_query = lax.dynamic_slice_in_dim(segments, offset + first, QB, 1)
        scores = block_scores(q_block, keys_all, seg_query, segments, query_pos)
        row_max = jnp.max(scores, axis=-1, keepdims=True)
        exponent = jnp.exp(scores - row_max)
        row_total = jnp.sum(exponent, axis=-1, keepdims=True)
        probs = (exponent / row_total).astype(jnp.bfloat16)
        result = jnp.einsum(
            "shqk,kshe->qshe", probs, values_all, preferred_element_type=jnp.float32
        )
        return (result.astype(jnp.bfloat16), (row_max + jnp.log(row_total))[..., 0])

    results, log_totals = lax.map(one_block, jnp.arange(number, dtype=jnp.int32))
    return (results.reshape(queries.shape), log_totals)


def attend_back(queries, keys_all, values_all, segments, offset, log_totals, grad_mixed):
    number = queries.shape[0] // QB

    def one_block(carry, item):
        grad_keys, grad_values = carry
        index, log_block = item
        first = index * QB
        q_block = lax.dynamic_slice_in_dim(queries, first, QB, 0)
        g_block = lax.dynamic_slice_in_dim(grad_mixed, first, QB, 0)
        query_pos = offset + first + lax.iota(jnp.int32, QB)
        seg_query = lax.dynamic_slice_in_dim(segments, offset + first, QB, 1)
        scores = block_scores(q_block, keys_all, seg_query, segments, query_pos)
        probs = jnp.exp(scores - log_block[..., None])
        grad_probs = jnp.einsum(
            "qshe,kshe->shqk", g_block, values_all, preferred_element_type=jnp.float32
        )
        grad_scores = probs * (grad_probs - jnp.sum(probs * grad_probs, axis=-1, keepdims=True))
        grad_low = grad_scores.astype(jnp.bfloat16)
        grad_query = jnp.einsum(
            "shqk,kshe->qshe", grad_low, keys_all, preferred_element_type=jnp.float32
        )
        grad_keys = grad_keys + jnp.einsum(
            "shqk,qshe->kshe", grad_low, q_block, preferred_element_type=jnp.float32
        )
        grad_values = grad_values + jnp.einsum(
            "shqk,qshe->kshe",
            probs.astype(jnp.bfloat16),
            g_block,
            preferred_element_type=jnp.float32,
        )
        return ((grad_keys, grad_values), grad_query)

    empty_sum = jnp.zeros(keys_all.shape, jnp.float32)
    (grad_keys, grad_values), grad_query = lax.scan(
        one_block, (empty_sum, empty_sum), (jnp.arange(number, dtype=jnp.int32), log_totals)
    )
    return (grad_query.reshape(queries.shape), grad_keys, grad_values)


def per_device(
    tokens,
    segments,
    gain_attn,
    query_scale,
    w_qkv,
    w_out,
    gain_mlp,
    w_up,
    b_up,
    w_down,
    b_down,
    cotangent,
):
    qkv_all, out_all, up_all, down_all = (
        lax.all_gather(w_qkv, ("dp", "ctx"), axis=1, tiled=True),
        lax.all_gather(w_out, ("dp", "ctx"), axis=1, tiled=True),
        lax.all_gather(w_up, ("dp", "ctx"), axis=0, tiled=True),
        lax.all_gather(w_down, ("dp", "ctx"), axis=1, tiled=True),
    )
    local_rows = tokens.shape[0]
    sequences = tokens.shape[1]
    piece_rows = local_rows * lax.axis_size("tensor")
    offset = lax.axis_index("ctx") * piece_rows
    width_local = w_qkv.shape[2]
    heads_local = width_local // HD
    units_local = w_up.shape[1]
    tensor_rank = lax.axis_index("tensor")

    def by_heads(values):
        return values.reshape(values.shape[0], sequences, heads_local, HD)

    inputs = tokens.astype(jnp.float32)
    unit_one, inverse_one = normalize(inputs)
    normed_one = (unit_one * gain_attn).astype(jnp.bfloat16)
    gathered_one = lax.all_gather(normed_one, "tensor", axis=0, tiled=True)
    projected = jnp.einsum(
        "lsd,cde->clse", gathered_one, qkv_all, preferred_element_type=jnp.float32
    )
    scaling = LOG_TWO_E / math.sqrt(HD) * jax.nn.softplus(query_scale)
    scaling_wide = jnp.tile(scaling, heads_local)
    queries = (projected[0] * scaling_wide).astype(jnp.bfloat16)
    keys = projected[1].astype(jnp.bfloat16)
    values = projected[2].astype(jnp.bfloat16)
    keys_all, values_all = (
        lax.all_gather(keys, "ctx", axis=0, tiled=True),
        lax.all_gather(values, "ctx", axis=0, tiled=True),
    )
    mixed_heads, log_totals = attend(
        by_heads(queries), by_heads(keys_all), by_heads(values_all), segments, offset
    )
    mixed = mixed_heads.reshape(piece_rows, sequences, width_local)
    row_block = mixed
    attended = lax.psum_scatter(
        jnp.einsum("lse,ed->lsd", row_block, out_all, preferred_element_type=jnp.float32),
        "tensor",
        scatter_dimension=0,
        tiled=True,
    )
    hidden = inputs + attended
    unit_two, inverse_two = normalize(hidden)
    normed_two = (unit_two * gain_mlp).astype(jnp.bfloat16)
    gathered_two, grad_all = (
        lax.all_gather(normed_two, "tensor", axis=0, tiled=True),
        lax.all_gather(cotangent, "tensor", axis=0, tiled=True),
    )
    bias_local = lax.dynamic_slice_in_dim(b_up, tensor_rank * units_local, units_local, 0)
    pre_act = (
        jnp.einsum("lsd,dh->lsh", gathered_two, up_all, preferred_element_type=jnp.float32)
        + bias_local
    )
    act_value, silu_pull = jax.vjp(jax.nn.silu, pre_act)
    activation = act_value.astype(jnp.bfloat16)
    row_block = activation
    branch = lax.psum_scatter(
        jnp.einsum("lsh,hd->lsd", row_block, down_all, preferred_element_type=jnp.float32).astype(
            jnp.bfloat16
        ),
        "tensor",
        scatter_dimension=0,
        tiled=True,
    ).astype(jnp.float32)
    grad_act = jnp.einsum("lsd,hd->lsh", grad_all, down_all, preferred_element_type=jnp.float32)
    grad_pre = silu_pull(grad_act)[0].astype(jnp.bfloat16)
    grad_w_down = jnp.einsum(
        "lsh,lsd->hd", activation, grad_all, preferred_element_type=jnp.float32
    )
    grad_w_up = jnp.einsum(
        "lsd,lsh->dh", gathered_two, grad_pre, preferred_element_type=jnp.float32
    )
    bias_part = jnp.sum(grad_pre.astype(jnp.float32), axis=(0, 1))
    bias_up = lax.dynamic_update_slice_in_dim(
        jnp.zeros(b_up.shape, jnp.float32), bias_part, tensor_rank * units_local, 0
    )
    row_block = grad_pre
    grad_normed_two = lax.psum_scatter(
        jnp.einsum("lsh,dh->lsd", row_block, up_all, preferred_element_type=jnp.float32),
        "tensor",
        scatter_dimension=0,
        tiled=True,
    )
    outputs = (hidden + (branch + b_down)).astype(jnp.bfloat16)
    grad_top = cotangent.astype(jnp.float32)
    gain_two = jnp.sum(grad_normed_two * unit_two, axis=(0, 1))
    bias_down = jnp.sum(grad_top, axis=(0, 1))
    grad_hidden = grad_top + norm_back(grad_normed_two, unit_two, inverse_two, gain_mlp)
    grad_hidden_low = grad_hidden.astype(jnp.bfloat16)
    grad_attn_all = lax.all_gather(grad_hidden_low, "tensor", axis=0, tiled=True)
    grad_w_out = jnp.einsum("lse,lsd->ed", mixed, grad_attn_all, preferred_element_type=jnp.float32)
    grad_mixed = jnp.einsum(
        "lsd,ed->lse", grad_attn_all, out_all, preferred_element_type=jnp.float32
    ).astype(jnp.bfloat16)
    grad_scaled, grad_keys_all, grad_values_all = attend_back(
        by_heads(queries),
        by_heads(keys_all),
        by_heads(values_all),
        segments,
        offset,
        log_totals,
        by_heads(grad_mixed),
    )
    total_rows = keys_all.shape[0]
    grad_keys_own, grad_values_own = (
        lax.psum_scatter(
            grad_keys_all.reshape(total_rows, sequences, width_local),
            "ctx",
            scatter_dimension=0,
            tiled=True,
        ),
        lax.psum_scatter(
            grad_values_all.reshape(total_rows, sequences, width_local),
            "ctx",
            scatter_dimension=0,
            tiled=True,
        ),
    )
    grad_scaled = grad_scaled.reshape(piece_rows, sequences, width_local)
    scale_part = jnp.sum((projected[0] * grad_scaled).reshape(-1, heads_local, HD), axis=(0, 1))
    grad_queries = (grad_scaled * scaling_wide).astype(jnp.bfloat16)
    stacked = jnp.stack(
        [grad_queries, grad_keys_own.astype(jnp.bfloat16), grad_values_own.astype(jnp.bfloat16)]
    )
    grad_w_qkv = jnp.einsum(
        "lsd,clse->cde", gathered_one, stacked, preferred_element_type=jnp.float32
    )
    row_block = stacked
    grad_normed_one = lax.psum_scatter(
        jnp.einsum("clse,cde->lsd", row_block, qkv_all, preferred_element_type=jnp.float32).astype(
            jnp.bfloat16
        ),
        "tensor",
        scatter_dimension=0,
        tiled=True,
    ).astype(jnp.float32)
    gain_one = jnp.sum(grad_normed_one * unit_one, axis=(0, 1))
    grad_inputs = grad_hidden + norm_back(grad_normed_one, unit_one, inverse_one, gain_attn)
    qkv_grad, out_grad, up_grad, down_grad = (
        lax.psum_scatter(
            grad_w_qkv.astype(jnp.bfloat16), ("dp", "ctx"), scatter_dimension=1, tiled=True
        ).astype(jnp.float32),
        lax.psum_scatter(
            grad_w_out.astype(jnp.bfloat16), ("dp", "ctx"), scatter_dimension=1, tiled=True
        ).astype(jnp.float32),
        lax.psum_scatter(
            grad_w_up.astype(jnp.bfloat16), ("dp", "ctx"), scatter_dimension=0, tiled=True
        ).astype(jnp.float32),
        lax.psum_scatter(
            grad_w_down.astype(jnp.bfloat16), ("dp", "ctx"), scatter_dimension=1, tiled=True
        ).astype(jnp.float32),
    )
    gain_one, scale_sum, gain_two, bias_up, bias_down = lax.psum(
        (gain_one, scale_part, gain_two, bias_up, bias_down), ("dp", "ctx", "tensor")
    )
    grad_query_scale = scale_sum * (LOG_TWO_E / math.sqrt(HD)) * jax.nn.sigmoid(query_scale)
    return (
        outputs,
        grad_inputs.astype(jnp.bfloat16),
        qkv_grad,
        out_grad,
        up_grad,
        down_grad,
        gain_one,
        grad_query_scale,
        gain_two,
        bias_up,
        bias_down,
    )


def solution(mesh):
    placed = (
        P(("ctx", "tensor"), "dp", None),
        P("dp", None),
        P(),
        P(),
        P(None, ("dp", "ctx"), "tensor"),
        P("tensor", ("dp", "ctx")),
        P(),
        P(("dp", "ctx"), "tensor"),
        P(),
        P("tensor", ("dp", "ctx")),
        P(),
        P(("ctx", "tensor"), "dp", None),
    )
    return jax.shard_map(
        per_device,
        mesh=mesh,
        in_specs=placed,
        out_specs=(
            P(("ctx", "tensor"), "dp", None),
            P(("ctx", "tensor"), "dp", None),
            P(None, ("dp", "ctx"), "tensor"),
            P("tensor", ("dp", "ctx")),
            P(("dp", "ctx"), "tensor"),
            P("tensor", ("dp", "ctx")),
            P(),
            P(),
            P(),
            P(),
            P(),
        ),
        check_vma=False,
    )
```

profile of v0, /device:TPU:0, one launch (start us, length us, event | category | flops | bytes accessed | tf_op | source)
XLA Modules:
  0.0 3992.4 jit_solution(16718758891617053831)
XLA Ops:
  14.9 70.6 %all-gather.13.cloned.1.call-done = bf16[2048,1,1280]{2,0,1:T(8,128)(2,1)} async-done(((bf16[1024,1,1280]{2,0,1:T(8,128)(2,1)}), bf16[2048,1,1280]{2,0,1:T(8,128)(2,1)}) %all-gather.13.cloned.1.call-update) | async-done | bytes 5242896 | tf_op jit(solution)/shard_map/all_gather | solution.py:134
  85.5 56.6 %all-gather.15.cloned.1.call-done = bf16[3,1280,640]{2,1,0:T(8,128)(2,1)} async-done(((bf16[3,80,640]{2,1,0:T(8,128)(2,1)}), bf16[3,1280,640]{2,1,0:T(8,128)(2,1)}) %all-gather.15.cloned.1.call-update) | async-done | bytes 4915216 | tf_op jit(solution)/shard_map/all_gather | solution.py:114
  168.6 62.1 %all-gather.31.cloned.1.call-done = bf16[1,8192,1,640]{1,3,0,2:T(8,128)(2,1)} async-done(((bf16[1,2048,1,640]{1,3,0,2:T(8,128)(2,1)}), bf16[1,8192,1,640]{1,3,0,2:T(8,128)(2,1)}) %all-gather.31.cloned.1.call-update) | async-done | bytes 10485776 | tf_op jit(solution)/shard_map/all_gather | solution.py:145
  230.7 71.7 %all-gather.29.cloned.1.call-done = bf16[1,8192,1,640]{1,3,0,2:T(8,128)(2,1)} async-done(((bf16[1,2048,1,640]{1,3,0,2:T(8,128)(2,1)}), bf16[1,8192,1,640]{1,3,0,2:T(8,128)(2,1)}) %all-gather.29.cloned.1.call-update) | async-done | bytes 10485776 | tf_op jit(solution)/shard_map/all_gather | solution.py:144
  302.9 620.6 %while.27 = (s32[]{:T(128)}, bf16[4,512,1,8,80]{1,4,3,2,0:T(8,128)(2,1)S(1)}, f32[4,1,8,512]{3,2,1,0:T(8,128)}, s32[4]{0:T(128)}, s32[]{:T(128)}, /*index=5*/s32...) while((s32[]{:T(128)}, ...), condition=%wide.region_4.5_spmd, body=%wide.region_1.4_spmd.sunk | while | flops 11052314624 | bytes 441886976 | solution.py:56
  311.0 51.8 %select_reduce_fusion.2 = (f32[8,512]{1,0:T(8,128)S(1)}, f32[8,512,8192]{2,1,0:T(8,128)}) fusion(pred[512,8192]{1,0:T(8,128)(4,1)} %fusion.144, bf16[8192,1,8,80]{0,3,2,1:T(8,128)(2,1)} %get-tuple-element.450, bf16[2048,1,8,80]{0,3,2,1:T(8,128)(2,1)} %get-tuple-element.449, s32[]{:T(128)S(6)} %select_n.78), kind=kOutput, calls=%fused_computation.2.clone.2 | convolution fusion | flops 5435813888 | bytes 149569536 | tf_op jit(solution)/shard_map/while/body/eval_jaxpr/qshe,kshe->shqk/dot_general | solution.py:28
  362.9 43.8 %fusion.145 = f32[8,512]{1,0:T(8,128)S(1)} fusion(f32[8,512,8192]{2,1,0:T(8,128)} %get-tuple-element.399, f32[8,512]{1,0:T(8,128)S(1)} %get-tuple-element.400, pred[512,8192]{1,0:T(8,128)(4,1)} %fusion.144), kind=kLoop, calls=%fused_computation.3.clone.1 | loop fusion | flops 100659200 | bytes 138444800 | tf_op jit(solution)/shard_map/while/body/eval_jaxpr/reduce_sum | solution.py:49
  406.6 51.5 %fusion.146 = bf16[4,512,1,8,80]{1,4,3,2,0:T(8,128)(2,1)S(1)} fusion(bf16[4,512,1,8,80]{1,4,3,2,0:T(8,128)(2,1)S(1)} %get-tuple-element.430, s32[]{:T(128)S(6)} %copy.62, bf16[8192,1,8,80]{0,3,2,1:T(8,128)(2,1)} %get-tuple-element.451, f32[8,512,8192]{2,1,0:T(8,128)} %get-tuple-element.399, f32[8,512]{1,0:T(8,128)S(1)} %fusion.145, ...), kind=kOutput, calls=%fused_computation.12.clone.1 | convolution fusion | flops 5503254528 | bytes 149585920 | tf_op jit(solution)/shard_map/while/body/eval_jaxpr/shqk,kshe->qshe/dot_general | solution.py:51
  466.9 50.7 %select_reduce_fusion.2 = (f32[8,512]{1,0:T(8,128)S(1)}, f32[8,512,8192]{2,1,0:T(8,128)}) fusion(pred[512,8192]{1,0:T(8,128)(4,1)} %fusion.144, bf16[8192,1,8,80]{0,3,2,1:T(8,128)(2,1)} %get-tuple-element.450, bf16[2048,1,8,80]{0,3,2,1:T(8,128)(2,1)} %get-tuple-element.449, s32[]{:T(128)S(6)} %select_n.78), kind=kOutput, calls=%fused_computation.2.clone.2 | convolution fusion | flops 5435813888 | bytes 149569536 | tf_op jit(solution)/shard_map/while/body/eval_jaxpr/qshe,kshe->shqk/dot_general | solution.py:28
  517.7 43.8 %fusion.145 = f32[8,512]{1,0:T(8,128)S(1)} fusion(f32[8,512,8192]{2,1,0:T(8,128)} %get-tuple-element.399, f32[8,512]{1,0:T(8,128)S(1)} %get-tuple-element.400, pred[512,8192]{1,0:T(8,128)(4,1)} %fusion.144), kind=kLoop, calls=%fused_computation.3.clone.1 | loop fusion | flops 100659200 | bytes 138444800 | tf_op jit(solution)/shard_map/while/body/eval_jaxpr/reduce_sum | solution.py:49
  561.4 51.5 %fusion.146 = bf16[4,512,1,8,80]{1,4,3,2,0:T(8,128)(2,1)S(1)} fusion(bf16[4,512,1,8,80]{1,4,3,2,0:T(8,128)(2,1)S(1)} %get-tuple-element.430, s32[]{:T(128)S(6)} %copy.62, bf16[8192,1,8,80]{0,3,2,1:T(8,128)(2,1)} %get-tuple-element.451, f32[8,512,8192]{2,1,0:T(8,128)} %get-tuple-element.399, f32[8,512]{1,0:T(8,128)S(1)} %fusion.145, ...), kind=kOutput, calls=%fused_computation.12.clone.1 | convolution fusion | flops 5503254528 | bytes 149585920 | tf_op jit(solution)/shard_map/while/body/eval_jaxpr/shqk,kshe->qshe/dot_general | solution.py:51
  621.7 50.7 %select_reduce_fusion.2 = (f32[8,512]{1,0:T(8,128)S(1)}, f32[8,512,8192]{2,1,0:T(8,128)}) fusion(pred[512,8192]{1,0:T(8,128)(4,1)} %fusion.144, bf16[8192,1,8,80]{0,3,2,1:T(8,128)(2,1)} %get-tuple-element.450, bf16[2048,1,8,80]{0,3,2,1:T(8,128)(2,1)} %get-tuple-element.449, s32[]{:T(128)S(6)} %select_n.78), kind=kOutput, calls=%fused_computation.2.clone.2 | convolution fusion | flops 5435813888 | bytes 149569536 | tf_op jit(solution)/shard_map/while/body/eval_jaxpr/qshe,kshe->shqk/dot_general | solution.py:28
  672.4 43.8 %fusion.145 = f32[8,512]{1,0:T(8,128)S(1)} fusion(f32[8,512,8192]{2,1,0:T(8,128)} %get-tuple-element.399, f32[8,512]{1,0:T(8,128)S(1)} %get-tuple-element.400, pred[512,8192]{1,0:T(8,128)(4,1)} %fusion.144), kind=kLoop, calls=%fused_computation.3.clone.1 | loop fusion | flops 100659200 | bytes 138444800 | tf_op jit(solution)/shard_map/while/body/eval_jaxpr/reduce_sum | solution.py:49
  716.2 51.5 %fusion.146 = bf16[4,512,1,8,80]{1,4,3,2,0:T(8,128)(2,1)S(1)} fusion(bf16[4,512,1,8,80]{1,4,3,2,0:T(8,128)(2,1)S(1)} %get-tuple-element.430, s32[]{:T(128)S(6)} %copy.62, bf16[8192,1,8,80]{0,3,2,1:T(8,128)(2,1)} %get-tuple-element.451, f32[8,512,8192]{2,1,0:T(8,128)} %get-tuple-element.399, f32[8,512]{1,0:T(8,128)S(1)} %fusion.145, ...), kind=kOutput, calls=%fused_computation.12.clone.1 | convolution fusion | flops 5503254528 | bytes 149585920 | tf_op jit(solution)/shard_map/while/body/eval_jaxpr/shqk,kshe->qshe/dot_general | solution.py:51
  776.5 50.7 %select_reduce_fusion.2 = (f32[8,512]{1,0:T(8,128)S(1)}, f32[8,512,8192]{2,1,0:T(8,128)}) fusion(pred[512,8192]{1,0:T(8,128)(4,1)} %fusion.144, bf16[8192,1,8,80]{0,3,2,1:T(8,128)(2,1)} %get-tuple-element.450, bf16[2048,1,8,80]{0,3,2,1:T(8,128)(2,1)} %get-tuple-element.449, s32[]{:T(128)S(6)} %select_n.78), kind=kOutput, calls=%fused_computation.2.clone.2 | convolution fusion | flops 5435813888 | bytes 149569536 | tf_op jit(solution)/shard_map/while/body/eval_jaxpr/qshe,kshe->shqk/dot_general | solution.py:28
  827.2 43.8 %fusion.145 = f32[8,512]{1,0:T(8,128)S(1)} fusion(f32[8,512,8192]{2,1,0:T(8,128)} %get-tuple-element.399, f32[8,512]{1,0:T(8,128)S(1)} %get-tuple-element.400, pred[512,8192]{1,0:T(8,128)(4,1)} %fusion.144), kind=kLoop, calls=%fused_computation.3.clone.1 | loop fusion | flops 100659200 | bytes 138444800 | tf_op jit(solution)/shard_map/while/body/eval_jaxpr/reduce_sum | solution.py:49
  871.0 51.5 %fusion.146 = bf16[4,512,1,8,80]{1,4,3,2,0:T(8,128)(2,1)S(1)} fusion(bf16[4,512,1,8,80]{1,4,3,2,0:T(8,128)(2,1)S(1)} %get-tuple-element.430, s32[]{:T(128)S(6)} %copy.62, bf16[8192,1,8,80]{0,3,2,1:T(8,128)(2,1)} %get-tuple-element.451, f32[8,512,8192]{2,1,0:T(8,128)} %get-tuple-element.399, f32[8,512]{1,0:T(8,128)S(1)} %fusion.145, ...), kind=kOutput, calls=%fused_computation.12.clone.1 | convolution fusion | flops 5503254528 | bytes 149585920 | tf_op jit(solution)/shard_map/while/body/eval_jaxpr/shqk,kshe->qshe/dot_general | solution.py:51
  936.4 121.2 %reduce-scatter.10.cloned.1.call-done = f32[1024,1,1280]{2,0,1:T(8,128)} async-done(((f32[2048,1,1280]{2,0,1:T(8,128)}), f32[1024,1,1280]{2,0,1:T(8,128)}) %reduce-scatter.10.cloned.1.call-update) | async-done | bytes 5242896 | tf_op jit(solution)/shard_map/reduce_scatter | solution.py:152
  1099.7 69.6 %all-gather.19.cloned.1.call-done = bf16[2048,1,1280]{2,0,1:T(8,128)(2,1)} async-done(((bf16[1024,1,1280]{2,0,1:T(8,128)(2,1)}), bf16[2048,1,1280]{2,0,1:T(8,128)(2,1)}) %all-gather.19.cloned.1.call-update) | async-done | bytes 5242896 | tf_op jit(solution)/shard_map/all_gather | solution.py:162
  1211.5 68.9 %all-gather.25.cloned.1.call-done = bf16[2048,1,1280]{2,0,1:T(8,128)(2,1)} async-done(((bf16[1024,1,1280]{2,0,1:T(8,128)(2,1)}), bf16[2048,1,1280]{2,0,1:T(8,128)(2,1)}) %all-gather.25.cloned.1.call-update) | async-done | bytes 5242896 | tf_op jit(solution)/shard_map/all_gather | solution.py:163
  1299.3 122.0 %reduce-scatter.14.cloned.1.call-done = f32[1024,1,1280]{2,0,1:T(8,128)} async-done(((f32[2048,1,1280]{2,0,1:T(8,128)}), f32[1024,1,1280]{2,0,1:T(8,128)}) %reduce-scatter.14.cloned.1.call-update) | async-done | bytes 5242896 | tf_op jit(solution)/shard_map/reduce_scatter | solution.py:194
  1432.4 68.6 %all-gather.27.cloned.1.call-done = bf16[2048,1,1280]{2,0,1:T(8,128)(2,1)} async-done(((bf16[1024,1,1280]{2,0,1:T(8,128)(2,1)}), bf16[2048,1,1280]{2,0,1:T(8,128)(2,1)}) %all-gather.27.cloned.1.call-update) | async-done | bytes 5242896 | tf_op jit(solution)/shard_map/all_gather | solution.py:206
  1509.6 1645.4 %while.28 = (s32[]{:T(128)}, f32[8192,1,8,80]{0,3,2,1:T(8,128)}, f32[8192,1,8,80]{0,3,2,1:T(8,128)}, f32[4,512,1,8,80]{1,0,4,3,2:T(4,128)}, s32[4]{0:T(128)}, /*...) while((s32[]{:T(128)}, f32[8192,1,8,80]{0,3,2,1:T(8,128)}, ...), condition=%wide.region_12.13_spmd.clone, body=%wide.region_10.12_spmd.clone.sunk | while | flops 27279749120 | bytes 1148086528 | solution.py:93
  1519.0 49.0 %fusion.155 = f32[8,512,8192]{2,1,0:T(8,128)} fusion(bf16[8192,1,8,80]{0,3,2,1:T(8,128)(2,1)} %get-tuple-element.499, bf16[2048,1,8,80]{0,3,2,1:T(8,128)(2,1)} %get-tuple-element.496, s32[]{:T(128)S(6)} %select_n.82), kind=kOutput, calls=%fused_computation.36.clone.2 | convolution fusion | flops 5368709120 | bytes 145358848 | tf_op jit(solution)/shard_map/while/body/eval_jaxpr/qshe,kshe->shqk/dot_general | solution.py:28
  1568.0 52.2 %bitcast_add_fusion.5 = f32[8192,1,8,80]{0,3,2,1:T(8,128)} fusion(f32[8192,1,8,80]{0,3,2,1:T(8,128)} %get-tuple-element.476, f32[8,512,8192]{2,1,0:T(8,128)} %fusion.155, f32[8,512]{1,0:T(8,128)S(1)} %dynamic-slice_bitcast_fusion.2, pred[512,8192]{1,0:T(8,128)(4,1)} %fusion.156, pred[]{:T(512)S(6)} %compare.3, ...), kind=kOutput, calls=%fused_computation.28.clone.2 | convolution fusion | flops 5479858176 | bytes 181026816 | tf_op jit(solution)/shard_map/while/body/eval_jaxpr/shqk,qshe->kshe/dot_general | solution.py:84
  1620.2 96.6 %multiply_reduce_fusion.6 = (f32[8,512]{1,0:T(8,128)S(1)}, f32[8,512,8192]{2,1,0:T(8,128)}) fusion(f32[8,512,8192]{2,1,0:T(8,128)} %fusion.155, f32[8,512]{1,0:T(8,128)S(1)} %dynamic-slice_bitcast_fusion.2, pred[512,8192]{1,0:T(8,128)(4,1)} %fusion.156, bf16[8192,1,8,80]{0,3,2,1:T(8,128)(2,1)} %get-tuple-element.502, ...), kind=kOutput, calls=%fused_computation.21.clone.2 | convolution fusion | flops 5502922752 | bytes 283803648 | tf_op jit(solution)/shard_map/while/body/eval_jaxpr/qshe,kshe->shqk/dot_general | solution.py:73
  1716.8 104.5 %multiply_convert_fusion.8 = bf16[8,512,8192]{2,1,0:T(8,128)(2,1)} fusion(f32[8,512,8192]{2,1,0:T(8,128)} %get-tuple-element.413, f32[8,512,8192]{2,1,0:T(8,128)} %fusion.155, f32[8,512]{1,0:T(8,128)S(1)} %get-tuple-element.414, f32[8,512]{1,0:T(8,128)S(1)} %dynamic-slice_bitcast_fusion.2, pred[512,8192]{1,0:T(8,128)(4,1)} %fusion.156), kind=kLoop, calls=%fused_computation.20.clone.1 | loop fusion | flops 167772160 | bytes 339771392 | tf_op jit(solution)/shard_map/while/body/eval_jaxpr/convert_element_type | solution.py:77
  1920.1 49.0 %fusion.155 = f32[8,512,8192]{2,1,0:T(8,128)} fusion(bf16[8192,1,8,80]{0,3,2,1:T(8,128)(2,1)} %get-tuple-element.499, bf16[2048,1,8,80]{0,3,2,1:T(8,128)(2,1)} %get-tuple-element.496, s32[]{:T(128)S(6)} %select_n.82), kind=kOutput, calls=%fused_computation.36.clone.2 | convolution fusion | flops 5368709120 | bytes 145358848 | tf_op jit(solution)/shard_map/while/body/eval_jaxpr/qshe,kshe->shqk/dot_general | solution.py:28
  1969.1 59.0 %bitcast_add_fusion.5 = f32[8192,1,8,80]{0,3,2,1:T(8,128)} fusion(f32[8192,1,8,80]{0,3,2,1:T(8,128)} %get-tuple-element.476, f32[8,512,8192]{2,1,0:T(8,128)} %fusion.155, f32[8,512]{1,0:T(8,128)S(1)} %dynamic-slice_bitcast_fusion.2, pred[512,8192]{1,0:T(8,128)(4,1)} %fusion.156, pred[]{:T(512)S(6)} %compare.3, ...), kind=kOutput, calls=%fused_computation.28.clone.2 | convolution fusion | flops 5479858176 | bytes 181026816 | tf_op jit(solution)/shard_map/while/body/eval_jaxpr/shqk,qshe->kshe/dot_general | solution.py:84
  2028.1 96.8 %multiply_reduce_fusion.6 = (f32[8,512]{1,0:T(8,128)S(1)}, f32[8,512,8192]{2,1,0:T(8,128)}) fusion(f32[8,512,8192]{2,1,0:T(8,128)} %fusion.155, f32[8,512]{1,0:T(8,128)S(1)} %dynamic-slice_bitcast_fusion.2, pred[512,8192]{1,0:T(8,128)(4,1)} %fusion.156, bf16[8192,1,8,80]{0,3,2,1:T(8,128)(2,1)} %get-tuple-element.502, ...), kind=kOutput, calls=%fused_computation.21.clone.2 | convolution fusion | flops 5502922752 | bytes 283803648 | tf_op jit(solution)/shard_map/while/body/eval_jaxpr/qshe,kshe->shqk/dot_general | solution.py:73
  2124.9 104.5 %multiply_convert_fusion.8 = bf16[8,512,8192]{2,1,0:T(8,128)(2,1)} fusion(f32[8,512,8192]{2,1,0:T(8,128)} %get-tuple-element.413, f32[8,512,8192]{2,1,0:T(8,128)} %fusion.155, f32[8,512]{1,0:T(8,128)S(1)} %get-tuple-element.414, f32[8,512]{1,0:T(8,128)S(1)} %dynamic-slice_bitcast_fusion.2, pred[512,8192]{1,0:T(8,128)(4,1)} %fusion.156), kind=kLoop, calls=%fused_computation.20.clone.1 | loop fusion | flops 167772160 | bytes 339771392 | tf_op jit(solution)/shard_map/while/body/eval_jaxpr/convert_element_type | solution.py:77
  2334.7 49.0 %fusion.155 = f32[8,512,8192]{2,1,0:T(8,128)} fusion(bf16[8192,1,8,80]{0,3,2,1:T(8,128)(2,1)} %get-tuple-element.499, bf16[2048,1,8,80]{0,3,2,1:T(8,128)(2,1)} %get-tuple-element.496, s32[]{:T(128)S(6)} %select_n.82), kind=kOutput, calls=%fused_computation.36.clone.2 | convolution fusion | flops 5368709120 | bytes 145358848 | tf_op jit(solution)/shard_map/while/body/eval_jaxpr/qshe,kshe->shqk/dot_general | solution.py:28
  2383.7 59.0 %bitcast_add_fusion.5 = f32[8192,1,8,80]{0,3,2,1:T(8,128)} fusion(f32[8192,1,8,80]{0,3,2,1:T(8,128)} %get-tuple-element.476, f32[8,512,8192]{2,1,0:T(8,128)} %fusion.155, f32[8,512]{1,0:T(8,128)S(1)} %dynamic-slice_bitcast_fusion.2, pred[512,8192]{1,0:T(8,128)(4,1)} %fusion.156, pred[]{:T(512)S(6)} %compare.3, ...), kind=kOutput, calls=%fused_computation.28.clone.2 | convolution fusion | flops 5479858176 | bytes 181026816 | tf_op jit(solution)/shard_map/while/body/eval_jaxpr/shqk,qshe->kshe/dot_general | solution.py:84
  2442.7 96.7 %multiply_reduce_fusion.6 = (f32[8,512]{1,0:T(8,128)S(1)}, f32[8,512,8192]{2,1,0:T(8,128)}) fusion(f32[8,512,8192]{2,1,0:T(8,128)} %fusion.155, f32[8,512]{1,0:T(8,128)S(1)} %dynamic-slice_bitcast_fusion.2, pred[512,8192]{1,0:T(8,128)(4,1)} %fusion.156, bf16[8192,1,8,80]{0,3,2,1:T(8,128)(2,1)} %get-tuple-element.502, ...), kind=kOutput, calls=%fused_computation.21.clone.2 | convolution fusion | flops 5502922752 | bytes 283803648 | tf_op jit(solution)/shard_map/while/body/eval_jaxpr/qshe,kshe->shqk/dot_general | solution.py:73
  2539.4 104.5 %multiply_convert_fusion.8 = bf16[8,512,8192]{2,1,0:T(8,128)(2,1)} fusion(f32[8,512,8192]{2,1,0:T(8,128)} %get-tuple-element.413, f32[8,512,8192]{2,1,0:T(8,128)} %fusion.155, f32[8,512]{1,0:T(8,128)S(1)} %get-tuple-element.414, f32[8,512]{1,0:T(8,128)S(1)} %dynamic-slice_bitcast_fusion.2, pred[512,8192]{1,0:T(8,128)(4,1)} %fusion.156), kind=kLoop, calls=%fused_computation.20.clone.1 | loop fusion | flops 167772160 | bytes 339771392 | tf_op jit(solution)/shard_map/while/body/eval_jaxpr/convert_element_type | solution.py:77
  2675.4 37.6 bitcast_add_fusion.4
  2749.3 49.0 %fusion.155 = f32[8,512,8192]{2,1,0:T(8,128)} fusion(bf16[8192,1,8,80]{0,3,2,1:T(8,128)(2,1)} %get-tuple-element.499, bf16[2048,1,8,80]{0,3,2,1:T(8,128)(2,1)} %get-tuple-element.496, s32[]{:T(128)S(6)} %select_n.82), kind=kOutput, calls=%fused_computation.36.clone.2 | convolution fusion | flops 5368709120 | bytes 145358848 | tf_op jit(solution)/shard_map/while/body/eval_jaxpr/qshe,kshe->shqk/dot_general | solution.py:28
  2798.3 59.0 %bitcast_add_fusion.5 = f32[8192,1,8,80]{0,3,2,1:T(8,128)} fusion(f32[8192,1,8,80]{0,3,2,1:T(8,128)} %get-tuple-element.476, f32[8,512,8192]{2,1,0:T(8,128)} %fusion.155, f32[8,512]{1,0:T(8,128)S(1)} %dynamic-slice_bitcast_fusion.2, pred[512,8192]{1,0:T(8,128)(4,1)} %fusion.156, pred[]{:T(512)S(6)} %compare.3, ...), kind=kOutput, calls=%fused_computation.28.clone.2 | convolution fusion | flops 5479858176 | bytes 181026816 | tf_op jit(solution)/shard_map/while/body/eval_jaxpr/shqk,qshe->kshe/dot_general | solution.py:84
  2857.3 96.7 %multiply_reduce_fusion.6 = (f32[8,512]{1,0:T(8,128)S(1)}, f32[8,512,8192]{2,1,0:T(8,128)}) fusion(f32[8,512,8192]{2,1,0:T(8,128)} %fusion.155, f32[8,512]{1,0:T(8,128)S(1)} %dynamic-slice_bitcast_fusion.2, pred[512,8192]{1,0:T(8,128)(4,1)} %fusion.156, bf16[8192,1,8,80]{0,3,2,1:T(8,128)(2,1)} %get-tuple-element.502, ...), kind=kOutput, calls=%fused_computation.21.clone.2 | convolution fusion | flops 5502922752 | bytes 283803648 | tf_op jit(solution)/shard_map/while/body/eval_jaxpr/qshe,kshe->shqk/dot_general | solution.py:73
  2954.0 104.5 %multiply_convert_fusion.8 = bf16[8,512,8192]{2,1,0:T(8,128)(2,1)} fusion(f32[8,512,8192]{2,1,0:T(8,128)} %get-tuple-element.413, f32[8,512,8192]{2,1,0:T(8,128)} %fusion.155, f32[8,512]{1,0:T(8,128)S(1)} %get-tuple-element.414, f32[8,512]{1,0:T(8,128)S(1)} %dynamic-slice_bitcast_fusion.2, pred[512,8192]{1,0:T(8,128)(4,1)} %fusion.156), kind=kLoop, calls=%fused_computation.20.clone.1 | loop fusion | flops 167772160 | bytes 339771392 | tf_op jit(solution)/shard_map/while/body/eval_jaxpr/convert_element_type | solution.py:77
  3198.1 110.3 %reduce-scatter.16.cloned.1.call-done = f32[2048,1,640]{0,2,1:T(8,128)} async-done(((f32[8192,1,640]{0,2,1:T(8,128)}), f32[2048,1,640]{0,2,1:T(8,128)}) %reduce-scatter.16.cloned.1.call-update) | async-done | bytes 5242896 | tf_op jit(solution)/shard_map/reduce_scatter | solution.py:222
  3312.8 151.4 %reduce-scatter.18.cloned.1.call-done = f32[2048,1,640]{0,2,1:T(8,128)} async-done(((f32[8192,1,640]{0,2,1:T(8,128)}), f32[2048,1,640]{0,2,1:T(8,128)}) %reduce-scatter.18.cloned.1.call-update) | async-done | bytes 5242896 | tf_op jit(solution)/shard_map/reduce_scatter | solution.py:228
  3530.5 59.2 %reduce-scatter.24.cloned.1.call-done = bf16[80,640]{1,0:T(8,128)(2,1)} async-done(((bf16[1280,640]{1,0:T(8,128)(2,1)}), bf16[80,640]{1,0:T(8,128)(2,1)}) %reduce-scatter.24.cloned.1.call-update) | async-done | bytes 102416 | tf_op jit(solution)/shard_map/reduce_scatter | solution.py:262
  3591.4 60.4 %reduce-scatter.22.cloned.1.call-done = bf16[640,80]{0,1:T(8,128)(2,1)} async-done(((bf16[640,1280]{0,1:T(8,128)(2,1)}), bf16[640,80]{0,1:T(8,128)(2,1)}) %reduce-scatter.22.cloned.1.call-update) | async-done | bytes 102416 | tf_op jit(solution)/shard_map/reduce_scatter | solution.py:259
  3653.3 144.9 %all-reduce.4.cloned.1.call-done = bf16[3,1280,640]{2,0,1:T(4,128)(2,1)} async-done(((bf16[3,1280,640]{2,0,1:T(4,128)(2,1)}), bf16[3,1280,640]{2,0,1:T(4,128)(2,1)}) %all-reduce.4.cloned.1.call-update) | async-done | bytes 4915216
  3800.2 66.0 %reduce-scatter.20.cloned.1.call-done = bf16[1024,1,1280]{2,0,1:T(8,128)(2,1)} async-done(((bf16[2048,1,1280]{2,0,1:T(8,128)(2,1)}), bf16[1024,1,1280]{2,0,1:T(8,128)(2,1)}) %reduce-scatter.20.cloned.1.call-update) | async-done | bytes 2621456 | tf_op jit(solution)/shard_map/reduce_scatter | solution.py:245
  3869.7 64.5 %reduce-scatter.12.cloned.1.call-done = bf16[1024,1,1280]{2,0,1:T(8,128)(2,1)} async-done(((bf16[2048,1,1280]{2,0,1:T(8,128)(2,1)}), bf16[1024,1,1280]{2,0,1:T(8,128)(2,1)}) %reduce-scatter.12.cloned.1.call-update) | async-done | bytes 2621456 | tf_op jit(solution)/shard_map/reduce_scatter | solution.py:173
  3944.1 40.5 %all-reduce.1 = (f32[1280]{0:T(1024)}, f32[80]{0:T(128)S(1)}, f32[1280]{0:T(1024)}, f32[1280]{0:T(1024)}, f32[1280]{0:T(1024)}) all-reduce(f32[1280]{0:T(1024)S(1)} %get-tuple-element.213, f32[80]{0:T(128)S(1)} %reduce_sum.113, f32[1280]{0:T(1024)S(1)} %copy-done.18, ...), channel_id=1, replica_groups=mesh['dp'=4,'ctx'=4,'tensor'=2] {'dp','ctx','tensor'}, use_global_device_ids=true, to_apply=%region_22.23 | all-reduce | flops 5200 | bytes 41600 | tf_op jit(solution)/shard_map/psum | solution.py:269
  (219 shorter events, 709.3 us)
Async XLA Ops:
  7.2 78.3 %all-gather.13.cloned.1.call-start = ((), (), s32[]{:S(2)}) async-start(), calls=%async_computation.9 | async-start | bytes 7864320 | tf_op jit(solution)/shard_map/all_gather | solution.py:134
  14.1 128.0 %all-gather.15.cloned.1.call-start = ((), (), s32[]{:S(2)}) async-start(), calls=%async_computation.10 | async-start | bytes 5222400 | tf_op jit(solution)/shard_map/all_gather | solution.py:114
  14.8 215.9 %all-gather.31.cloned.1.call-start = ((), (), s32[]{:S(2)}) async-start(), calls=%async_computation.27 | async-start | bytes 13107200 | tf_op jit(solution)/shard_map/all_gather | solution.py:145
  161.8 1.5 copy-start.28
  161.8 140.5 %all-gather.29.cloned.1.call-start = ((), (), s32[]{:S(2)}) async-start(), calls=%async_computation.26 | async-start | bytes 13107200 | tf_op jit(solution)/shard_map/all_gather | solution.py:144
  162.4 763.9 %all-gather.17.cloned.1.call-start = ((), (), s32[]{:S(2)}) async-start(), calls=%async_computation.11 | async-start | bytes 1740800 | tf_op jit(solution)/shard_map/all_gather | solution.py:115
  163.0 894.6 %reduce-scatter.10.cloned.1.call-start = ((), (), s32[]{:S(2)}) async-start(), calls=%async_computation.12 | async-start | bytes 15728640 | tf_op jit(solution)/shard_map/reduce_scatter | solution.py:152
  163.3 3.1 copy-start.23
  926.3 9.3 copy-start.5
  935.6 122.0 %copy-start.1 = (bf16[1024,1,1280]{2,0,1:T(8,128)(2,1)S(1)}, bf16[1024,1,1280]{2,0,1:T(8,128)(2,1)}, u32[]{:S(2)}) copy-start(bf16[1024,1,1280]{2,0,1:T(8,128)(2,1)} %param.16) | copy-start | bytes 7864324
  935.6 164.1 %all-gather.21.cloned.1.call-start = ((), (), s32[]{:S(2)}) async-start(), calls=%async_computation.14 | async-start | bytes 1740800 | tf_op jit(solution)/shard_map/all_gather | solution.py:116
  936.4 126.7 %copy-start.9 = (f32[1280]{0:T(1024)S(1)}, f32[1280]{0:T(1024)}, u32[]{:S(2)}) copy-start(f32[1280]{0:T(1024)} %param.22) | copy-start | bytes 15364
  936.4 233.0 %all-gather.19.cloned.1.call-start = ((), (), s32[]{:S(2)}) async-start(), calls=%async_computation.13 | async-start | bytes 7864320 | tf_op jit(solution)/shard_map/all_gather | solution.py:162
  1060.8 2.3 copy-start
  1060.9 366.3 %copy-start.11 = (f32[1024]{0:T(1024)}, f32[1024]{0:T(1024)S(1)}, u32[]{:S(2)}) copy-start(f32[1024]{0:T(1024)S(1)} %add_rsqrt_fusion) | copy-start | bytes 12292
  1063.1 3.6 copy-start.25
  1065.1 146.3 %all-gather.23.cloned.1.call-start = ((), (), s32[]{:S(2)}) async-start(), calls=%async_computation.15 | async-start | bytes 1740800 | tf_op jit(solution)/shard_map/all_gather | solution.py:117
  1065.9 214.5 %all-gather.25.cloned.1.call-start = ((), (), s32[]{:S(2)}) async-start(), calls=%async_computation.17 | async-start | bytes 7864320 | tf_op jit(solution)/shard_map/all_gather | solution.py:163
  1066.5 354.8 %reduce-scatter.14.cloned.1.call-start = ((), (), s32[]{:S(2)}) async-start(), calls=%async_computation.18 | async-start | bytes 15728640 | tf_op jit(solution)/shard_map/reduce_scatter | solution.py:194
  1066.8 213.6 %copy-start.21 = (f32[640]{0:T(1024)}, f32[640]{0:T(1024)S(1)}, u32[]{:S(2)}) copy-start(f32[640]{0:T(1024)S(1)} %dynamic_slice.29) | copy-start | bytes 7684
  1178.9 113.4 %copy-start.27 = (bf16[1280,640]{1,0:T(8,128)(2,1)S(1)}, bf16[1280,640]{1,0:T(8,128)(2,1)}, u32[]{:S(2)}) copy-start(bf16[1280,640]{1,0:T(8,128)(2,1)} %all-gather.21.cloned.1.call-done) | copy-start | bytes 4915204
  1290.8 1.5 copy-start.31
  1299.2 128.6 %copy-start.4 = (bf16[1024,1,1280]{2,0,1:T(8,128)(2,1)S(1)}, bf16[1024,1,1280]{2,0,1:T(8,128)(2,1)}, u32[]{:S(2)}) copy-start(bf16[1024,1,1280]{2,0,1:T(8,128)(2,1)} %param.27) | copy-start | bytes 7864324
  1299.2 201.8 %all-gather.27.cloned.1.call-start = ((), (), s32[]{:S(2)}) async-start(), calls=%async_computation.19 | async-start | bytes 7864320 | tf_op jit(solution)/shard_map/all_gather | solution.py:206
  1421.2 6.6 copy-start.3
  1432.3 1876.1 %reduce-scatter.16.cloned.1.call-start = ((), (), s32[]{:S(2)}) async-start(), calls=%async_computation.20 | async-start | bytes 26214400 | tf_op jit(solution)/shard_map/reduce_scatter | solution.py:222
  3155.1 309.1 %reduce-scatter.18.cloned.1.call-start = ((), (), s32[]{:S(2)}) async-start(), calls=%async_computation.21 | async-start | bytes 26214400 | tf_op jit(solution)/shard_map/reduce_scatter | solution.py:228
  3155.7 373.2 %reduce-scatter.26.cloned.1.call-start = ((), (), s32[]{:S(2)}) async-start(), calls=%async_computation.25 | async-start | bytes 1740800 | tf_op jit(solution)/shard_map/reduce_scatter | solution.py:265
  3165.5 10.7 copy-start.24
  3165.5 424.2 %reduce-scatter.24.cloned.1.call-start = ((), (), s32[]{:S(2)}) async-start(), calls=%async_computation.24 | async-start | bytes 1740800 | tf_op jit(solution)/shard_map/reduce_scatter | solution.py:262
  3176.1 475.6 %reduce-scatter.22.cloned.1.call-start = ((), (), s32[]{:S(2)}) async-start(), calls=%async_computation.23 | async-start | bytes 1740800 | tf_op jit(solution)/shard_map/reduce_scatter | solution.py:259
  3176.3 9.0 copy-start.6
  3193.3 605.0 %all-reduce.4.cloned.1.call-start = ((), (), s32[]{:S(2)}) async-start(), calls=%async_computation.28 | async-start | bytes 13107200
  3464.2 4.5 copy-start.7
  3467.2 1.5 copy-start.8
  3499.3 367.0 %reduce-scatter.20.cloned.1.call-start = ((), (), s32[]{:S(2)}) async-start(), calls=%async_computation.22 | async-start | bytes 7864320 | tf_op jit(solution)/shard_map/reduce_scatter | solution.py:245
  3515.6 1.4 copy-start.26
  3515.7 418.5 %reduce-scatter.12.cloned.1.call-start = ((), (), s32[]{:S(2)}) async-start(), calls=%async_computation.16 | async-start | bytes 7864320 | tf_op jit(solution)/shard_map/reduce_scatter | solution.py:173
  3526.7 1.9 copy-start.20
  3526.7 339.6 %copy-start.2 = (bf16[1024,1,1280]{2,0,1:T(8,128)(2,1)S(1)}, bf16[1024,1,1280]{2,0,1:T(8,128)(2,1)}, u32[]{:S(2)}) copy-start(bf16[1024,1,1280]{2,0,1:T(8,128)(2,1)} %param.16) | copy-start | bytes 7864324
  3526.7 339.6 %copy-start.13 = (f32[1280]{0:T(1024)S(1)}, f32[1280]{0:T(1024)}, u32[]{:S(2)}) copy-start(f32[1280]{0:T(1024)} %param.18) | copy-start | bytes 15364
  3526.7 339.6 %copy-start.15 = (f32[1024]{0:T(1024)S(1)}, f32[1024]{0:T(1024)}, u32[]{:S(2)}) copy-start(f32[1024]{0:T(1024)} %copy-done.14) | copy-start | bytes 12292
  3526.7 407.5 %copy-start.10 = (f32[1280]{0:T(1024)S(1)}, f32[1280]{0:T(1024)}, u32[]{:S(2)}) copy-start(f32[1280]{0:T(1024)} %param.22) | copy-start | bytes 15364
  3526.7 407.5 %copy-start.12 = (f32[1024]{0:T(1024)S(1)}, f32[1024]{0:T(1024)}, u32[]{:S(2)}) copy-start(f32[1024]{0:T(1024)} %copy-done.11) | copy-start | bytes 12292
  3526.7 407.5 %copy-start.17 = (f32[1024]{0:T(1024)S(1)}, f32[1024]{0:T(1024)}, u32[]{:S(2)}) copy-start(f32[1024]{0:T(1024)} %copy-done.16) | copy-start | bytes 12292
  3526.7 407.5 %copy-start.19 = (f32[1280]{0:T(1024)S(1)}, f32[1280]{0:T(1024)}, u32[]{:S(2)}) copy-start(f32[1280]{0:T(1024)} %param.26) | copy-start | bytes 15364
  3869.7 74.4 %copy-start.18 = (f32[1280]{0:T(1024)S(1)}, f32[1280]{0:T(1024)}, u32[]{:S(2)}) copy-start(f32[1280]{0:T(1024)} %get-tuple-element.211) | copy-start | bytes 15364
  3869.7 114.9 %copy-start.29 = (f32[80]{0:T(128)S(1)}, f32[80]{0:T(128)}, u32[]{:S(2)}) copy-start(f32[80]{0:T(128)} %param.19) | copy-start | bytes 964
  (4 other events, 2.5 us)
Sparse Core Ops, SparseCore 0:
  14.2 71.2 all-gather.12
  87.7 54.3 all-gather.14
  161.9 68.7 all-gather.30
  232.1 70.1 all-gather.28
  304.4 39.9 all-gather.16
  935.7 121.8 reduce-scatter.9
  1059.8 39.9 all-gather.20
  1101.8 67.4 all-gather.18
  1171.5 39.9 all-gather.22
  1212.9 67.4 all-gather.24
  1299.3 121.8 reduce-scatter.13
  1432.4 68.5 all-gather.26
  3155.2 153.1 reduce-scatter.15
  3311.0 153.1 reduce-scatter.17
  3467.7 59.3 reduce-scatter.25
  3531.2 58.4 reduce-scatter.23
  3593.3 58.4 reduce-scatter.21
  3655.8 142.4 all-reduce.3
  3800.6 65.6 reduce-scatter.19
  3868.5 65.6 reduce-scatter.11
where the time goes:
time: 4000 us; the launch traced here: 3990 us
  matrix products  1630 us (41%)
  waiting for transfers between devices  1440 us (36%)
  other arithmetic  696 us (17%)
  local copies, waits for them, and re-layouts  169 us (4%)
  blocking collectives  40.5 us (1%)
    convert_element_type x4, other arithmetic, one_block(): grad_low = grad_scores.astype(jnp.bfloat16)  418 us
    dot_general x8, matrix products, block_scores(): jnp.einsum('qshe,kshe->shqk', q_block, keys_all, preferred_element_type=j...  400 us
    dot_general x4, matrix products, one_block(): jnp.einsum('qshe,kshe->shqk', g_block, values_all, preferred_element_type...  387 us
    dot_general x4, matrix products, one_block(): jnp.einsum('shqk,qshe->kshe', probs.astype(jnp.bfloat16), g_block, prefer...  229 us
    dot_general x4, matrix products, one_block(): jnp.einsum('shqk,kshe->qshe', probs, values_all, preferred_element_type=j...  206 us
    reduce_sum x4, other arithmetic, one_block(): row_total = jnp.sum(exponent, axis=-1, keepdims=True)  175 us
    reduce_scatter x1, waiting for transfers between devices, per_device(): lax.psum_scatter(grad_values_all.reshape(total_rows, sequences, width_loc...  151 us
    unnamed x21, waiting for transfers between devices  149 us
  transfers between devices with their start and end apart: 20, of which 18 were waited for; matrix products, arithmetic and copies ran while one was open for 19% of the time, Pallas kernels for 0%

commit v1 on v0

v1 whole, which is shorter than its diff:
```python
import functools
import math

import jax
import jax.numpy as jnp
from jax import lax
from jax.experimental import pallas as pl
from jax.experimental.layout import Layout, with_layout_constraint
from jax.experimental.pallas import tpu as pltpu
from jax.sharding import PartitionSpec as P

HD = 80
IDS = 32
BLOCK_Q = 512
BLOCK_K = 512
EPSILON = 1e-06
LOG_TWO_E = 1.442695041
LOG2E = 1.4426950408889634
NEGATIVE = -1e30
VMEM_BYTES = 60 << 20
bf16, f32 = jnp.bfloat16, jnp.float32


def dot(a, b, contract_a, contract_b):
    return lax.dot_general(
        a, b, ((contract_a, contract_b), ((), ())), preferred_element_type=f32
    )


def nn(a, b):
    return dot(a, b, (1,), (0,))


def nt(a, b):
    return dot(a, b, (1,), (1,))


def attend_body(lo_ref, clean_ref, x_ref, start_ref, o_ref, wide_ref, lse_ref, key_rows, *, chunks, chunk):
    per_q, per_k = chunk // BLOCK_Q, chunk // BLOCK_K
    for c in range(chunks):
        key_rows[pl.ds(c * chunk, chunk), :] = x_ref[c, 0, 1].T

    def query_block(i, _):
        c = i // per_q
        off = pl.multiple_of((i % per_q) * BLOCK_Q, BLOCK_Q)
        q = x_ref[c, 0, 0, :, pl.ds(off, BLOCK_Q)]
        first = start_ref[0, pl.ds(c, 1), pl.ds(off, BLOCK_Q)]
        query_pos = i * BLOCK_Q + lax.broadcasted_iota(jnp.int32, (BLOCK_K, BLOCK_Q), 1)
        key_iota = lax.broadcasted_iota(jnp.int32, (BLOCK_K, BLOCK_Q), 0)

        def step(masked, j, carry):
            top, total, acc = carry
            k = key_rows[pl.ds(pl.multiple_of(j * BLOCK_K, BLOCK_K), BLOCK_K), :]
            scores = nn(k, q) * LOG2E
            if masked:
                key_pos = j * BLOCK_K + key_iota
                scores = jnp.where((key_pos <= query_pos) & (key_pos >= first), scores, NEGATIVE)
            new_top = jnp.maximum(top, jnp.max(scores, axis=0, keepdims=True))
            weights = jnp.exp2(scores - new_top)
            shrink = jnp.exp2(top - new_top)
            total = total * shrink + jnp.sum(weights, axis=0, keepdims=True)
            v = x_ref[j // per_k, 0, 2, :, pl.ds(pl.multiple_of((j % per_k) * BLOCK_K, BLOCK_K), BLOCK_K)]
            acc = acc * shrink + nn(v, weights.astype(bf16))
            return new_top, total, acc

        carry = (
            jnp.full((1, BLOCK_Q), NEGATIVE, f32),
            jnp.zeros((1, BLOCK_Q), f32),
            jnp.zeros((HD, BLOCK_Q), f32),
        )
        diagonal = (i * BLOCK_Q) // BLOCK_K
        end = (i * BLOCK_Q + BLOCK_Q - 1) // BLOCK_K + 1
        carry = lax.fori_loop(diagonal, end, functools.partial(step, True), carry)
        carry = lax.fori_loop(clean_ref[i], diagonal, functools.partial(step, False), carry)
        carry = lax.fori_loop(lo_ref[i], clean_ref[i], functools.partial(step, True), carry)
        top, total, acc = carry
        result = acc / total
        o_ref[c, :, pl.ds(off, BLOCK_Q)] = result.astype(bf16)
        wide_ref[c, :, pl.ds(off, BLOCK_Q)] = result
        lse_ref[0, pl.ds(c, 1), pl.ds(off, BLOCK_Q)] = top + jnp.log2(total)
        return 0

    lax.fori_loop(0, chunks * per_q, query_block, 0)


def attend_back_body(
    hi_ref, clean_ref, x_ref, g_ref, wide_ref, lse_ref, start_ref, scale_ref,
    dx_ref, part_ref, dq, dk, dv, delta, *, chunks, chunk,
):
    per_q, per_k = chunk // BLOCK_Q, chunk // BLOCK_K
    for c in range(chunks):
        delta[c : c + 1, :] = jnp.sum(g_ref[c].astype(f32) * wide_ref[c], axis=0, keepdims=True)
        dq[c] = jnp.zeros((HD, chunk), f32)

    def key_block(j, _):
        cj = j // per_k
        koff = pl.multiple_of((j % per_k) * BLOCK_K, BLOCK_K)
        kt = x_ref[cj, 0, 1, :, pl.ds(koff, BLOCK_K)]
        k = kt.T
        v = x_ref[cj, 0, 2, :, pl.ds(koff, BLOCK_K)].T
        dk[...] = jnp.zeros_like(dk)
        dv[...] = jnp.zeros_like(dv)
        key_pos = j * BLOCK_K + lax.broadcasted_iota(jnp.int32, (BLOCK_K, BLOCK_Q), 0)
        query_iota = lax.broadcasted_iota(jnp.int32, (BLOCK_K, BLOCK_Q), 1)

        def step(masked, i, _):
            c = i // per_q
            off = pl.multiple_of((i % per_q) * BLOCK_Q, BLOCK_Q)
            q = x_ref[c, 0, 0, :, pl.ds(off, BLOCK_Q)]
            g = g_ref[c, :, pl.ds(off, BLOCK_Q)]
            scores = nn(k, q) * LOG2E
            if masked:
                first = start_ref[0, pl.ds(c, 1), pl.ds(off, BLOCK_Q)]
                query_pos = i * BLOCK_Q + query_iota
                scores = jnp.where((key_pos <= query_pos) & (key_pos >= first), scores, NEGATIVE)
            probs = jnp.exp2(scores - lse_ref[0, pl.ds(c, 1), pl.ds(off, BLOCK_Q)])
            grad_raw = probs * (nn(v, g) - delta[pl.ds(c, 1), pl.ds(off, BLOCK_Q)])
            low = grad_raw.astype(bf16)
            dv[...] += nt(g, probs.astype(bf16))
            dk[...] += nt(q, low)
            dq[c, :, pl.ds(off, BLOCK_Q)] += nn(kt, low)
            return 0

        diagonal = (j * BLOCK_K) // BLOCK_Q
        end = (j * BLOCK_K + BLOCK_K - 1) // BLOCK_Q + 1
        lax.fori_loop(diagonal, end, functools.partial(step, True), 0)
        lax.fori_loop(end, clean_ref[j], functools.partial(step, False), 0)
        lax.fori_loop(clean_ref[j], hi_ref[j], functools.partial(step, True), 0)
        dx_ref[cj, 1, :, pl.ds(koff, BLOCK_K)] = dk[...].astype(bf16)
        dx_ref[cj, 2, :, pl.ds(koff, BLOCK_K)] = dv[...].astype(bf16)
        return 0

    lax.fori_loop(0, chunks * per_k, key_block, 0)
    part = jnp.zeros((HD, 128), f32)
    for c in range(chunks):
        grad = dq[c]
        dx_ref[c, 0] = (grad * scale_ref[:, 0:1]).astype(bf16)
        term = grad * x_ref[c, 0, 0].astype(f32)
        for u in range(chunk // 128):
            part = part + term[:, u * 128 : (u + 1) * 128]
    part_ref[...] = part


def kernel_cost(length, matmuls):
    pairs = length * 2048
    return pl.CostEstimate(
        flops=matmuls * 512 * pairs, bytes_accessed=length * 2048, transcendentals=pairs
    )


def attend(tables, x, start, p):
    chunks, _, _, _, chunk = x.shape
    flat = lambda g, *_: (0, 0, 0)
    return pl.pallas_call(
        functools.partial(attend_body, chunks=chunks, chunk=chunk),
        grid_spec=pltpu.PrefetchScalarGridSpec(
            num_scalar_prefetch=2,
            grid=(1,),
            in_specs=[
                pl.BlockSpec((chunks, 1, 3, HD, chunk), lambda g, *_: (0, p, 0, 0, 0)),
                pl.BlockSpec((1, chunks, chunk), flat),
            ],
            out_specs=[
                pl.BlockSpec((chunks, HD, chunk), flat),
                pl.BlockSpec((chunks, HD, chunk), flat),
                pl.BlockSpec((1, chunks, chunk), flat),
            ],
            scratch_shapes=[pltpu.VMEM((chunks * chunk, HD), bf16)],
        ),
        out_shape=[
            jax.ShapeDtypeStruct((chunks, HD, chunk), bf16),
            jax.ShapeDtypeStruct((chunks, HD, chunk), f32),
            jax.ShapeDtypeStruct((1, chunks, chunk), f32),
        ],
        compiler_params=pltpu.CompilerParams(vmem_limit_bytes=VMEM_BYTES),
        cost_estimate=kernel_cost(chunks * chunk, 2),
        name="attend",
    )(*tables, x, start)


def attend_back(tables, x, grad, wide, lse, start, scale, p):
    chunks, _, _, _, chunk = x.shape
    flat = lambda g, *_: (0, 0, 0)
    return pl.pallas_call(
        functools.partial(attend_back_body, chunks=chunks, chunk=chunk),
        grid_spec=pltpu.PrefetchScalarGridSpec(
            num_scalar_prefetch=2,
            grid=(1,),
            in_specs=[
                pl.BlockSpec((chunks, 1, 3, HD, chunk), lambda g, *_: (0, p, 0, 0, 0)),
                pl.BlockSpec((chunks, HD, chunk), flat),
                pl.BlockSpec((chunks, HD, chunk), flat),
                pl.BlockSpec((1, chunks, chunk), flat),
                pl.BlockSpec((1, chunks, chunk), flat),
                pl.BlockSpec((HD, 128), lambda g, *_: (0, 0)),
            ],
            out_specs=[
                pl.BlockSpec((chunks, 3, HD, chunk), lambda g, *_: (0, 0, 0, 0)),
                pl.BlockSpec((HD, 128), lambda g, *_: (0, 0)),
            ],
            scratch_shapes=[
                pltpu.VMEM((chunks, HD, chunk), f32),
                pltpu.VMEM((HD, BLOCK_K), f32),
                pltpu.VMEM((HD, BLOCK_K), f32),
                pltpu.VMEM((chunks, chunk), f32),
            ],
        ),
        out_shape=[
            jax.ShapeDtypeStruct((chunks, 3, HD, chunk), bf16),
            jax.ShapeDtypeStruct((HD, 128), f32),
        ],
        compiler_params=pltpu.CompilerParams(vmem_limit_bytes=VMEM_BYTES),
        cost_estimate=kernel_cost(chunks * chunk, 5),
        name="attend_back",
    )(*tables, x, grad, wide, lse, start, scale)


def weight_grad_body(me_ref, *refs, spots):
    n = len(spots)
    pieces, (w_ref, *dxs), (out_ref, gain_ref), (buffers, acc, lhs, sems) = (
        refs[:n], refs[n:-6], refs[-6:-4], refs[-4:]
    )
    features = 3 * HD

    def copy(i):
        rows = spots[i][2]
        return pltpu.make_async_copy(pieces[i], buffers.at[i % 2, pl.ds(0, rows)], sems.at[i % 2])

    copy(0).start()
    for i, (distance, first, rows) in enumerate(spots):
        if i + 1 < n:
            copy(i + 1).start()
        chunk = me_ref[0] ^ distance
        for p, dx in enumerate(dxs):
            for c in range(3):
                lhs[p * features + c * HD : p * features + (c + 1) * HD, 0:rows] = dx[
                    chunk, c, :, first : first + rows
                ]
        copy(i).wait()
        width = acc.shape[1]
        for lane in range(0, width, 256):
            part = nn(lhs[:, 0:rows], buffers[i % 2, 0:rows, lane : lane + 256])
            if i:
                part = part + acc[:, lane : lane + 256]
            acc[:, lane : lane + 256] = part
    total = acc[...]
    out_ref[...] = total.astype(bf16)
    gain_ref[...] = jnp.sum(total * w_ref[...].astype(f32), axis=0, keepdims=True)


def weight_grad(me, pieces, spots, w_rows, dxs):
    features, width = w_rows.shape
    rows = max(n for _, _, n in spots)
    whole = pl.BlockSpec(memory_space=pltpu.VMEM)
    return pl.pallas_call(
        functools.partial(weight_grad_body, spots=spots),
        in_specs=[pl.BlockSpec(memory_space=pltpu.SMEM)]
        + [pl.BlockSpec(memory_space=pl.ANY)] * len(pieces)
        + [whole] * (1 + len(dxs)),
        out_specs=[whole, whole],
        out_shape=[
            jax.ShapeDtypeStruct((features, width), bf16),
            jax.ShapeDtypeStruct((1, width), f32),
        ],
        scratch_shapes=[
            pltpu.VMEM((2, rows, width), bf16),
            pltpu.VMEM((features, width), f32),
            pltpu.VMEM((features, rows), bf16),
            pltpu.SemaphoreType.DMA((2,)),
        ],
        compiler_params=pltpu.CompilerParams(vmem_limit_bytes=VMEM_BYTES),
        cost_estimate=pl.CostEstimate(
            flops=2 * features * width * sum(n for _, _, n in spots),
            bytes_accessed=2 * width * sum(n for _, _, n in spots),
            transcendentals=0,
        ),
        name="weight_grad",
    )(me, *pieces, w_rows, *dxs)


def block_tables(segments):
    length = segments.shape[0]
    ids = jnp.arange(IDS, dtype=jnp.int32)
    below = jnp.sum(segments[None, :] < ids[:, None], axis=1, dtype=jnp.int32)
    upto = jnp.sum(segments[None, :] <= ids[:, None], axis=1, dtype=jnp.int32)
    hot = segments[None, :] == ids[:, None]
    start = jnp.sum(jnp.where(hot, below[:, None], 0), axis=0)
    end = jnp.sum(jnp.where(hot, upto[:, None], 0), axis=0) - 1
    q_block = jnp.arange(length // BLOCK_Q, dtype=jnp.int32)
    k_block = jnp.arange(length // BLOCK_K, dtype=jnp.int32)
    start_first, start_last = start[::BLOCK_Q], start[BLOCK_Q - 1 :: BLOCK_Q]
    lo = start_first // BLOCK_K
    clean = (start_last + BLOCK_K - 1) // BLOCK_K
    clean = jnp.maximum(jnp.minimum(clean, q_block * BLOCK_Q // BLOCK_K), lo)
    end_first, end_last = end[::BLOCK_K], end[BLOCK_K - 1 :: BLOCK_K]
    after = (k_block * BLOCK_K + BLOCK_K - 1) // BLOCK_Q + 1
    hi = end_last // BLOCK_Q + 1
    q_clean = jnp.minimum(jnp.maximum((end_first + 1) // BLOCK_Q, after), hi)
    return start, (lo, clean), (hi, q_clean)


def in_rows(grad):
    return with_layout_constraint(grad.astype(bf16), Layout((0, 1)))


def inverse_rms(values):
    return lax.rsqrt(jnp.mean(values * values, axis=-1, keepdims=True) + EPSILON)


def norm_back(grad_norm, unit, inverse, gain):
    grad_unit = grad_norm * gain
    return inverse * (grad_unit - unit * jnp.mean(grad_unit * unit, axis=-1, keepdims=True))


def per_device(
    tokens,
    segments,
    gain_attn,
    query_scale,
    w_qkv,
    w_out,
    gain_mlp,
    w_up,
    b_up,
    w_down,
    b_down,
    cotangent,
):
    n_dp, n_ctx, n_tensor = (lax.axis_size(a) for a in ("dp", "ctx", "tensor"))
    ctx_rank, tensor_rank = lax.axis_index("ctx"), lax.axis_index("tensor")
    rows, sequences, width = tokens.shape
    shard, columns = w_qkv.shape[1:]
    local_heads = columns // HD
    group = n_ctx * n_tensor
    length = rows * group
    data = ("dp", "ctx")
    everyone = ("dp", "ctx", "tensor")
    split = local_heads % n_ctx == 0
    ctx_parts = n_ctx if split else 1
    own = local_heads // ctx_parts
    owners = ("ctx", "tensor") if split else ("tensor",)
    n_owners = ctx_parts * n_tensor
    head_width = own * 3 * HD

    inputs = tokens[:, 0].astype(f32)
    inverse_one = inverse_rms(inputs)
    unit_one = inputs * inverse_one
    normed_one = (unit_one * gain_attn).astype(bf16)

    def tensor_pair(x):
        if n_tensor != 2:
            return lax.all_gather(x, "tensor", axis=0)
        other = lax.ppermute(x, "tensor", [(0, 1), (1, 0)])
        first = tensor_rank == 0
        return jnp.stack([jnp.where(first, x, other), jnp.where(first, other, x)])

    def scatter_pair(x):
        if n_tensor != 2:
            return lax.psum_scatter(x, "tensor", scatter_dimension=0, tiled=False).astype(f32)
        keep = jnp.where(tensor_rank == 0, x[0], x[1])
        send = jnp.where(tensor_rank == 0, x[1], x[0])
        return keep.astype(f32) + lax.ppermute(send, "tensor", [(0, 1), (1, 0)]).astype(f32)

    def by_distance(x, rank):
        count = x.shape[0]
        bit = 1
        while bit < count:
            y = x.reshape((count // (2 * bit), 2, bit) + x.shape[1:])
            y = jnp.where((rank & bit) > 0, jnp.flip(y, 1), y)
            x = y.reshape(x.shape)
            bit *= 2
        return x

    def exchange(x, axis, rank):
        count = x.shape[0]
        if count & (count - 1):
            return lax.all_to_all(x, axis, 0, 0)
        x = by_distance(x, rank)
        got = [x[0]] + [
            lax.ppermute(x[k], axis, [(i, i ^ k) for i in range(count)]) for k in range(1, count)
        ]
        return by_distance(jnp.stack(got), rank)

    qkv_rows = w_qkv.reshape(3, shard, ctx_parts, own, HD)
    for_owner = qkv_rows.transpose(2, 1, 3, 0, 4).reshape(ctx_parts, shard, head_width)
    if split:
        for_owner = exchange(for_owner, "ctx", ctx_rank)
        normed_one, for_owner = lax.optimization_barrier((normed_one, for_owner))
        owner_w = lax.all_gather(for_owner, "dp", axis=0).reshape(width, head_width)
    else:
        owner_w = lax.all_gather(for_owner[0], data, axis=0).reshape(width, head_width)

    start, forward_tables, backward_tables = block_tables(segments[0])
    qkv_cols = w_qkv.reshape(3, shard, ctx_parts, own, HD).transpose(1, 3, 2, 0, 4)
    out_cols = w_out.T.reshape(shard, ctx_parts, own, HD).transpose(0, 2, 1, 3)
    pair = tensor_pair(
        jnp.concatenate(
            [qkv_cols.reshape(shard, 3 * columns), out_cols.reshape(shard, columns), w_up, w_down.T], axis=1
        )
    )

    def interleave(x, inner):
        x = x.reshape(n_tensor, shard, own * ctx_parts, inner)
        return x.transpose(1, 2, 0, 3).reshape(shard, -1)

    def side_by_side(x):
        return x.transpose(1, 0, 2).reshape(shard, -1)

    full_rows = jnp.stack(
        [
            interleave(pair[..., 3 * columns : 4 * columns], HD),
            side_by_side(pair[..., 4 * columns : 5 * columns]),
            side_by_side(pair[..., 5 * columns :]),
        ]
    )
    qkv_rows_full = interleave(pair[..., : 3 * columns], 3 * HD)
    heads_x = jnp.zeros((group, head_width, rows), bf16)
    scaling = LOG_TWO_E / math.sqrt(HD) * jax.nn.softplus(query_scale)
    scale_rows = jnp.tile(
        jnp.concatenate([scaling, jnp.ones((2 * HD,), f32)]), own
    )[:, None]

    def project(piece):
        return (dot(owner_w, piece, (0,), (1,)) * scale_rows).astype(bf16)

    if group == 8 and n_tensor == 2:
        me = ctx_rank * n_tensor + tensor_rank

        def swap(x, bit):
            return lax.ppermute(x, ("ctx", "tensor"), [(i, i ^ bit) for i in range(group)])

        def add(heads_x, at, piece):
            distance, first, _ = at
            return lax.dynamic_update_slice(heads_x, project(piece)[None], (me ^ distance, 0, first))

        half = rows // 2
        spots = [(0, 0, rows), (2, 0, rows)]
        pieces = [normed_one, swap(normed_one, 2)]
        for at, piece in zip(spots, pieces, strict=True):
            heads_x = add(heads_x, at, piece)
        w_rows = owner_w.T
        (over_x, over_y, heads_x, w_rows, full_rows, qkv_rows_full, start, forward_tables, backward_tables) = (
            lax.optimization_barrier(
                (swap(normed_one, 1), swap(normed_one, 4), heads_x, w_rows, full_rows, qkv_rows_full,
                 start, forward_tables, backward_tables)
            )
        )
        corner_low = swap(over_x[:half], 4)
        corner_high = swap(over_y[half:], 1)
        for at, piece in (
            ((1, 0, rows), over_x),
            ((4, 0, rows), over_y),
            ((5, 0, half), corner_low),
            ((5, half, half), corner_high),
        ):
            for bit in (0, 2):
                spots.append((at[0] ^ bit, *at[1:]))
                pieces.append(swap(piece, 2) if bit else piece)
                heads_x = add(heads_x, spots[-1], pieces[-1])
    else:
        spots = None
        normed_all = lax.all_gather(normed_one, ("ctx", "tensor"), axis=0)
        heads_x = project(normed_all.reshape(length, width)).reshape(head_width, group, rows).transpose(1, 0, 2)

    whole = lax.all_gather(full_rows, data, axis=1, tiled=True)
    out_t, up_all, down_t = whole[0], whole[1], whole[2]
    qkv_all = lax.all_gather(qkv_rows_full, data, axis=0, tiled=True)

    chunk = max(rows, BLOCK_Q, BLOCK_K)
    merge = chunk // rows
    chunks = length // chunk

    def to_chunks(x):
        if merge == 1:
            return x
        x = jnp.moveaxis(x.reshape((chunks, merge) + x.shape[1:]), 1, -2)
        return x.reshape(x.shape[:-2] + (chunk,))

    def from_chunks(x):
        if merge == 1:
            return x
        x = jnp.moveaxis(x.reshape(x.shape[:-1] + (merge, rows)), -2, 1)
        return x.reshape((group,) + x.shape[2:])

    def to_tokens(x):
        x = from_chunks(x)
        if not split:
            x = lax.dynamic_slice_in_dim(x, ctx_rank * n_tensor, n_tensor, 0)
        return lax.all_to_all(x, owners, 0, 0)

    def to_heads(x):
        x = lax.all_to_all(x, owners, 0, 0)
        if not split:
            x = lax.all_gather(x, "ctx", axis=0, tiled=True)
        return to_chunks(x)

    heads_x = to_chunks(heads_x)
    heads_x = heads_x.reshape(chunks, own, 3, HD, chunk)
    start = start.reshape(1, chunks, chunk)

    part = n_owners * HD

    mixed, wides, lses = [], [], []
    for p in range(own):
        o, wide, lse = attend(forward_tables, heads_x, start, p)
        wides.append(wide)
        lses.append(lse)
        mixed.append(to_tokens(o).reshape(part, rows))

    hidden = inputs
    for p in range(own):
        hidden = hidden + dot(mixed[p], out_t[:, p * part : (p + 1) * part], (0,), (1,))
    inverse_two = inverse_rms(hidden)
    unit_two = hidden * inverse_two
    normed_two = (unit_two * gain_mlp).astype(bf16)
    pre_act = nn(normed_two, up_all) + b_up
    sigma = jax.nn.sigmoid(pre_act)
    activation = (pre_act * sigma).astype(bf16)
    outputs = (hidden + (nt(activation, down_t) + b_down)).astype(bf16)

    top_low = cotangent[:, 0]
    grad_top = top_low.astype(f32)
    grad_pre = (nn(top_low, down_t) * (sigma * (1 + pre_act * (1 - sigma)))).astype(bf16)
    grad_normed_two = nt(grad_pre, up_all)
    grad_hidden = grad_top + norm_back(grad_normed_two, unit_two, inverse_two, gain_mlp)
    grad_hidden_low = grad_hidden.astype(bf16)
    grad_heads = [
        to_heads(nt(out_t[:, p * part : (p + 1) * part].T, grad_hidden_low).astype(bf16).reshape(n_owners, HD, rows))
        for p in range(own)
    ]
    grad_out_t = [dot(grad_hidden_low, m, (0,), (1,)) for m in mixed]
    grad_up = dot(normed_two, grad_pre, (0,), (0,))
    grad_down_t = dot(top_low, activation, (0,), (0,))
    stacked = jnp.concatenate([in_rows(g) for g in (*grad_out_t, grad_up, grad_down_t)], axis=1)
    stacked, qkv_all = lax.optimization_barrier((stacked, qkv_all))
    reduced = lax.psum_scatter(stacked, data, scatter_dimension=0, tiled=True)
    reduced = [reduced[:, n * width : (n + 1) * width] for n in range(3)]
    gain_two = jnp.sum(grad_normed_two * unit_two, axis=0)
    bias_up = jnp.sum(grad_pre.astype(f32), axis=0)
    bias_down = jnp.sum(grad_top, axis=0)
    split_out = reduced[0].reshape(shard, own, ctx_parts, n_tensor, HD).transpose(3, 0, 2, 1, 4)
    split_up, split_down = (
        reduced[n].reshape(shard, n_tensor, columns).transpose(1, 0, 2) for n in (1, 2)
    )
    mine = scatter_pair(
        jnp.stack([split_out.reshape(n_tensor, shard, columns), split_up, split_down], axis=1)
    )
    out_grad, up_grad, down_grad = mine[0].T, mine[1], mine[2].T

    scale_tile = jnp.broadcast_to(scaling[:, None], (HD, 128))
    scale_sum = jnp.zeros((HD,), f32)
    gain_part = jnp.zeros((width,), f32)
    dxs, backs = [], []
    for p in range(own):
        if p:
            heads_x, grad_heads[p], dxs[p - 1] = lax.optimization_barrier((heads_x, grad_heads[p], dxs[p - 1]))
        dx, part_sum = attend_back(
            backward_tables, heads_x, grad_heads[p], wides[p], lses[p], start, scale_tile, p
        )
        scale_sum = scale_sum + jnp.sum(part_sum, axis=1)
        if p:
            dx, backs[-1] = lax.optimization_barrier((dx, backs[-1]))
        dxs.append(dx)
        backs.append(to_tokens(dx).reshape(3 * part, rows))
    if spots is None:
        grad_ws = []
        for p in range(own):
            grad_w = lax.dot_general(
                to_chunks(jnp.swapaxes(normed_all, 1, 2)),
                dxs[p].reshape(chunks, 3 * HD, chunk),
                (((0, 2), (0, 2)), ((), ())),
                preferred_element_type=f32,
            )
            weights_p = owner_w.reshape(width, own, 3 * HD)[:, p].astype(f32)
            gain_part = gain_part + jnp.sum(grad_w * weights_p, axis=1)
            grad_ws.append(grad_w.astype(bf16))
        piece = jnp.concatenate(grad_ws, axis=1)
    else:
        piece, gain_part = weight_grad(me.reshape(1), pieces, spots, w_rows, dxs)
        piece, gain_part = piece.T, gain_part[0]
    piece = piece.reshape(n_dp, n_ctx * shard, head_width)
    gain_one, scale_sum = gain_part / gain_attn, scale_sum / scaling
    if not split:
        once = (ctx_rank == 0).astype(f32)
        gain_one, scale_sum = gain_one * once, scale_sum * once
    def back_one(p):
        return dot(backs[p], qkv_all[:, p * 3 * part : (p + 1) * 3 * part], (0,), (1,))

    grad_normed_one = sum((back_one(p) for p in range(own - 1)), jnp.zeros((), f32))
    dp_rank = lax.axis_index("dp")
    sums = jnp.concatenate([gain_one, gain_two, bias_up, bias_down, scale_sum])
    if n_dp == 4 and n_ctx == 4 and n_tensor == 2:

        def across(x, axis, bit):
            return lax.ppermute(x, axis, [(i, i ^ bit) for i in range(lax.axis_size(axis))])

        for bit in (2, 1):
            upper = (dp_rank & bit) > 0
            kept = jnp.where(upper, piece[bit:], piece[:bit])
            sent = jnp.where(upper, piece[:bit], piece[bit:])
            piece = (kept.astype(f32) + across(sent, "dp", bit).astype(f32)).astype(bf16)
            sums = sums + across(sums, "dp", bit)
            piece, sums, out_grad, up_grad, down_grad = lax.optimization_barrier(
                (piece, sums, out_grad, up_grad, down_grad)
            )
        piece = piece[0]
        backs[-1], piece, sums, grad_normed_one = lax.optimization_barrier(
            (backs[-1], piece, sums, grad_normed_one)
        )
        sums = sums + across(sums, "ctx", 1) + across(sums, "ctx", 2) + across(sums, "ctx", 3)
        sums = sums + across(sums, "tensor", 1)
    else:
        piece = jnp.sum(lax.all_to_all(piece, "dp", 0, 0).astype(f32), axis=0).astype(bf16)
        sums = lax.psum(sums, everyone)
    piece = piece.reshape(n_ctx, shard, head_width)
    if split:
        piece = exchange(piece, "ctx", ctx_rank)
    else:
        piece = lax.dynamic_slice_in_dim(piece, ctx_rank, 1, 0)
    qkv_grad = piece.reshape(ctx_parts, shard, own, 3, HD).transpose(3, 1, 0, 2, 4)
    qkv_grad = qkv_grad.reshape(w_qkv.shape).astype(f32)

    grad_normed_one = grad_normed_one + back_one(own - 1)
    grad_inputs = grad_hidden + norm_back(grad_normed_one, unit_one, inverse_one, gain_attn)
    gain_one, gain_two, bias_up, bias_down = (sums[n * width : (n + 1) * width] for n in range(4))
    grad_query_scale = sums[4 * width :] * (LOG_TWO_E / math.sqrt(HD)) * jax.nn.sigmoid(query_scale)
    return (
        outputs[:, None],
        grad_inputs.astype(bf16)[:, None],
        qkv_grad,
        out_grad,
        up_grad,
        down_grad,
        gain_one,
        grad_query_scale,
        gain_two,
        bias_up,
        bias_down,
    )


def solution(mesh):
    placed = (
        P(("ctx", "tensor"), "dp", None),
        P("dp", None),
        P(),
        P(),
        P(None, ("dp", "ctx"), "tensor"),
        P("tensor", ("dp", "ctx")),
        P(),
        P(("dp", "ctx"), "tensor"),
        P(),
        P("tensor", ("dp", "ctx")),
        P(),
        P(("ctx", "tensor"), "dp", None),
    )
    return jax.shard_map(
        per_device,
        mesh=mesh,
        in_specs=placed,
        out_specs=(
            P(("ctx", "tensor"), "dp", None),
            P(("ctx", "tensor"), "dp", None),
            P(None, ("dp", "ctx"), "tensor"),
            P("tensor", ("dp", "ctx")),
            P(("dp", "ctx"), "tensor"),
            P("tensor", ("dp", "ctx")),
            P(),
            P(),
            P(),
            P(),
            P(),
        ),
        check_vma=False,
    )
```

time: 4000 us -> 620 us (0.15)
  matrix products: 1630 us -> 124 us
  waiting for transfers between devices: 1440 us -> 85.6 us
  other arithmetic: 696 us -> 41.7 us
  Pallas kernels: 0 us -> 208 us
  local copies, waits for them, and re-layouts: 169 us -> 59.4 us
  starting transfers between devices: 1.2 us -> 80.3 us
  blocking collectives: 40.5 us -> 0 us
    dot_general x40 -> x24, matrix products: 1630 us -> 124 us  [dot(): lax.dot_general(a, b, ((contract_a, contract_b), ((), ())), preferred_ele...]
    reduce_scatter x9 -> x1, waiting for transfers between devices: 755 us -> 0.02 us  [per_device(): reduced = lax.psum_scatter(stacked, data, scatter_dimension=0, tiled=True)]
    all_gather x10 -> x3, waiting for transfers between devices: 534 us -> 10.4 us  [the longest x1 10.4 us: per_device(): owner_w = lax.all_gather(for_owner, 'dp', axis=0).reshape(width, head_width)]
    convert_element_type x13 -> x4, other arithmetic: 446 us -> 3.65 us  [the longest x1 2.15 us: per_device(): normed_one = (unit_one * gain_attn).astype(bf16)]
    pallas_call x0 -> x5, Pallas kernels: none -> 208 us  [the longest x2 105 us: attend_back(): pl.pallas_call(functools.partial(attend_back_body, chunks=chunks, chunk=c...]
    reduce_sum x10 -> x7, other arithmetic: 195 us -> 4.68 us  [the longest x1 1.79 us: per_device(): bias_down = jnp.sum(grad_top, axis=0)]
    unnamed x21 -> x4, waiting for transfers between devices: 149 us -> 0.07 us
    dynamic_update_slice x9 -> x0, local copies, waits for them, and re-layouts: 110 us -> none  [the longest x8 109 us: attend_back(): lax.scan(one_block, (empty_sum, empty_sum), (jnp.arange(number, dtype=jnp...]
  transfers between devices with their start and end apart: 20 -> 35, of which waited for: 18 -> 7; matrix products, arithmetic and copies ran while one was open for 19% -> 34% of each run, Pallas kernels for 0% -> 34%
where the time goes in v1:
time: 620 us; the launch traced here: 614 us
  Pallas kernels  208 us (34%)
  matrix products  124 us (20%)
  waiting for transfers between devices  85.6 us (14%)
  starting transfers between devices  80.3 us (13%)
  local copies, waits for them, and re-layouts  59.4 us (10%)
  other arithmetic  41.7 us (7%)
  between operations  15.2 us (2%)
    dot_general x24, matrix products, dot(): lax.dot_general(a, b, ((contract_a, contract_b), ((), ())), preferred_ele...  124 us
    pallas_call x2, Pallas kernels, attend_back(): pl.pallas_call(functools.partial(attend_back_body, chunks=chunks, chunk=c...  105 us
    pallas_call x2, Pallas kernels, attend(): pl.pallas_call(functools.partial(attend_body, chunks=chunks, chunk=chunk)...  81.2 us
    ppermute x9, waiting for transfers between devices, swap(): lax.ppermute(x, ('ctx', 'tensor'), [(i, i ^ bit) for i in range(group)])  41.6 us
    ppermute x8, starting transfers between devices, across(): lax.ppermute(x, axis, [(i, i ^ bit) for i in range(lax.axis_size(axis))])  38.8 us
    pallas_call x1, Pallas kernels, weight_grad(): pl.pallas_call(functools.partial(weight_grad_body, spots=spots), in_specs...  21.9 us
    all_to_all x4, starting transfers between devices, to_tokens(): return lax.all_to_all(x, owners, 0, 0)  17.8 us
    all_to_all x2, waiting for transfers between devices, to_heads(): x = lax.all_to_all(x, owners, 0, 0)  13 us
  transfers between devices with their start and end apart: 35, of which 7 were waited for; matrix products, arithmetic and copies ran while one was open for 34% of the time, Pallas kernels for 34%

profile of v1, /device:TPU:0, one launch (start us, length us, event | category | flops | bytes accessed | tf_op | source)
XLA Modules:
  0.0 614.2 jit_solution(10838135854027342911)
XLA Ops:
  57.1 2.5 copy.144
  63.4 10.4 %all-gather.9.cloned.1.call-done = bf16[16,80,480]{2,1,0:T(8,128)(2,1)} async-done(((bf16[4,80,480]{2,1,0:T(8,128)(2,1)}), bf16[16,80,480]{2,1,0:T(8,128)(2,1)}) %all-gather.9.cloned.1.call-update) | async-done | bytes 1228816 | tf_op jit(solution)/shard_map/all_gather | solution.py:389
  73.8 2.5 copy.132
  76.3 4.2 broadcast_in_dim.79
  80.5 2.6 fusion.31
  83.0 4.3 fusion.33
  87.4 15.2 %collective-permute-done.3.refs_2_ = bf16[1024,1280]{1,0:T(8,128)(2,1)} collective-permute-done((bf16[1024,1280]{1,0:T(8,128)(2,1)}, bf16[1024,1280]{1,0:T(8,128)(2,1)}, u32[]{:S(2)}, u32[]{:S(2)}) %collective-permute-start.3) | collective-permute-done | bytes 2621472 | tf_op jit(solution)/shard_map/ppermute | solution.py:430
  103.5 2.5 slice.148
  107.6 2.5 slice.149
  112.3 5.0 fusion.35
  117.4 26.3 %collective-permute-done.9.refs_6_ = bf16[512,1280]{1,0:T(8,128)(2,1)} collective-permute-done((bf16[512,1280]{1,0:T(8,128)(2,1)}, bf16[512,1280]{1,0:T(8,128)(2,1)}, u32[]{:S(2)}, u32[]{:S(2)}) %collective-permute-start.9) | collective-permute-done | bytes 1310752 | tf_op jit(solution)/shard_map/ppermute | solution.py:430
  144.2 4.8 fusion.37
  149.0 4.4 fusion.39
  153.4 4.4 fusion.41
  157.7 3.1 fusion.53
  162.6 3.1 fusion.49
  167.5 40.8 %attend.2 = (bf16[8,80,1024]{2,1,0:T(8,128)(2,1)}, f32[8,80,1024]{2,1,0:T(8,128)}, f32[1,8,1024]{2,1,0:T(8,128)}) custom-call(s32[16]{0:T(128)} %get-tuple-element.59.lo_ref, s32[16]{0:T(128)} %get-tuple-element.60.clean_ref, bf16[8,2,3,80,1024]{4,3,2,1,0:T(8,128)(2,1)} %bitcast.44.x_ref, s32[1,8,1024]{2,1,0:T(8,128)} %reshape.165.start_ref), custom_call_target="tpu_custom_call" | custom-call | flops 17179869184 | bytes 16777216 | tf_op jit(solution)/shard_map/attend/pallas_call | solution.py:154
  208.3 4.3 all-to-all-start
  212.6 40.4 %attend.3 = (bf16[8,80,1024]{2,1,0:T(8,128)(2,1)}, f32[8,80,1024]{2,1,0:T(8,128)}, f32[1,8,1024]{2,1,0:T(8,128)}) custom-call(s32[16]{0:T(128)} %get-tuple-element.59.lo_ref, s32[16]{0:T(128)} %get-tuple-element.60.clean_ref, bf16[8,2,3,80,1024]{4,3,2,1,0:T(8,128)(2,1)} %bitcast.44.x_ref, s32[1,8,1024]{2,1,0:T(8,128)} %reshape.165.start_ref), custom_call_target="tpu_custom_call" | custom-call | flops 17179869184 | bytes 16777216 | tf_op jit(solution)/shard_map/attend/pallas_call | solution.py:154
  253.0 4.3 all-to-all-start.1
  257.4 2.4 slice_bitcast_fusion.2
  261.5 5.9 fusion.28
  267.4 7.6 %all-to-all-done.1 = bf16[8,80,1024]{2,1,0:T(8,128)(2,1)} async-done(((bf16[8,80,1024]{2,1,0:T(8,128)(2,1)}), bf16[8,80,1024]{2,1,0:T(8,128)(2,1)}, u32[]{:S(2)}, u32[]{:S(2)}) %all-to-all-start.1) | async-done | bytes 1310752 | tf_op jit(solution)/shard_map/all_to_all | solution.py:489
  275.0 6.1 multiply_reduce_fusion.2
  281.2 7.5 %fusion.21 = f32[1024,1280]{1,0:T(8,128)S(1)} fusion(bf16[3,1280,1280]{2,1,0:T(8,128)(2,1)} %all-gather.5.cloned.1.call-done, f32[1024,1280]{1,0:T(8,128)S(1)} %get-tuple-element.139, f32[1280]{0:T(1024)S(1)} %copy-done.24, f32[1024]{0:T(1024)S(1)} %add_rsqrt_fusion), kind=kOutput, calls=%fused_computation.42 | convolution fusion | flops 3359375360 | bytes 13771776 | tf_op jit(solution)/shard_map/dot_general | solution.py:25
  288.8 5.4 convert_reduce_fusion.1
  294.2 4.5 multiply_reduce_fusion
  301.1 4.5 convolution_convert_fusion.2
  305.6 3.6 convolution_convert_fusion.3
  309.2 4.2 convolution_convert_fusion.1
  313.4 4.9 fusion.3
  318.3 4.5 pad_maximum_fusion
  324.8 4.7 convolution_convert_fusion.4
  329.5 4.3 all-to-all-start.3
  333.8 4.7 convolution_convert_fusion.5
  338.5 13.0 %all-to-all-done.3.g_ref = bf16[8,80,1024]{2,1,0:T(8,128)(2,1)} async-done(((bf16[8,80,1024]{2,1,0:T(8,128)(2,1)}), bf16[8,80,1024]{2,1,0:T(8,128)(2,1)}, u32[]{:S(2)}, u32[]{:S(2)}) %all-to-all-start.3) | async-done | bytes 1310752 | tf_op jit(solution)/shard_map/all_to_all | solution.py:492
  351.5 3.6 all-to-all-start.2
  355.8 52.4 %attend_back.2 = (bf16[8,3,80,1024]{3,2,1,0:T(8,128)(2,1)}, f32[80,128]{1,0:T(8,128)}) custom-call(s32[16]{0:T(128)} %get-tuple-element.68.hi_ref, s32[16]{0:T(128)} %get-tuple-element.69.clean_ref, bf16[8,2,3,80,1024]{4,3,2,1,0:T(8,128)(2,1)} %bitcast.44.x_ref, bf16[8,80,1024]{2,1,0:T(8,128)(2,1)} %all-to-all-done.3.g_ref, ...), custom_call_target="tpu_custom_call" | custom-call | flops 42949672960 | bytes 16777216 | tf_op jit(solution)/shard_map/attend_back/pallas_call | solution.py:184
  409.3 4.5 all-to-all-start.4
  414.0 52.2 %attend_back.3 = (bf16[8,3,80,1024]{3,2,1,0:T(8,128)(2,1)}, f32[80,128]{1,0:T(8,128)}) custom-call(s32[16]{0:T(128)} %get-tuple-element.68.hi_ref, s32[16]{0:T(128)} %get-tuple-element.69.clean_ref, bf16[8,2,3,80,1024]{4,3,2,1,0:T(8,128)(2,1)} %bitcast.44.x_ref, bf16[8,80,1024]{2,1,0:T(8,128)(2,1)} %copy-done.15, f32[8,80,1024]{2,1,0:T(8,128)} %get-tuple-element.75.wide_ref, ...), custom_call_target="tpu_custom_call" | custom-call | flops 42949672960 | bytes 16777216 | tf_op jit(solution)/shard_map/attend_back/pallas_call | solution.py:184
  467.0 4.7 all-to-all-start.5
  471.8 21.9 %weight_grad.1 = (bf16[480,1280]{1,0:T(8,128)(2,1)}, f32[1,1280]{1,0:T(1,128)}) custom-call(s32[1]{0:T(128)} %bitcast.57.me_ref, bf16[1024,1280]{1,0:T(8,128)(2,1)} %fusion.4.refs_0_, bf16[1024,1280]{1,0:T(8,128)(2,1)} %collective-permute-done.5.refs_1_, bf16[1024,1280]{1,0:T(8,128)(2,1)} %collective-permute-done.3.refs_2_, ...), custom_call_target="tpu_custom_call" | custom-call | flops 10066329600 | bytes 20971520 | tf_op jit(solution)/shard_map/weight_grad/pallas_call | solution.py:255
  496.3 33.3 %collective-permute-start.13 = (bf16[2,320,480]{2,1,0:T(8,128)(2,1)}, bf16[2,320,480]{2,1,0:T(8,128)(2,1)}, u32[]{:S(2)}, u32[]{:S(2)}) collective-permute-start(bf16[2,320,480]{2,1,0:T(8,128)(2,1)} %bitcast.60), channel_id=1, source_target_pairs={{0,16},{8,24},{16,0},{24,8},{1,17},{9,25},{17,1},{25,9},{2,18},{10... | collective-permute-start | bytes 1843208 | tf_op jit(solution)/shard_map/ppermute | solution.py:595
  534.1 11.0 %fusion.19 = bf16[1024,1,1280]{2,0,1:T(8,128)(2,1)} fusion(f32[1024,1280]{1,0:T(8,128)} %copy-done, bf16[3,1280,1280]{2,1,0:T(8,128)(2,1)} %all-gather.5.cloned.1.call-done, f32[1280]{0:T(1024)S(1)} %copy-done.37, f32[1024,1280]{1,0:T(8,128)} %copy-done.39, f32[1280]{0:T(1024)S(1)} %copy-done.38), kind=kOutput, calls=%fused_computation.38 | convolution fusion | flops 3367239680 | bytes 16394240 | tf_op jit(solution)/shard_map/dot_general | solution.py:25
  545.5 12.8 %collective-permute-done.14 = f32[5200]{0:T(1024)S(1)} collective-permute-done((f32[5200]{0:T(1024)S(1)}, f32[5200]{0:T(1024)S(1)}, u32[]{:S(2)}, u32[]{:S(2)}) %collective-permute-start.14) | collective-permute-done | bytes 20832 | tf_op jit(solution)/shard_map/ppermute | solution.py:595
  563.7 10.4 %fusion.15 = f32[1024,1280]{1,0:T(8,128)} fusion(bf16[1920,1024]{1,0:T(8,128)(2,1)} %bitcast.55, bf16[1280,3840]{1,0:T(8,128)(2,1)} %all-gather.7.cloned.1.call-done), kind=kOutput, calls=%fused_computation.33 | convolution fusion | flops 5033164800 | bytes 14090240 | tf_op jit(solution)/shard_map/dot_general | solution.py:25
  576.8 11.7 %fusion.5 = (f32[1024]{0:T(1024)S(1)}, f32[1024,1280]{1,0:T(8,128)}) fusion(bf16[1024,1,1280]{2,0,1:T(8,128)(2,1)S(1)} %copy-done.2, f32[1024]{0:T(1024)S(1)} %copy-done.19, f32[1280]{0:T(1024)S(1)} %copy-done.27, f32[1024,1280]{1,0:T(8,128)} %fusion.15, bf16[1920,1024]{1,0:T(8,128)(2,1)} %bitcast.56, bf16[1280,3840]{1,0:T(8,128)(2,1)} %all-gather.7.cloned.1.call-done), kind=kOutput, calls=%fused_computation.13 | convolution fusion | flops 5041028096 | bytes 21967872 | tf_op jit(solution)/shard_map/dot_general | solution.py:25
  593.3 9.4 %fusion.22 = bf16[1024,1,1280]{2,0,1:T(8,128)(2,1)} fusion(f32[1024,1280]{1,0:T(8,128)} %get-tuple-element.144, bf16[1024,1,1280]{2,0,1:T(8,128)(2,1)S(1)} %copy-done.2, f32[1024]{0:T(1024)S(1)} %broadcast_multiply_fusion, f32[1024]{0:T(1024)S(1)} %copy-done.19, f32[1024]{0:T(1024)S(1)} %copy-done.23, f32[1024,1280]{1,0:T(8,128)} %copy-done, ...), kind=kLoop, calls=%fused_computation.43 | loop fusion | flops 18350080 | bytes 23614464 | tf_op jit(solution)/shard_map/broadcast_in_dim | solution.py:629
  (250 shorter events, 95.9 us)
Async XLA Ops:
  7.2 66.6 %all-gather.9.cloned.1.call-start = ((), (), s32[]{:S(2)}) async-start(), calls=%async_computation.10 | async-start | bytes 1638400 | tf_op jit(solution)/shard_map/all_gather | solution.py:389
  11.0 20.8 %collective-permute-start.2 = (bf16[80,480]{1,0:T(8,128)(2,1)}, bf16[80,480]{1,0:T(8,128)(2,1)}, u32[]{:S(2)}, u32[]{:S(2)}) collective-permute-start(bf16[80,480]{1,0:T(8,128)(2,1)} %bitcast.275), channel_id=1, source_target_pairs={{0,6},{2,4},{4,2},{6,0},{1,7},{3,5},{5,3},{7,1},{8,14},{10,12},{12... | collective-permute-start | bytes 230408 | tf_op jit(solution)/shard_map/ppermute | solution.py:380
  14.1 17.7 %collective-permute-start.1 = (bf16[80,480]{1,0:T(8,128)(2,1)}, bf16[80,480]{1,0:T(8,128)(2,1)}, u32[]{:S(2)}, u32[]{:S(2)}) collective-permute-start(bf16[80,480]{1,0:T(8,128)(2,1)} %bitcast.8), channel_id=1, source_target_pairs={{0,4},{2,6},{4,0},{6,2},{1,5},{3,7},{5,1},{7,3},{8,12},{10,14},{12... | collective-permute-start | bytes 230408 | tf_op jit(solution)/shard_map/ppermute | solution.py:380
  15.4 16.4 %collective-permute-start = (bf16[80,480]{1,0:T(8,128)(2,1)}, bf16[80,480]{1,0:T(8,128)(2,1)}, u32[]{:S(2)}, u32[]{:S(2)}) collective-permute-start(bf16[80,480]{1,0:T(8,128)(2,1)} %bitcast.6), channel_id=1, source_target_pairs={{0,2},{2,0},{4,6},{6,4},{1,3},{3,1},{5,7},{7,5},{8,10},{10,8},{12,... | collective-permute-start | bytes 230408 | tf_op jit(solution)/shard_map/ppermute | solution.py:380
  24.6 20.9 %collective-permute-start.6 = (bf16[80,3840]{1,0:T(8,128)(2,1)}, bf16[80,3840]{1,0:T(8,128)(2,1)}, u32[]{:S(2)}, u32[]{:S(2)}) collective-permute-start(bf16[80,3840]{1,0:T(8,128)(2,1)} %copy.138), channel_id=1, source_target_pairs={{0,1},{1,0},{2,3},{3,2},{4,5},{5,4},{6,7},{7,6},{8,9},{9,8},{10,11... | collective-permute-start | bytes 1843208 | tf_op jit(solution)/shard_map/ppermute | solution.py:353
  30.2 17.5 %copy-start.9 = (bf16[3,80,4,2,80]{1,4,0,2,3:T(8,128)(2,1)S(1)}, bf16[3,80,4,2,80]{1,4,0,2,3:T(8,128)(2,1)}, u32[]{:S(2)}) copy-start(bf16[3,80,4,2,80]{1,4,0,2,3:T(8,128)(2,1)} %copy.133) | copy-start | bytes 921604
  37.8 45.3 %collective-permute-start.5 = (bf16[1024,1280]{1,0:T(8,128)(2,1)}, bf16[1024,1280]{1,0:T(8,128)(2,1)}, u32[]{:S(2)}, u32[]{:S(2)}) collective-permute-start(bf16[1024,1280]{1,0:T(8,128)(2,1)} %fusion.4.refs_0_), channel_id=1, source_target_pairs={{0,2},{1,3},{2,0},{3,1},{4,6},{5,7},{6,4},{7,5},{8,10},{9,11},{10,... | collective-permute-start | bytes 7864328 | tf_op jit(solution)/shard_map/ppermute | solution.py:430
  40.4 216.9 %all-gather.5.cloned.1.call-start = ((), (), s32[]{:S(2)}) async-start(), calls=%async_computation.7 | async-start | bytes 10444800 | tf_op jit(solution)/shard_map/all_gather | solution.py:465
  43.0 59.6 %collective-permute-start.3 = (bf16[1024,1280]{1,0:T(8,128)(2,1)}, bf16[1024,1280]{1,0:T(8,128)(2,1)}, u32[]{:S(2)}, u32[]{:S(2)}) collective-permute-start(bf16[1024,1280]{1,0:T(8,128)(2,1)} %fusion.4.refs_0_), channel_id=1, source_target_pairs={{0,1},{1,0},{2,3},{3,2},{4,5},{5,4},{6,7},{7,6},{8,9},{9,8},{10,11... | collective-permute-start | bytes 7864328 | tf_op jit(solution)/shard_map/ppermute | solution.py:430
  43.4 59.3 %collective-permute-start.4 = (bf16[1024,1280]{1,0:T(8,128)(2,1)}, bf16[1024,1280]{1,0:T(8,128)(2,1)}, u32[]{:S(2)}, u32[]{:S(2)}) collective-permute-start(bf16[1024,1280]{1,0:T(8,128)(2,1)} %fusion.4.refs_0_), channel_id=1, source_target_pairs={{0,4},{1,5},{2,6},{3,7},{4,0},{5,1},{6,2},{7,3},{8,12},{9,13},{10,... | collective-permute-start | bytes 7864328 | tf_op jit(solution)/shard_map/ppermute | solution.py:430
  102.7 220.2 %all-gather.7.cloned.1.call-start = ((), (), s32[]{:S(2)}) async-start(), calls=%async_computation.8 | async-start | bytes 10444800 | tf_op jit(solution)/shard_map/all_gather | solution.py:467
  102.9 41.2 %collective-permute-start.7 = (bf16[1024,1280]{1,0:T(8,128)(2,1)}, bf16[1024,1280]{1,0:T(8,128)(2,1)}, u32[]{:S(2)}, u32[]{:S(2)}) collective-permute-start(bf16[1024,1280]{1,0:T(8,128)(2,1)} %collective-permute-done.3.refs_2_), channel_id=1, source_target_pairs={{0,2},{1,3},{2,0},{3,1},{4,6},{5,7},{6,4},{7,5},{8,10},{9,11},{10,... | collective-permute-start | bytes 7864328 | tf_op jit(solution)/shard_map/ppermute | solution.py:430
  103.0 50.3 %collective-permute-start.8 = (bf16[1024,1280]{1,0:T(8,128)(2,1)}, bf16[1024,1280]{1,0:T(8,128)(2,1)}, u32[]{:S(2)}, u32[]{:S(2)}) collective-permute-start(bf16[1024,1280]{1,0:T(8,128)(2,1)} %collective-permute-done.4.refs_4_), channel_id=1, source_target_pairs={{0,2},{1,3},{2,0},{3,1},{4,6},{5,7},{6,4},{7,5},{8,10},{9,11},{10,... | collective-permute-start | bytes 7864328 | tf_op jit(solution)/shard_map/ppermute | solution.py:430
  106.0 37.7 %collective-permute-start.9 = (bf16[512,1280]{1,0:T(8,128)(2,1)}, bf16[512,1280]{1,0:T(8,128)(2,1)}, u32[]{:S(2)}, u32[]{:S(2)}) collective-permute-start(bf16[512,1280]{1,0:T(8,128)(2,1)} %slice.148), channel_id=1, source_target_pairs={{0,4},{1,5},{2,6},{3,7},{4,0},{5,1},{6,2},{7,3},{8,12},{9,13},{10,... | collective-permute-start | bytes 3932168 | tf_op jit(solution)/shard_map/ppermute | solution.py:430
  110.2 33.5 %collective-permute-start.11 = (bf16[512,1280]{1,0:T(8,128)(2,1)}, bf16[512,1280]{1,0:T(8,128)(2,1)}, u32[]{:S(2)}, u32[]{:S(2)}) collective-permute-start(bf16[512,1280]{1,0:T(8,128)(2,1)} %slice.149), channel_id=1, source_target_pairs={{0,1},{1,0},{2,3},{3,2},{4,5},{5,4},{6,7},{7,6},{8,9},{9,8},{10,11... | collective-permute-start | bytes 3932168 | tf_op jit(solution)/shard_map/ppermute | solution.py:430
  112.3 31.8 %copy-start.14 = (bf16[16,80,480]{2,1,0:T(8,128)(2,1)S(1)}, bf16[16,80,480]{2,1,0:T(8,128)(2,1)}, u32[]{:S(2)}) copy-start(bf16[16,80,480]{2,1,0:T(8,128)(2,1)} %all-gather.9.cloned.1.call-done) | copy-start | bytes 3686404
  143.6 17.2 %collective-permute-start.10 = (bf16[512,1280]{1,0:T(8,128)(2,1)}, bf16[512,1280]{1,0:T(8,128)(2,1)S(1)}, u32[]{:S(2)}, u32[]{:S(2)}) collective-permute-start(bf16[512,1280]{1,0:T(8,128)(2,1)} %collective-permute-done.9.refs_6_), channel_id=1, source_target_pairs={{0,2},{1,3},{2,0},{3,1},{4,6},{5,7},{6,4},{7,5},{8,10},{9,11},{10,... | collective-permute-start | bytes 3932168 | tf_op jit(solution)/shard_map/ppermute | solution.py:430
  143.6 22.1 %collective-permute-start.12 = (bf16[512,1280]{1,0:T(8,128)(2,1)}, bf16[512,1280]{1,0:T(8,128)(2,1)S(1)}, u32[]{:S(2)}, u32[]{:S(2)}) collective-permute-start(bf16[512,1280]{1,0:T(8,128)(2,1)} %collective-permute-done.11.refs_8_), channel_id=1, source_target_pairs={{0,2},{1,3},{2,0},{3,1},{4,6},{5,7},{6,4},{7,5},{8,10},{9,11},{10,... | collective-permute-start | bytes 3932168 | tf_op jit(solution)/shard_map/ppermute | solution.py:430
  208.3 44.7 %all-to-all-start = ((bf16[8,80,1024]{2,1,0:T(8,128)(2,1)}), bf16[8,80,1024]{2,1,0:T(8,128)(2,1)}, u32[]{:S(2)}, u32[]{:S(2)}) async-start(bf16[8,80,1024]{2,1,0:T(8,128)(2,1)} %get-tuple-element.65), calls=%async_computation | async-start | bytes 2621440 | tf_op jit(solution)/shard_map/all_to_all | solution.py:489
  253.0 22.0 %all-to-all-start.1 = ((bf16[8,80,1024]{2,1,0:T(8,128)(2,1)}), bf16[8,80,1024]{2,1,0:T(8,128)(2,1)}, u32[]{:S(2)}, u32[]{:S(2)}) async-start(bf16[8,80,1024]{2,1,0:T(8,128)(2,1)} %get-tuple-element.67), calls=%async_computation.1 | async-start | bytes 2621440 | tf_op jit(solution)/shard_map/all_to_all | solution.py:489
  257.3 272.5 %reduce-scatter.2.cloned.1.call-start = ((), (), s32[]{:S(2)}) async-start(), calls=%async_computation.9 | async-start | bytes 10444800 | tf_op jit(solution)/shard_map/reduce_scatter | solution.py:536
  281.1 28.1 %copy-start = (f32[1024,1280]{1,0:T(8,128)}, f32[1024,1280]{1,0:T(8,128)S(1)}, u32[]{:S(2)}) copy-start(f32[1024,1280]{1,0:T(8,128)S(1)} %get-tuple-element.139) | copy-start | bytes 15728644
  281.1 28.1 %copy-start.20 = (f32[1024]{0:T(1024)}, f32[1024]{0:T(1024)S(1)}, u32[]{:S(2)}) copy-start(f32[1024]{0:T(1024)S(1)} %add_rsqrt_fusion) | copy-start | bytes 12292
  288.8 24.6 %copy-start.39 = (f32[1024,1280]{1,0:T(8,128)}, f32[1024,1280]{1,0:T(8,128)S(1)}, u32[]{:S(2)}) copy-start(f32[1024,1280]{1,0:T(8,128)S(1)} %fusion.21) | copy-start | bytes 15728644
  329.5 22.0 %all-to-all-start.3 = ((bf16[8,80,1024]{2,1,0:T(8,128)(2,1)}), bf16[8,80,1024]{2,1,0:T(8,128)(2,1)}, u32[]{:S(2)}, u32[]{:S(2)}) async-start(bf16[8,80,1024]{2,1,0:T(8,128)(2,1)} %bitcast.248), calls=%async_computation.3 | async-start | bytes 2621440 | tf_op jit(solution)/shard_map/all_to_all | solution.py:492
  333.8 21.3 %copy-start.33 = (f32[80]{0:T(128)S(1)}, f32[80]{0:T(128)}, u32[]{:S(2)}) copy-start(f32[80]{0:T(128)} %copy-done.32) | copy-start | bytes 964
  351.5 56.7 %all-to-all-start.2 = ((bf16[8,80,1024]{2,1,0:T(8,128)(2,1)}), bf16[8,80,1024]{2,1,0:T(8,128)(2,1)S(1)}, u32[]{:S(2)}, u32[]{:S(2)}) async-start(bf16[8,80,1024]{2,1,0:T(8,128)(2,1)} %bitcast.249), calls=%async_computation.2 | async-start | bytes 2621440 | tf_op jit(solution)/shard_map/all_to_all | solution.py:492
  409.3 57.7 %all-to-all-start.4 = ((bf16[8,3,80,1024]{3,2,1,0:T(8,128)(2,1)}), bf16[8,3,80,1024]{3,2,1,0:T(8,128)(2,1)}, u32[]{:S(2)}, u32[]{:S(2)}) async-start(bf16[8,3,80,1024]{3,2,1,0:T(8,128)(2,1)} %get-tuple-element.80.refs_11_), calls=%async_computation.4 | async-start | bytes 7864320 | tf_op jit(solution)/shard_map/all_to_all | solution.py:489
  467.0 107.3 %all-to-all-start.5 = ((bf16[8,3,80,1024]{3,2,1,0:T(8,128)(2,1)}), bf16[8,3,80,1024]{3,2,1,0:T(8,128)(2,1)}, u32[]{:S(2)}, u32[]{:S(2)}) async-start(bf16[8,3,80,1024]{3,2,1,0:T(8,128)(2,1)} %get-tuple-element.78.refs_12_), calls=%async_computation.5 | async-start | bytes 7864320 | tf_op jit(solution)/shard_map/all_to_all | solution.py:489
  493.7 35.9 %copy-start.30 = (f32[1,1280]{1,0:T(1,128)S(1)}, f32[1,1280]{1,0:T(1,128)}, u32[]{:S(2)}) copy-start(f32[1,1280]{1,0:T(1,128)} %get-tuple-element.82) | copy-start | bytes 15364
  493.7 35.9 %copy-start.27 = (f32[1280]{0:T(1024)S(1)}, f32[1280]{0:T(1024)}, u32[]{:S(2)}) copy-start(f32[1280]{0:T(1024)} %param.14) | copy-start | bytes 15364
  493.7 35.9 %copy-start.29 = (f32[1280]{0:T(1024)S(1)}, f32[1280]{0:T(1024)}, u32[]{:S(2)}) copy-start(f32[1280]{0:T(1024)} %get-tuple-element.103) | copy-start | bytes 15364
  493.7 35.9 %copy-start.28 = (f32[1280]{0:T(1024)S(1)}, f32[1280]{0:T(1024)}, u32[]{:S(2)}) copy-start(f32[1280]{0:T(1024)} %get-tuple-element.141) | copy-start | bytes 15364
  493.8 35.9 %copy-start.34 = (f32[80]{0:T(128)S(1)}, f32[80]{0:T(128)}, u32[]{:S(2)}) copy-start(f32[80]{0:T(128)} %param.15) | copy-start | bytes 964
  496.3 37.9 %copy-start.37 = (f32[1280]{0:T(1024)S(1)}, f32[1280]{0:T(1024)}, u32[]{:S(2)}) copy-start(f32[1280]{0:T(1024)} %param.22) | copy-start | bytes 15364
  496.3 62.0 %collective-permute-start.13 = (bf16[2,320,480]{2,1,0:T(8,128)(2,1)}, bf16[2,320,480]{2,1,0:T(8,128)(2,1)}, u32[]{:S(2)}, u32[]{:S(2)}) collective-permute-start(bf16[2,320,480]{2,1,0:T(8,128)(2,1)} %bitcast.60), channel_id=1, source_target_pairs={{0,16},{8,24},{16,0},{24,8},{1,17},{9,25},{17,1},{25,9},{2,18},{10... | collective-permute-start | bytes 1843208 | tf_op jit(solution)/shard_map/ppermute | solution.py:595
  529.7 28.6 %collective-permute-start.14 = (f32[5200]{0:T(1024)S(1)}, f32[5200]{0:T(1024)S(1)}, u32[]{:S(2)}, u32[]{:S(2)}) collective-permute-start(f32[5200]{0:T(1024)S(1)} %constant_dynamic-update-slice_fusion), channel_id=1, source_target_pairs={{0,16},{8,24},{16,0},{24,8},{1,17},{9,25},{17,1},{25,9},{2,18},{10... | collective-permute-start | bytes 62408 | tf_op jit(solution)/shard_map/ppermute | solution.py:595
  532.2 27.5 %collective-permute-start.15 = (bf16[3,80,640]{2,1,0:T(8,128)(2,1)S(1)}, bf16[3,80,640]{2,1,0:T(8,128)(2,1)}, u32[]{:S(2)}, u32[]{:S(2)}) collective-permute-start(bf16[3,80,640]{2,1,0:T(8,128)(2,1)S(1)} %select_bitcast_fusion.2), channel_id=1, source_target_pairs={{0,1},{1,0},{2,3},{3,2},{4,5},{5,4},{6,7},{7,6},{8,9},{9,8},{10,11... | collective-permute-start | bytes 921608 | tf_op jit(solution)/shard_map/ppermute | solution.py:362
  561.6 12.5 %collective-permute-start.16 = (bf16[1,320,480]{2,1,0:T(8,128)(2,1)S(1)}, bf16[1,320,480]{2,1,0:T(8,128)(2,1)S(1)}, u32[]{:S(2)}, u32[]{:S(2)}) collective-permute-start(bf16[1,320,480]{2,1,0:T(8,128)(2,1)S(1)} %broadcast_select_fusion.1), channel_id=1, source_target_pairs={{0,8},{8,0},{16,24},{24,16},{1,9},{9,1},{17,25},{25,17},{2,10},{10... | collective-permute-start | bytes 921608 | tf_op jit(solution)/shard_map/ppermute | solution.py:595
  561.7 12.4 %collective-permute-start.17 = (f32[5200]{0:T(1024)S(1)}, f32[5200]{0:T(1024)S(1)}, u32[]{:S(2)}, u32[]{:S(2)}) collective-permute-start(f32[5200]{0:T(1024)S(1)} %add.177), channel_id=1, source_target_pairs={{0,8},{8,0},{16,24},{24,16},{1,9},{9,1},{17,25},{25,17},{2,10},{10... | collective-permute-start | bytes 62408 | tf_op jit(solution)/shard_map/ppermute | solution.py:595
  574.3 16.7 %collective-permute-start.23 = (f32[5200]{0:T(1024)S(1)}, f32[5200]{0:T(1024)S(1)}, u32[]{:S(2)}, u32[]{:S(2)}) collective-permute-start(f32[5200]{0:T(1024)S(1)} %add.180), channel_id=1, source_target_pairs={{0,6},{2,4},{4,2},{6,0},{1,7},{3,5},{5,3},{7,1},{8,14},{10,12},{12... | collective-permute-start | bytes 62408 | tf_op jit(solution)/shard_map/ppermute | solution.py:595
  575.1 16.0 %collective-permute-start.22 = (f32[5200]{0:T(1024)S(1)}, f32[5200]{0:T(1024)S(1)}, u32[]{:S(2)}, u32[]{:S(2)}) collective-permute-start(f32[5200]{0:T(1024)S(1)} %add.180), channel_id=1, source_target_pairs={{0,4},{2,6},{4,0},{6,2},{1,5},{3,7},{5,1},{7,3},{8,12},{10,14},{12... | collective-permute-start | bytes 62408 | tf_op jit(solution)/shard_map/ppermute | solution.py:595
  576.1 15.0 %collective-permute-start.21 = (f32[5200]{0:T(1024)S(1)}, f32[5200]{0:T(1024)}, u32[]{:S(2)}, u32[]{:S(2)}) collective-permute-start(f32[5200]{0:T(1024)S(1)} %add.180), channel_id=1, source_target_pairs={{0,2},{2,0},{4,6},{6,4},{1,3},{3,1},{5,7},{7,5},{8,10},{10,8},{12,... | collective-permute-start | bytes 62408 | tf_op jit(solution)/shard_map/ppermute | solution.py:595
  576.8 16.5 %copy-start.21 = (f32[1024]{0:T(1024)S(1)}, f32[1024]{0:T(1024)}, u32[]{:S(2)}) copy-start(f32[1024]{0:T(1024)} %copy-done.20) | copy-start | bytes 12292
  588.6 15.4 %collective-permute-start.20 = (bf16[80,480]{1,0:T(8,128)(2,1)S(1)}, bf16[80,480]{1,0:T(8,128)(2,1)S(1)}, u32[]{:S(2)}, u32[]{:S(2)}) collective-permute-start(bf16[80,480]{1,0:T(8,128)(2,1)S(1)} %bitcast.271), channel_id=1, source_target_pairs={{0,6},{2,4},{4,2},{6,0},{1,7},{3,5},{5,3},{7,1},{8,14},{10,12},{12... | collective-permute-start | bytes 230408 | tf_op jit(solution)/shard_map/ppermute | solution.py:380
  590.1 13.9 %collective-permute-start.19 = (bf16[80,480]{1,0:T(8,128)(2,1)S(1)}, bf16[80,480]{1,0:T(8,128)(2,1)S(1)}, u32[]{:S(2)}, u32[]{:S(2)}) collective-permute-start(bf16[80,480]{1,0:T(8,128)(2,1)S(1)} %bitcast.272), channel_id=1, source_target_pairs={{0,4},{2,6},{4,0},{6,2},{1,5},{3,7},{5,1},{7,3},{8,12},{10,14},{12... | collective-permute-start | bytes 230408 | tf_op jit(solution)/shard_map/ppermute | solution.py:380
  591.0 13.0 %collective-permute-start.18 = (bf16[80,480]{1,0:T(8,128)(2,1)S(1)}, bf16[80,480]{1,0:T(8,128)(2,1)S(1)}, u32[]{:S(2)}, u32[]{:S(2)}) collective-permute-start(bf16[80,480]{1,0:T(8,128)(2,1)S(1)} %bitcast.273), channel_id=1, source_target_pairs={{0,2},{2,0},{4,6},{6,4},{1,3},{3,1},{5,7},{7,5},{8,10},{10,8},{12,... | collective-permute-start | bytes 230408 | tf_op jit(solution)/shard_map/ppermute | solution.py:380
  591.9 10.9 %collective-permute-start.24 = (f32[5200]{0:T(1024)S(1)}, f32[5200]{0:T(1024)S(1)}, u32[]{:S(2)}, u32[]{:S(2)}) collective-permute-start(f32[5200]{0:T(1024)S(1)} %add_add_fusion), channel_id=1, source_target_pairs={{0,1},{1,0},{2,3},{3,2},{4,5},{5,4},{6,7},{7,6},{8,9},{9,8},{10,11... | collective-permute-start | bytes 62408 | tf_op jit(solution)/shard_map/ppermute | solution.py:595
  (30 other events, 183.3 us)
Sparse Core Ops, SparseCore 0:
  40.6 33.1 all-gather.8
  102.8 88.6 all-gather.4
  193.8 86.7 all-gather.6
  323.0 175.1 reduce-scatter.1

commit v2 on v1

v2 whole, which is shorter than its diff:
```python
import functools
import math

import jax
import jax.numpy as jnp
from jax import lax
from jax.experimental import pallas as pl
from jax.experimental.layout import Layout, with_layout_constraint
from jax.experimental.pallas import tpu as pltpu
from jax.sharding import PartitionSpec as P

HD = 80
IDS = 32
BLOCK_Q = 512
BLOCK_K = 512
PARTS = 2
WIDE = HD + IDS
EPSILON = 1e-06
LOG_TWO_E = 1.442695041
LOG2E = 1.4426950408889634
NEGATIVE = -1e30
VMEM_BYTES = 60 << 20
bf16, f32 = jnp.bfloat16, jnp.float32


def dot(a, b, contract_a, contract_b):
    return lax.dot_general(
        a, b, ((contract_a, contract_b), ((), ())), preferred_element_type=f32
    )


def nn(a, b):
    return dot(a, b, (1,), (0,))


def nt(a, b):
    return dot(a, b, (1,), (1,))


def place(block, per, size):
    return block // per, pl.multiple_of((block % per) * size, size)


def run_tiles(length, count, tiles, prepare, process):
    n_q, n_k = length // BLOCK_Q, length // BLOCK_K

    def diagonal(t):
        t = jnp.minimum(t, n_q - 1)
        return t * n_k + t * BLOCK_Q // BLOCK_K

    def turns(number, tile, masked):
        prepare(tile(0), 0)

        def turn(t, _):
            prepare(tile(2 * t + 1), 1)
            process(tile(2 * t), 0, masked)
            prepare(tile(2 * t + 2), 0)
            process(tile(2 * t + 1), 1, masked)
            return 0

        lax.fori_loop(0, number, turn, 0)

    turns(n_q // 2, diagonal, True)
    turns(count[0] // 2, lambda t: tiles[t], False)


def attend_body(count, tiles, x_ref, segment_ref, o_ref, wide_ref, lse_ref, key_rows, query_cols, acc, top, total, scores, *, chunks, chunk):
    nk = chunks * chunk // BLOCK_K
    per_q, per_k = chunk // BLOCK_Q, chunk // BLOCK_K
    lanes = BLOCK_Q // PARTS
    for c in range(chunks):
        hot = lax.broadcasted_iota(jnp.int32, (IDS, chunk), 0) == segment_ref[0, c : c + 1, :]
        keys = jnp.concatenate([x_ref[c, 0, 1], jnp.where(hot, 1.0, 0.0).astype(bf16)], axis=0)
        key_rows[pl.ds(c * chunk, chunk), :] = keys.T
        query_cols[c] = jnp.concatenate([x_ref[c, 0, 0], jnp.where(hot, 0.0, NEGATIVE).astype(bf16)], axis=0)
        acc[c] = jnp.zeros((HD, chunk), f32)
    top[...] = jnp.full(top.shape, NEGATIVE, f32)
    total[...] = jnp.zeros(total.shape, f32)
    key_iota = lax.broadcasted_iota(jnp.int32, (BLOCK_K, lanes), 0)
    query_iota = lax.broadcasted_iota(jnp.int32, (BLOCK_K, lanes), 1)

    def prepare(tile, slot):
        c, off = place(tile // nk, per_q, BLOCK_Q)
        k = key_rows[pl.ds(pl.multiple_of((tile % nk) * BLOCK_K, BLOCK_K), BLOCK_K), :]
        for u in range(PARTS):
            scores[slot, :, u * lanes : (u + 1) * lanes] = nn(k, query_cols[c, :, pl.ds(off + u * lanes, lanes)]) * LOG2E

    def process(tile, slot, masked):
        i, j = tile // nk, tile % nk
        c, off = place(i, per_q, BLOCK_Q)
        ck_, koff = place(j, per_k, BLOCK_K)
        v = x_ref[ck_, 0, 2, :, pl.ds(koff, BLOCK_K)]
        for u in range(PARTS):
            at = pl.ds(off + u * lanes, lanes)
            row = pl.ds(c, 1)
            s = scores[slot, :, u * lanes : (u + 1) * lanes]
            if masked:
                s = jnp.where(key_iota - query_iota <= i * BLOCK_Q + u * lanes - j * BLOCK_K, s, NEGATIVE)
            old = top[row, at]
            new = jnp.maximum(old, jnp.max(s, axis=0, keepdims=True))
            p = jnp.exp2(s - new)
            shrink = jnp.exp2(old - new)
            top[row, at] = new
            total[row, at] = total[row, at] * shrink + jnp.sum(p, axis=0, keepdims=True)
            acc[c, :, at] = acc[c, :, at] * shrink + nn(v, p.astype(bf16))

    run_tiles(chunks * chunk, count, tiles, prepare, process)
    for c in range(chunks):
        t = total[c : c + 1, :]
        o = acc[c] / t
        wide_ref[c] = o
        o_ref[c] = o.astype(bf16)
        lse_ref[0, c : c + 1, :] = top[c : c + 1, :] + jnp.log2(t)


def attend_back_body(count, tiles, x_ref, g_ref, wide_ref, lse_ref, segment_ref, scale_ref, dx_ref, part_ref, key_rows, query_cols, value_rows, dq, dk, dv, delta, scores, grads, *, chunks, chunk):
    nk = chunks * chunk // BLOCK_K
    per_q, per_k = chunk // BLOCK_Q, chunk // BLOCK_K
    lanes = BLOCK_Q // PARTS
    for c in range(chunks):
        hot = lax.broadcasted_iota(jnp.int32, (IDS, chunk), 0) == segment_ref[0, c : c + 1, :]
        keys = jnp.concatenate([x_ref[c, 0, 1], jnp.where(hot, 1.0, 0.0).astype(bf16)], axis=0)
        key_rows[pl.ds(c * chunk, chunk), :] = keys.T
        query_cols[c] = jnp.concatenate([x_ref[c, 0, 0], jnp.where(hot, 0.0, NEGATIVE).astype(bf16)], axis=0)
        value_rows[pl.ds(c * chunk, chunk), :] = x_ref[c, 0, 2].T
        delta[c : c + 1, :] = jnp.sum(g_ref[c].astype(f32) * wide_ref[c], axis=0, keepdims=True)
        for ref in (dq, dk, dv):
            ref[c] = jnp.zeros((HD, chunk), f32)
    key_iota = lax.broadcasted_iota(jnp.int32, (BLOCK_K, lanes), 0)
    query_iota = lax.broadcasted_iota(jnp.int32, (BLOCK_K, lanes), 1)

    def prepare(tile, slot):
        c, off = place(tile // nk, per_q, BLOCK_Q)
        rows = pl.ds(pl.multiple_of((tile % nk) * BLOCK_K, BLOCK_K), BLOCK_K)
        k, v = key_rows[rows, :], value_rows[rows, :]
        for u in range(PARTS):
            at = pl.ds(off + u * lanes, lanes)
            scores[slot, :, u * lanes : (u + 1) * lanes] = nn(k, query_cols[c, :, at])
            grads[slot, :, u * lanes : (u + 1) * lanes] = nn(v, g_ref[c, :, at])

    def process(tile, slot, masked):
        i, j = tile // nk, tile % nk
        c, off = place(i, per_q, BLOCK_Q)
        kc, koff = place(j, per_k, BLOCK_K)
        kat = pl.ds(koff, BLOCK_K)
        kt = x_ref[kc, 0, 1, :, kat]
        for u in range(PARTS):
            at = pl.ds(off + u * lanes, lanes)
            row = pl.ds(c, 1)
            s = scores[slot, :, u * lanes : (u + 1) * lanes] * LOG2E
            if masked:
                s = jnp.where(key_iota - query_iota <= i * BLOCK_Q + u * lanes - j * BLOCK_K, s, NEGATIVE)
            p = jnp.exp2(s - lse_ref[0, row, at])
            low = (p * (grads[slot, :, u * lanes : (u + 1) * lanes] - delta[row, at])).astype(bf16)
            q, g = x_ref[c, 0, 0, :, at], g_ref[c, :, at]
            dv[kc, :, kat] += nt(g, p.astype(bf16))
            dk[kc, :, kat] += nt(q, low)
            dq[c, :, at] += nn(kt, low)

    run_tiles(chunks * chunk, count, tiles, prepare, process)
    part = jnp.zeros((HD, 128), f32)
    for c in range(chunks):
        grad = dq[c]
        dx_ref[c, 0] = (grad * scale_ref[:, 0:1]).astype(bf16)
        dx_ref[c, 1] = dk[c].astype(bf16)
        dx_ref[c, 2] = dv[c].astype(bf16)
        term = grad * x_ref[c, 0, 0].astype(f32)
        for u in range(chunk // 128):
            part = part + term[:, u * 128 : (u + 1) * 128]
    part_ref[...] = part


def kernel_cost(length, matmuls):
    pairs = length * 2048
    return pl.CostEstimate(
        flops=matmuls * 512 * pairs, bytes_accessed=length * 2048, transcendentals=pairs
    )


def attend(tables, x, segments, p):
    chunks, _, _, _, chunk = x.shape
    flat = lambda g, *_: (0, 0, 0)
    return pl.pallas_call(
        functools.partial(attend_body, chunks=chunks, chunk=chunk),
        grid_spec=pltpu.PrefetchScalarGridSpec(
            num_scalar_prefetch=2,
            grid=(1,),
            in_specs=[
                pl.BlockSpec((chunks, 1, 3, HD, chunk), lambda g, *_: (0, p, 0, 0, 0)),
                pl.BlockSpec((1, chunks, chunk), flat),
            ],
            out_specs=[
                pl.BlockSpec((chunks, HD, chunk), flat),
                pl.BlockSpec((chunks, HD, chunk), flat),
                pl.BlockSpec((1, chunks, chunk), flat),
            ],
            scratch_shapes=[
                pltpu.VMEM((chunks * chunk, WIDE), bf16),
                pltpu.VMEM((chunks, WIDE, chunk), bf16),
                pltpu.VMEM((chunks, HD, chunk), f32),
                pltpu.VMEM((chunks, chunk), f32),
                pltpu.VMEM((chunks, chunk), f32),
                pltpu.VMEM((2, BLOCK_K, BLOCK_Q), f32),
            ],
        ),
        out_shape=[
            jax.ShapeDtypeStruct((chunks, HD, chunk), bf16),
            jax.ShapeDtypeStruct((chunks, HD, chunk), f32),
            jax.ShapeDtypeStruct((1, chunks, chunk), f32),
        ],
        compiler_params=pltpu.CompilerParams(vmem_limit_bytes=VMEM_BYTES),
        cost_estimate=kernel_cost(chunks * chunk, 2),
        name="attend",
    )(*tables, x, segments)


def attend_back(tables, x, grad, wide, lse, segments, scale, p):
    chunks, _, _, _, chunk = x.shape
    flat = lambda g, *_: (0, 0, 0)
    return pl.pallas_call(
        functools.partial(attend_back_body, chunks=chunks, chunk=chunk),
        grid_spec=pltpu.PrefetchScalarGridSpec(
            num_scalar_prefetch=2,
            grid=(1,),
            in_specs=[
                pl.BlockSpec((chunks, 1, 3, HD, chunk), lambda g, *_: (0, p, 0, 0, 0)),
                pl.BlockSpec((chunks, HD, chunk), flat),
                pl.BlockSpec((chunks, HD, chunk), flat),
                pl.BlockSpec((1, chunks, chunk), flat),
                pl.BlockSpec((1, chunks, chunk), flat),
                pl.BlockSpec((HD, 128), lambda g, *_: (0, 0)),
            ],
            out_specs=[
                pl.BlockSpec((chunks, 3, HD, chunk), lambda g, *_: (0, 0, 0, 0)),
                pl.BlockSpec((HD, 128), lambda g, *_: (0, 0)),
            ],
            scratch_shapes=[
                pltpu.VMEM((chunks * chunk, WIDE), bf16),
                pltpu.VMEM((chunks, WIDE, chunk), bf16),
                pltpu.VMEM((chunks * chunk, HD), bf16),
                pltpu.VMEM((chunks, HD, chunk), f32),
                pltpu.VMEM((chunks, HD, chunk), f32),
                pltpu.VMEM((chunks, HD, chunk), f32),
                pltpu.VMEM((chunks, chunk), f32),
                pltpu.VMEM((2, BLOCK_K, BLOCK_Q), f32),
                pltpu.VMEM((2, BLOCK_K, BLOCK_Q), f32),
            ],
        ),
        out_shape=[
            jax.ShapeDtypeStruct((chunks, 3, HD, chunk), bf16),
            jax.ShapeDtypeStruct((HD, 128), f32),
        ],
        compiler_params=pltpu.CompilerParams(vmem_limit_bytes=VMEM_BYTES),
        cost_estimate=kernel_cost(chunks * chunk, 5),
        name="attend_back",
    )(*tables, x, grad, wide, lse, segments, scale)


def project_body(slots_ref, w_ref, scale_ref, *refs, places):
    n = len(places)
    pieces, (out_ref, done_ref, buffers, results, in_sems, out_sems) = refs[:n], refs[-6:]
    done_ref[...] = jnp.zeros(done_ref.shape, f32)

    def fetch(i):
        return pltpu.make_async_copy(pieces[i], buffers.at[i], in_sems.at[i])

    def store(i):
        first, rows = places[i], results.shape[2]
        return pltpu.make_async_copy(
            results.at[i], out_ref.at[slots_ref[i], :, pl.ds(first, rows)], out_sems.at[i]
        )

    for i in range(n):
        fetch(i).start()
    for i in range(n):
        fetch(i).wait()
        results[i] = (nt(w_ref[...], buffers[i]) * scale_ref[...]).astype(bf16)
        store(i).start()
    for i in range(n):
        store(i).wait()


def project_into(heads, after, shape, slots, places, w, scale, pieces):
    features, width = w.shape
    n, rows = len(pieces), pieces[0].shape[0]
    kept = [] if heads is None else [heads]
    tail = [] if after is None else [after]
    whole = pl.BlockSpec(memory_space=pltpu.VMEM)
    anywhere = pl.BlockSpec(memory_space=pl.ANY)
    return pl.pallas_call(
        functools.partial(project_body, places=places),
        in_specs=[pl.BlockSpec(memory_space=pltpu.SMEM), whole, whole] + [anywhere] * (n + len(kept) + len(tail)),
        out_specs=[anywhere, whole],
        out_shape=[jax.ShapeDtypeStruct(shape, bf16), jax.ShapeDtypeStruct((8, 128), f32)],
        scratch_shapes=[
            pltpu.VMEM((n, rows, width), bf16),
            pltpu.VMEM((n, features, rows), bf16),
            pltpu.SemaphoreType.DMA((n,)),
            pltpu.SemaphoreType.DMA((n,)),
        ],
        input_output_aliases={3 + n: 0} if kept else {},
        compiler_params=pltpu.CompilerParams(vmem_limit_bytes=VMEM_BYTES),
        cost_estimate=pl.CostEstimate(
            flops=2 * n * features * width * rows, bytes_accessed=4 * n * width * rows, transcendentals=0
        ),
        name="project",
    )(slots, w, scale, *pieces, *kept, *tail)


def weight_grad_body(me_ref, *refs, spots):
    n = len(spots)
    pieces, (w_ref, dx, out_ref, gain_ref, buffers, acc, sems) = refs[:n], refs[n:]
    rows, width = buffers.shape[1:]

    def copy(i):
        return pltpu.make_async_copy(pieces[i], buffers.at[i], sems.at[i])

    for i in range(n):
        copy(i).start()
    for i, (distance, first) in enumerate(spots):
        part_dx = dx[me_ref[0] ^ distance, :, :, first : first + rows]
        part_dx = part_dx.reshape(part_dx.shape[0] * part_dx.shape[1], rows)
        copy(i).wait()
        for lane in range(0, width, 256):
            part = nn(part_dx, buffers[i, :, lane : lane + 256])
            acc[:, lane : lane + 256] = part + acc[:, lane : lane + 256] if i else part
    total = acc[...]
    out_ref[...] = total.astype(bf16)
    gain_ref[...] = jnp.sum(total * w_ref[...].astype(f32), axis=0, keepdims=True)


def weight_grad(me, pieces, spots, w, dx):
    features, width = w.shape
    whole = pl.BlockSpec(memory_space=pltpu.VMEM)
    return pl.pallas_call(
        functools.partial(weight_grad_body, spots=spots),
        in_specs=[pl.BlockSpec(memory_space=pltpu.SMEM)]
        + [pl.BlockSpec(memory_space=pl.ANY)] * len(pieces)
        + [whole] * 2,
        out_specs=[whole, whole],
        out_shape=[
            jax.ShapeDtypeStruct((features, width), bf16),
            jax.ShapeDtypeStruct((1, width), f32),
        ],
        scratch_shapes=[
            pltpu.VMEM((len(pieces),) + pieces[0].shape, bf16),
            pltpu.VMEM((features, width), f32),
            pltpu.SemaphoreType.DMA((len(pieces),)),
        ],
        compiler_params=pltpu.CompilerParams(vmem_limit_bytes=VMEM_BYTES),
        cost_estimate=pl.CostEstimate(flops=1, bytes_accessed=1, transcendentals=0),
        name="weight_grad",
    )(me, *pieces, w, dx)


def back_one_body(back_ref, w_ref, out_ref):
    out_ref[...] = nn(w_ref[...], back_ref[...]).T


def finish_body(back_ref, w_ref, other_ref, tokens_ref, gain_ref, hidden_ref, out_ref):
    grad_normed = other_ref[...] + nn(w_ref[...], back_ref[...]).T
    inputs = tokens_ref[...].astype(f32)
    inverse = inverse_rms(inputs)
    out_ref[...] = (
        hidden_ref[...] + norm_back(grad_normed, inputs * inverse, inverse, gain_ref[...])
    ).astype(bf16)


def input_grad(back, w, p, others):
    features, rows = back.shape
    width = w.shape[0]
    block = math.gcd(rows, 256)
    by_tokens = pl.BlockSpec((block, width), lambda t: (t, 0))
    specs = [by_tokens, by_tokens, pl.BlockSpec((1, width), lambda t: (0, 0)), by_tokens] if others else []
    return pl.pallas_call(
        finish_body if others else back_one_body,
        grid=(rows // block,),
        in_specs=[
            pl.BlockSpec((features, block), lambda t: (0, t)),
            pl.BlockSpec((width, features), lambda t: (0, p)),
        ]
        + specs,
        out_specs=by_tokens,
        out_shape=jax.ShapeDtypeStruct((rows, width), bf16 if others else f32),
        compiler_params=pltpu.CompilerParams(vmem_limit_bytes=VMEM_BYTES),
        cost_estimate=pl.CostEstimate(
            flops=2 * features * width * rows if others else 1,
            bytes_accessed=16 * width * rows if others else 1,
            transcendentals=0,
        ),
        name="input_grad",
    )(back, w, *others)


def tile_list(segments):
    length = segments.shape[0]
    n_q, n_k = length // BLOCK_Q, length // BLOCK_K
    first = jnp.sum(segments[None, :] < segments[::BLOCK_Q][:, None], axis=1, dtype=jnp.int32)[:, None]
    q_block = jnp.arange(n_q, dtype=jnp.int32)[:, None]
    k_last = jnp.arange(n_k, dtype=jnp.int32)[None, :] * BLOCK_K + BLOCK_K - 1
    below = ((k_last < q_block * BLOCK_Q) & (k_last >= first)).reshape(-1)
    pair = jnp.arange(n_q * n_k, dtype=jnp.int32)
    rank = jnp.sum(jnp.where((pair[None, :] <= pair[:, None]) & below[None, :], 1, 0), axis=1) - 1
    count = rank[-1] + 1
    spot = jnp.arange(n_q * n_k + 2, dtype=jnp.int32)
    chosen = jnp.where(below, rank, -1)[None, :] == spot[:, None]
    tiles = jnp.sum(jnp.where(chosen, pair[None, :], 0), axis=1)
    tiles = jnp.where(spot == count, n_k - 1, tiles)
    return (count + count % 2).reshape(1), tiles


def in_rows(grad):
    return with_layout_constraint(grad.astype(bf16), Layout((0, 1)))


def inverse_rms(values):
    return lax.rsqrt(jnp.mean(values * values, axis=-1, keepdims=True) + EPSILON)


def norm_back(grad_norm, unit, inverse, gain):
    grad_unit = grad_norm * gain
    return inverse * (grad_unit - unit * jnp.mean(grad_unit * unit, axis=-1, keepdims=True))


def per_device(
    tokens,
    segments,
    gain_attn,
    query_scale,
    w_qkv,
    w_out,
    gain_mlp,
    w_up,
    b_up,
    w_down,
    b_down,
    cotangent,
):
    n_dp, n_ctx, n_tensor = (lax.axis_size(a) for a in ("dp", "ctx", "tensor"))
    ctx_rank, tensor_rank = lax.axis_index("ctx"), lax.axis_index("tensor")
    rows, sequences, width = tokens.shape
    shard, columns = w_qkv.shape[1:]
    local_heads = columns // HD
    group = n_ctx * n_tensor
    length = rows * group
    data = ("dp", "ctx")
    everyone = ("dp", "ctx", "tensor")
    split = local_heads % n_ctx == 0
    ctx_parts = n_ctx if split else 1
    own = local_heads // ctx_parts
    owners = ("ctx", "tensor") if split else ("tensor",)
    n_owners = ctx_parts * n_tensor
    head_width = own * 3 * HD

    inputs = tokens[:, 0].astype(f32)
    inverse_one = inverse_rms(inputs)
    unit_one = inputs * inverse_one
    normed_one = (unit_one * gain_attn).astype(bf16)

    def other_side(x):
        if n_tensor != 2:
            return lax.all_gather(x, "tensor", axis=0)
        return lax.ppermute(x, "tensor", [(0, 1), (1, 0)])

    def in_order(x, other):
        if n_tensor != 2:
            return other
        first = tensor_rank == 0
        return jnp.stack([jnp.where(first, x, other), jnp.where(first, other, x)])

    def scatter_pair(x):
        if n_tensor != 2:
            return lax.psum_scatter(x, "tensor", scatter_dimension=0, tiled=False).astype(f32)
        keep = jnp.where(tensor_rank == 0, x[0], x[1])
        send = jnp.where(tensor_rank == 0, x[1], x[0])
        return keep.astype(f32) + lax.ppermute(send, "tensor", [(0, 1), (1, 0)]).astype(f32)

    def by_distance(x, rank):
        count = x.shape[0]
        bit = 1
        while bit < count:
            y = x.reshape((count // (2 * bit), 2, bit) + x.shape[1:])
            y = jnp.where((rank & bit) > 0, jnp.flip(y, 1), y)
            x = y.reshape(x.shape)
            bit *= 2
        return x

    def exchange(x, axis, rank):
        count = x.shape[0]
        x = by_distance(x, rank)
        got = [x[0]] + [
            lax.ppermute(x[k], axis, [(i, i ^ k) for i in range(count)]) for k in range(1, count)
        ]
        return by_distance(jnp.stack(got), rank)

    qkv_rows = w_qkv.reshape(3, shard, ctx_parts, own, HD)
    for_owner = qkv_rows.transpose(2, 1, 3, 0, 4).reshape(ctx_parts, shard, head_width)
    if split:
        for_owner = exchange(for_owner, "ctx", ctx_rank)
    others = [other_side(w) for w in (w_qkv, w_out, w_up, w_down)]
    halves = [normed_one[: rows // 2], normed_one[rows // 2 :]]
    halves, for_owner, others = lax.optimization_barrier((halves, for_owner, others))
    pairs = [in_order(w, other) for w, other in zip((w_qkv, w_out, w_up, w_down), others, strict=True)]
    if split:
        owner_w = lax.all_gather(for_owner, "dp", axis=0).reshape(width, head_width)
    else:
        owner_w = lax.all_gather(for_owner[0], data, axis=0).reshape(width, head_width)

    tiles = tile_list(segments[0])
    qkv_cols = pairs[0].reshape(n_tensor, 3, shard, ctx_parts, own, HD).transpose(0, 2, 4, 3, 1, 5)
    out_cols = pairs[1].reshape(n_tensor, ctx_parts, own, HD, shard).transpose(0, 4, 2, 1, 3)

    def interleave(x, inner):
        x = x.reshape(n_tensor, shard, own * ctx_parts, inner)
        return x.transpose(1, 2, 0, 3).reshape(shard, -1)

    def side_by_side(x):
        return x.transpose(1, 0, 2).reshape(shard, -1)

    full_rows = jnp.stack(
        [
            interleave(out_cols, HD),
            side_by_side(pairs[2]),
            side_by_side(jnp.swapaxes(pairs[3], 1, 2)),
        ]
    )
    qkv_rows_full = interleave(qkv_cols, 3 * HD)
    scaling = LOG_TWO_E / math.sqrt(HD) * jax.nn.softplus(query_scale)
    scale_rows = jnp.tile(
        jnp.concatenate([scaling, jnp.ones((2 * HD,), f32)]), own
    )[:, None]

    w_rows = owner_w.T
    if group == 8 and n_tensor == 2:
        me = ctx_rank * n_tensor + tensor_rank
        spots, pieces = [], []

        def swap(x, bit):
            return lax.ppermute(x, ("ctx", "tensor"), [(i, i ^ bit) for i in range(group)])

        def add(heads_x, after, parts):
            spots.extend((distance, first) for distance, first, _ in parts)
            pieces.extend(piece for _, _, piece in parts)
            slots = jnp.stack([me ^ distance for distance, _, _ in parts])
            places = [first for _, first, _ in parts]
            shape = (group, head_width, rows)
            return project_into(heads_x, after, shape, slots, places, w_rows, scale_rows, [piece for _, _, piece in parts])

        def with_core(distance, low, high):
            return [
                (distance ^ bit, first, swap(piece, bit) if bit else piece)
                for bit in (0, 2)
                for first, piece in ((0, low), (rows // 2, high))
            ]

        own_parts = with_core(0, *halves)
        heads_x, _ = add(None, None, own_parts[:2])
        heads_x, done = add(heads_x, None, own_parts[2:])
        over_x, over_y = [swap(halves[0], 1)], [swap(halves[1], 4)]
        over_x.append(swap(halves[1], 1))
        over_y.append(swap(halves[0], 4))
        corner = [swap(over_x[0], 4), swap(over_y[0], 1)]
        over_x, over_y, full_rows, qkv_rows_full, tiles, done = lax.optimization_barrier(
            (over_x, over_y, full_rows, qkv_rows_full, tiles, done)
        )
        heads_x, done = add(heads_x, done, with_core(1, *over_x))
        heads_x, done = add(heads_x, done, with_core(4, over_y[1], over_y[0]))
        corner, done = lax.optimization_barrier((corner, done))
        heads_x, _ = add(heads_x, done, with_core(5, *corner))
    else:
        spots = None
        normed_all = lax.all_gather(normed_one, ("ctx", "tensor"), axis=0)
        heads_x = (nt(w_rows, normed_all.reshape(length, width)) * scale_rows).astype(bf16)
        heads_x = heads_x.reshape(head_width, group, rows).transpose(1, 0, 2)
    whole = lax.all_gather(full_rows, data, axis=1, tiled=True)
    out_t, up_all, down_t = whole[0], whole[1], whole[2]
    qkv_all = lax.all_gather(qkv_rows_full, data, axis=0, tiled=True)

    chunk = max(rows, BLOCK_Q, BLOCK_K)
    merge = chunk // rows
    chunks = length // chunk

    def to_chunks(x):
        if merge == 1:
            return x
        x = jnp.moveaxis(x.reshape((chunks, merge) + x.shape[1:]), 1, -2)
        return x.reshape(x.shape[:-2] + (chunk,))

    def from_chunks(x):
        if merge == 1:
            return x
        x = jnp.moveaxis(x.reshape(x.shape[:-1] + (merge, rows)), -2, 1)
        return x.reshape((group,) + x.shape[2:])

    def to_tokens(x):
        x = from_chunks(x)
        if not split:
            x = lax.dynamic_slice_in_dim(x, ctx_rank * n_tensor, n_tensor, 0)
        return lax.all_to_all(x, owners, 0, 0)

    def to_heads(x):
        x = lax.all_to_all(x, owners, 0, 0)
        if not split:
            x = lax.all_gather(x, "ctx", axis=0, tiled=True)
        return to_chunks(x)

    heads_x = to_chunks(heads_x)
    heads_x = heads_x.reshape(chunks, own, 3, HD, chunk)
    seg_chunks = segments.reshape(1, chunks, chunk)

    part = n_owners * HD

    mixed, wides, lses = [], [], []
    for p in range(own):
        o, wide, lse = attend(tiles, heads_x, seg_chunks, p)
        wides.append(wide)
        lses.append(lse)
        mixed.append(to_tokens(o).reshape(part, rows))

    hidden = inputs
    for p in range(own):
        hidden = hidden + dot(mixed[p], out_t[:, p * part : (p + 1) * part], (0,), (1,))
    inverse_two = inverse_rms(hidden)
    unit_two = hidden * inverse_two
    normed_two = (unit_two * gain_mlp).astype(bf16)
    pre_act = nn(normed_two, up_all) + b_up
    sigma = jax.nn.sigmoid(pre_act)
    activation = (pre_act * sigma).astype(bf16)
    outputs = (hidden + (nt(activation, down_t) + b_down)).astype(bf16)

    top_low = cotangent[:, 0]
    grad_top = top_low.astype(f32)
    grad_pre = (nn(top_low, down_t) * (sigma * (1 + pre_act * (1 - sigma)))).astype(bf16)
    grad_normed_two = nt(grad_pre, up_all)
    grad_hidden = grad_top + norm_back(grad_normed_two, unit_two, inverse_two, gain_mlp)
    grad_hidden_low = grad_hidden.astype(bf16)
    grad_heads = [
        nt(out_t[:, p * part : (p + 1) * part].T, grad_hidden_low).astype(bf16).reshape(n_owners, HD, rows)
        for p in range(own)
    ]
    grad_heads[0], low, act, normed, outputs = lax.optimization_barrier(
        (grad_heads[0], grad_hidden_low, activation, normed_two, outputs)
    )
    grad_heads = [to_heads(g) for g in grad_heads]
    grad_out_t = [dot(low, m, (0,), (1,)) for m in mixed]
    grad_up = dot(normed, grad_pre, (0,), (0,))
    grad_down_t = dot(top_low, act, (0,), (0,))
    stacked = jnp.concatenate([in_rows(g) for g in (*grad_out_t, grad_up, grad_down_t)], axis=1)
    stacked, qkv_all = lax.optimization_barrier((stacked, qkv_all))
    reduced = lax.psum_scatter(stacked, data, scatter_dimension=0, tiled=True)
    reduced = [reduced[:, n * width : (n + 1) * width] for n in range(3)]
    gain_two = jnp.sum(grad_normed_two * unit_two, axis=0)
    bias_up = jnp.sum(grad_pre.astype(f32), axis=0)
    bias_down = jnp.sum(grad_top, axis=0)
    scale_tile = jnp.broadcast_to(scaling[:, None], (HD, 128))
    scale_sum = jnp.zeros((HD,), f32)
    gain_part = jnp.zeros((width,), f32)
    backs, wgrads, travelled = [], [], []
    for p in range(own):
        if p:
            heads_x, grad_heads[p], wgrads[-1] = lax.optimization_barrier((heads_x, grad_heads[p], wgrads[-1]))
        dx, part_sum = attend_back(
            tiles, heads_x, grad_heads[p], wides[p], lses[p], seg_chunks, scale_tile, p
        )
        if p:
            dx, backs[-1] = lax.optimization_barrier((dx, backs[-1]))
        scale_sum = scale_sum + jnp.sum(part_sum, axis=1)
        backs.append(to_tokens(dx).reshape(3 * part, rows))
        if p == own - 1:
            grad_normed_one = jnp.zeros((rows, width), f32)
            for n in range(own - 1):
                grad_normed_one = grad_normed_one + input_grad(backs[n], qkv_all, n, ())
            dx, grad_normed_one = lax.optimization_barrier((dx, grad_normed_one))
        if spots is None:
            grad_w = lax.dot_general(
                to_chunks(jnp.swapaxes(normed_all, 1, 2)),
                dx.reshape(chunks, 3 * HD, chunk),
                (((0, 2), (0, 2)), ((), ())),
                preferred_element_type=f32,
            )
            weights_p = owner_w.reshape(width, own, 3 * HD)[:, p].astype(f32)
            gain_part = gain_part + jnp.sum(grad_w * weights_p, axis=1)
            wgrads.append(grad_w.astype(bf16))
        else:
            own_w = w_rows[p * 3 * HD : (p + 1) * 3 * HD]
            grad_w, gain_add = weight_grad(me.reshape(1), pieces, spots, own_w, dx)
            wgrads.append(grad_w.T)
            gain_part = gain_part + gain_add[0]
        if p == own - 1:
            split_out = reduced[0].reshape(shard, own, ctx_parts, n_tensor, HD).transpose(3, 0, 2, 1, 4)
            split_up, split_down = (
                reduced[n].reshape(shard, n_tensor, columns).transpose(1, 0, 2) for n in (1, 2)
            )
            mine = scatter_pair(
                jnp.stack([split_out.reshape(n_tensor, shard, columns), split_up, split_down], axis=1)
            )
            out_grad, up_grad, down_grad = mine[0].T, mine[1], mine[2].T
            wgrads[-1], gain_part, backs[-1], out_grad, up_grad, down_grad = lax.optimization_barrier(
                (wgrads[-1], gain_part, backs[-1], out_grad, up_grad, down_grad)
            )
        rows_by = by_distance(wgrads[-1].reshape(n_dp, n_ctx * shard, 3 * HD), lax.axis_index("dp"))
        wgrads[-1] = rows_by[0]
        travelled.append(
            [lax.ppermute(rows_by[k], "dp", [(i, i ^ k) for i in range(n_dp)]) for k in range(1, n_dp)]
        )
    gain_one, scale_sum = gain_part / gain_attn, scale_sum / scaling
    if not split:
        once = (ctx_rank == 0).astype(f32)
        gain_one, scale_sum = gain_one * once, scale_sum * once
    def across(x, axis):
        count = lax.axis_size(axis)
        return [x] + [lax.ppermute(x, axis, [(i, i ^ k) for i in range(count)]) for k in range(1, count)]

    sums = jnp.concatenate([gain_one, gain_two, bias_up, bias_down, scale_sum])
    small = all(n & (n - 1) == 0 and n <= 4 for n in (n_dp, n_ctx, n_tensor))
    if small:
        sums = sum(across(sums, "dp"))
    piece = jnp.concatenate(
        [sum((g.astype(f32) for g in far), w.astype(f32)).astype(bf16) for w, far in zip(wgrads, travelled, strict=True)],
        axis=1,
    )
    piece, sums = lax.optimization_barrier((piece, sums))
    piece = piece.reshape(n_ctx, shard, head_width)
    if split:
        piece = exchange(piece, "ctx", ctx_rank)
    else:
        piece = lax.dynamic_slice_in_dim(piece, ctx_rank, 1, 0)
    if small:
        sums = sum(across(sums, "ctx"))
        sums, piece = lax.optimization_barrier((sums, piece))
        sums = sum(across(sums, "tensor"))
    else:
        sums = lax.psum(sums, everyone)
    qkv_grad = piece.reshape(ctx_parts, shard, own, 3, HD).transpose(3, 1, 0, 2, 4)
    qkv_grad = qkv_grad.reshape(w_qkv.shape).astype(f32)

    grad_inputs = input_grad(
        backs[-1], qkv_all, own - 1, (grad_normed_one, tokens[:, 0], gain_attn[None], grad_hidden)
    )
    gain_one, gain_two, bias_up, bias_down = (sums[n * width : (n + 1) * width] for n in range(4))
    grad_query_scale = sums[4 * width :] * (LOG_TWO_E / math.sqrt(HD)) * jax.nn.sigmoid(query_scale)
    return (
        outputs[:, None],
        grad_inputs[:, None],
        qkv_grad,
        out_grad,
        up_grad,
        down_grad,
        gain_one,
        grad_query_scale,
        gain_two,
        bias_up,
        bias_down,
    )


def solution(mesh):
    placed = (
        P(("ctx", "tensor"), "dp", None),
        P("dp", None),
        P(),
        P(),
        P(None, ("dp", "ctx"), "tensor"),
        P("tensor", ("dp", "ctx")),
        P(),
        P(("dp", "ctx"), "tensor"),
        P(),
        P("tensor", ("dp", "ctx")),
        P(),
        P(("ctx", "tensor"), "dp", None),
    )
    return jax.shard_map(
        per_device,
        mesh=mesh,
        in_specs=placed,
        out_specs=(
            P(("ctx", "tensor"), "dp", None),
            P(("ctx", "tensor"), "dp", None),
            P(None, ("dp", "ctx"), "tensor"),
            P("tensor", ("dp", "ctx")),
            P(("dp", "ctx"), "tensor"),
            P("tensor", ("dp", "ctx")),
            P(),
            P(),
            P(),
            P(),
            P(),
        ),
        check_vma=False,
    )
```

time: 620 us -> 557 us (0.90)
  matrix products: 124 us -> 58.3 us
  Pallas kernels: 208 us -> 243 us
  starting transfers between devices: 80.3 us -> 63.6 us
  local copies, waits for them, and re-layouts: 59.4 us -> 43 us
  waiting for transfers between devices: 85.6 us -> 100 us
  other arithmetic: 41.7 us -> 28.2 us
    dot_general x24 -> x12, matrix products: 124 us -> 58.3 us  [dot(): lax.dot_general(a, b, ((contract_a, contract_b), ((), ())), preferred_ele...]
    pallas_call x0 -> x7, Pallas kernels: none -> 58 us  [the longest x5 34 us: project_into(): pl.pallas_call(functools.partial(project_body, places=places), in_specs=[...]
    pallas_call x2, Pallas kernels: 81.2 us -> 58.2 us  [attend(): pl.pallas_call(functools.partial(attend_body, chunks=chunks, chunk=chunk)...]
    ppermute x9 -> x17, starting transfers between devices: 40.5 us -> 21.3 us  [the longest x6 9.02 us: per_device(): lax.ppermute(rows_by[k], 'dp', [(i, i ^ k) for i in range(n_dp)])]
    ppermute x1, waiting for transfers between devices: 0.01 us -> 10.6 us  [scatter_pair(): lax.ppermute(send, 'tensor', [(0, 1), (1, 0)]).astype(f32)]
    broadcast_in_dim x1 -> x0, other arithmetic: 9.38 us -> none  [per_device(): grad_inputs.astype(bf16)[:, None]]
    ppermute x9 -> x17, waiting for transfers between devices: 12.8 us -> 18.5 us  [the longest x6 15 us: per_device(): lax.ppermute(rows_by[k], 'dp', [(i, i ^ k) for i in range(n_dp)])]
    pallas_call x1 -> x2, Pallas kernels: 21.9 us -> 25.1 us  [weight_grad(): pl.pallas_call(functools.partial(weight_grad_body, spots=spots), in_specs...]
  transfers between devices with their start and end apart: 35 -> 48, of which waited for: 7 -> 18; matrix products, arithmetic and copies ran while one was open for 34% -> 22% of each run, Pallas kernels for 34% -> 44%
where the time goes in v2:
time: 557 us; the launch traced here: 552 us
  Pallas kernels  243 us (44%)
  waiting for transfers between devices  100 us (18%)
  starting transfers between devices  63.6 us (11%)
  matrix products  58.3 us (10%)
  local copies, waits for them, and re-layouts  43 us (8%)
  other arithmetic  28.2 us (5%)
  between operations  15.8 us (3%)
    pallas_call x2, Pallas kernels, attend_back(): pl.pallas_call(functools.partial(attend_back_body, chunks=chunks, chunk=c...  102 us
    dot_general x12, matrix products, dot(): lax.dot_general(a, b, ((contract_a, contract_b), ((), ())), preferred_ele...  58.3 us
    pallas_call x2, Pallas kernels, attend(): pl.pallas_call(functools.partial(attend_body, chunks=chunks, chunk=chunk)...  58.2 us
    ppermute x14, waiting for transfers between devices, swap(): lax.ppermute(x, ('ctx', 'tensor'), [(i, i ^ bit) for i in range(group)])  40.1 us
    pallas_call x5, Pallas kernels, project_into(): pl.pallas_call(functools.partial(project_body, places=places), in_specs=[...  34 us
    pallas_call x2, Pallas kernels, weight_grad(): pl.pallas_call(functools.partial(weight_grad_body, spots=spots), in_specs...  25.1 us
    pallas_call x2, Pallas kernels, input_grad(): pl.pallas_call(finish_body if others else back_one_body, grid=(rows // bl...  24 us
    all_to_all x4, starting transfers between devices, to_tokens(): return lax.all_to_all(x, owners, 0, 0)  18.2 us
  transfers between devices with their start and end apart: 48, of which 18 were waited for; matrix products, arithmetic and copies ran while one was open for 22% of the time, Pallas kernels for 44%

profile of v2, /device:TPU:0, one launch (start us, length us, event | category | flops | bytes accessed | tf_op | source)
XLA Modules:
  0.0 552.3 jit_solution(6138331146569196182)
XLA Ops:
  7.2 3.0 collective-permute-start.3
  60.6 4.6 all-gather.9.cloned.1.call-done
  65.2 2.5 copy.156
  67.7 5.8 %project.5 = (bf16[8,480,1024]{2,1,0:T(8,128)(2,1)}, f32[8,128]{1,0:T(8,128)}) custom-call(s32[2]{0:T(128)} %pad_add_fusion.1.slots_ref, bf16[480,1280]{1,0:T(8,128)(2,1)} %bitcast.203, f32[480,1]{1,0:T(8,128)} %broadcast_in_dim_tile.4.scale_ref, bf16[512,1280]{1,0:T(8,128)(2,1)} %get-tuple-element.76.refs_0_, bf16[512,1280]{1,0:T(8,128)(2,1)} %get-tuple-element.77.refs_1_), custom_call_target="tpu_custom_call" | custom-call | flops 1258291200 | bytes 5242880 | tf_op jit(solution)/shard_map/project/pallas_call | solution.py:290
  73.5 5.8 %project.6 = (bf16[8,480,1024]{2,1,0:T(8,128)(2,1)}, f32[8,128]{1,0:T(8,128)}) custom-call(s32[2]{0:T(128)} %pad_add_fusion.slots_ref, bf16[480,1280]{1,0:T(8,128)(2,1)} %bitcast.204, f32[480,1]{1,0:T(8,128)} %broadcast_in_dim_tile.4.scale_ref, bf16[512,1280]{1,0:T(8,128)(2,1)} %collective-permute-done.11.refs_0_.refs_2_, ...), custom_call_target="tpu_custom_call", output_to_operand_aliasing={{0}: (5, {})} | custom-call | flops 1258291200 | bytes 5242880 | tf_op jit(solution)/shard_map/project/pallas_call | solution.py:290
  79.3 15.4 %collective-permute-done.10.refs_0_.refs_8_ = bf16[512,1280]{1,0:T(8,128)(2,1)} collective-permute-done((bf16[512,1280]{1,0:T(8,128)(2,1)}, bf16[512,1280]{1,0:T(8,128)(2,1)}, u32[]{:S(2)}, u32[]{:S(2)}) %collective-permute-start.10) | collective-permute-done | bytes 1310752 | tf_op jit(solution)/shard_map/ppermute | solution.py:539
  100.3 7.5 %project.7 = (bf16[8,480,1024]{2,1,0:T(8,128)(2,1)}, f32[8,128]{1,0:T(8,128)}) custom-call(s32[4]{0:T(128)} %pad_add_fusion.4.slots_ref, bf16[480,1280]{1,0:T(8,128)(2,1)} %bitcast.205, f32[480,1]{1,0:T(8,128)} %broadcast_in_dim_tile.4.scale_ref, bf16[512,1280]{1,0:T(8,128)(2,1)} %collective-permute-done.7.refs_0_.refs_4_, ...), custom_call_target="tpu_custom_call", output_to_operand_aliasing={{0}: (7, {})} | custom-call | flops 2516582400 | bytes 10485760 | tf_op jit(solution)/shard_map/project/pallas_call | solution.py:290
  107.9 7.5 %project.8 = (bf16[8,480,1024]{2,1,0:T(8,128)(2,1)}, f32[8,128]{1,0:T(8,128)}) custom-call(s32[4]{0:T(128)} %pad_add_fusion.3.slots_ref, bf16[480,1280]{1,0:T(8,128)(2,1)} %bitcast.206, f32[480,1]{1,0:T(8,128)} %broadcast_in_dim_tile.4.scale_ref, bf16[512,1280]{1,0:T(8,128)(2,1)} %collective-permute-done.10.refs_0_.refs_8_, ...), custom_call_target="tpu_custom_call", output_to_operand_aliasing={{0}: (7, {})} | custom-call | flops 2516582400 | bytes 10485760 | tf_op jit(solution)/shard_map/project/pallas_call | solution.py:290
  115.3 18.4 %collective-permute-done.13.refs_0_.refs_12_ = bf16[512,1280]{1,0:T(8,128)(2,1)} collective-permute-done((bf16[512,1280]{1,0:T(8,128)(2,1)}, bf16[512,1280]{1,0:T(8,128)(2,1)}, u32[]{:S(2)}, u32[]{:S(2)}) %collective-permute-start.13) | collective-permute-done | bytes 1310752 | tf_op jit(solution)/shard_map/ppermute | solution.py:539
  137.1 3.7 collective-permute-done.20.refs_3_.refs_15_
  140.8 7.5 %project.9 = (bf16[8,480,1024]{2,1,0:T(8,128)(2,1)}, f32[8,128]{1,0:T(8,128)}) custom-call(s32[4]{0:T(128)} %pad_add_fusion.2.slots_ref, bf16[480,1280]{1,0:T(8,128)(2,1)} %bitcast.207, f32[480,1]{1,0:T(8,128)} %broadcast_in_dim_tile.4.scale_ref, bf16[512,1280]{1,0:T(8,128)(2,1)} %collective-permute-done.13.refs_0_.refs_12_, ...), custom_call_target="tpu_custom_call", output_to_operand_aliasing={{0}: (7, {})} | custom-call | flops 2516582400 | bytes 10485760 | tf_op jit(solution)/shard_map/project/pallas_call | solution.py:290
  148.3 29.1 %attend.2 = (bf16[8,80,1024]{2,1,0:T(8,128)(2,1)}, f32[8,80,1024]{2,1,0:T(8,128)}, f32[1,8,1024]{2,1,0:T(8,128)}) custom-call(s32[1]{0:T(128)} %bitcast.28.count, s32[258]{0:T(512)} %fusion.25.tiles, bf16[8,2,3,80,1024]{4,3,2,1,0:T(8,128)(2,1)} %bitcast.199, s32[1,8,1024]{2,1,0:T(8,128)} %bitcast.252), custom_call_target="tpu_custom_call" | custom-call | flops 17179869184 | bytes 16777216 | tf_op jit(solution)/shard_map/attend/pallas_call | solution.py:183
  177.4 4.5 all-to-all-start
  181.9 29.1 %attend.3 = (bf16[8,80,1024]{2,1,0:T(8,128)(2,1)}, f32[8,80,1024]{2,1,0:T(8,128)}, f32[1,8,1024]{2,1,0:T(8,128)}) custom-call(s32[1]{0:T(128)} %bitcast.28.count, s32[258]{0:T(512)} %fusion.25.tiles, bf16[8,2,3,80,1024]{4,3,2,1,0:T(8,128)(2,1)} %bitcast.200, s32[1,8,1024]{2,1,0:T(8,128)} %bitcast.253), custom_call_target="tpu_custom_call" | custom-call | flops 17179869184 | bytes 16777216 | tf_op jit(solution)/shard_map/attend/pallas_call | solution.py:183
  211.0 4.3 all-to-all-start.1
  219.3 5.9 %fusion.13 = f32[1024,1280]{1,0:T(8,128)} fusion(bf16[640,1024]{1,0:T(8,128)(2,1)} %bitcast.42, bf16[1280,1280]{1,0:T(8,128)(2,1)S(1)} %slice_bitcast_fusion.2), kind=kOutput, calls=%fused_computation.37 | convolution fusion | flops 1677721600 | bytes 8192000 | tf_op jit(solution)/shard_map/dot_general | solution.py:27
  225.1 10.3 %all-to-all-done.1 = bf16[8,80,1024]{2,1,0:T(8,128)(2,1)} async-done(((bf16[8,80,1024]{2,1,0:T(8,128)(2,1)}), bf16[8,80,1024]{2,1,0:T(8,128)(2,1)}, u32[]{:S(2)}, u32[]{:S(2)}) %all-to-all-start.1) | async-done | bytes 1310752 | tf_op jit(solution)/shard_map/all_to_all | solution.py:599
  235.4 5.9 %multiply_reduce_fusion.2 = (f32[1024]{0:T(1024)S(1)}, f32[1024,1280]{1,0:T(8,128)S(1)}) fusion(bf16[640,1024]{1,0:T(8,128)(2,1)} %bitcast.43, bf16[1280,1280]{1,0:T(8,128)(2,1)} %copy-done.2, f32[1024,1280]{1,0:T(8,128)} %fusion.13, bf16[1024,1,1280]{2,0,1:T(8,128)(2,1)S(1)} %copy-done.1), kind=kOutput, calls=%fused_computation.22 | convolution fusion | flops 1684274176 | bytes 16060416 | tf_op jit(solution)/shard_map/dot_general | solution.py:27
  242.1 7.8 %multiply_convert_fusion = (bf16[1024,1280]{1,0:T(8,128)(2,1)}, f32[1024,1280]{1,0:T(8,128)S(1)}) fusion(f32[1280]{0:T(1024)S(1)} %copy-done.25, bf16[1024,1280]{1,0:T(8,128)(2,1)S(1)} %multiply_convert_fusion.1, bf16[3,1280,1280]{2,1,0:T(8,128)(2,1)} %all-gather.5.cloned.1.call-done), kind=kOutput, calls=%fused_computation.18 | convolution fusion | flops 3363307520 | bytes 13767680 | tf_op jit(solution)/shard_map/dot_general | solution.py:27
  249.9 5.6 %convert_reduce_fusion.1 = (f32[1280]{0:T(1024)}, bf16[1024,1280]{1,0:T(8,128)(2,1)S(1)}) fusion(f32[1024,1280]{1,0:T(8,128)S(1)} %get-tuple-element.189, f32[1280]{0:T(1024)S(1)} %copy-done.25, bf16[3,1280,1280]{2,1,0:T(8,128)(2,1)S(1)} %bitcast.230, bf16[1024,1,1280]{2,0,1:T(8,128)(2,1)S(1)} %copy-done.4), kind=kOutput, calls=%fused_computation.15 | convolution fusion | flops 3371170560 | bytes 13775872 | tf_op jit(solution)/shard_map/dot_general | solution.py:27
  255.5 4.5 multiply_reduce_fusion
  260.0 3.9 fusion.27
  263.9 3.0 convolution_convert_fusion.5
  266.9 5.0 add_convert_fusion
  272.0 3.6 convolution_convert_fusion.3
  275.6 3.7 convolution_convert_fusion.2
  279.3 3.9 convolution_convert_fusion.1
  283.3 4.0 fusion
  287.3 4.3 pad_maximum_fusion
  291.7 4.9 all-to-all-start.3
  297.7 5.3 convolution_convert_fusion.4
  303.0 11.3 %all-to-all-done.3.g_ref = bf16[8,80,1024]{2,1,0:T(8,128)(2,1)S(1)} async-done(((bf16[8,80,1024]{2,1,0:T(8,128)(2,1)}), bf16[8,80,1024]{2,1,0:T(8,128)(2,1)S(1)}, u32[]{:S(2)}, u32[]{:S(2)}) %all-to-all-start.3) | async-done | bytes 1310752 | tf_op jit(solution)/shard_map/all_to_all | solution.py:602
  315.4 4.0 all-to-all-start.2
  320.1 50.9 %attend_back.2 = (bf16[8,3,80,1024]{3,2,1,0:T(8,128)(2,1)}, f32[80,128]{1,0:T(8,128)}) custom-call(s32[1]{0:T(128)} %bitcast.28.count, s32[258]{0:T(512)} %fusion.25.tiles, bf16[8,2,3,80,1024]{4,3,2,1,0:T(8,128)(2,1)} %bitcast.201, bf16[8,80,1024]{2,1,0:T(8,128)(2,1)} %copy-done.7, f32[8,80,1024]{2,1,0:T(8,128)} %get-tuple-element.106.wide_ref, ...), custom_call_target="tpu_custom_call" | custom-call | flops 42949672960 | bytes 16777216 | tf_op jit(solution)/shard_map/attend_back/pallas_call | solution.py:220
  371.0 12.6 %weight_grad.2 = (bf16[240,1280]{1,0:T(8,128)(2,1)}, f32[1,1280]{1,0:T(1,128)}) custom-call(s32[1]{0:T(128)} %bitcast.32.me_ref, bf16[512,1280]{1,0:T(8,128)(2,1)} %get-tuple-element.76.refs_0_, bf16[512,1280]{1,0:T(8,128)(2,1)} %get-tuple-element.77.refs_1_, bf16[512,1280]{1,0:T(8,128)(2,1)} %collective-permute-done.11.refs_0_.refs_2_, ...), custom_call_target="tpu_custom_call" | custom-call | flops 1 | bytes 1 | tf_op jit(solution)/shard_map/weight_grad/pallas_call | solution.py:335
  386.3 4.7 all-to-all-start.4
  391.0 51.1 %attend_back.3 = (bf16[8,3,80,1024]{3,2,1,0:T(8,128)(2,1)}, f32[80,128]{1,0:T(8,128)}) custom-call(s32[1]{0:T(128)} %bitcast.28.count, s32[258]{0:T(512)} %fusion.25.tiles, bf16[8,2,3,80,1024]{4,3,2,1,0:T(8,128)(2,1)} %bitcast.202, bf16[8,80,1024]{2,1,0:T(8,128)(2,1)} %copy-done.6, f32[8,80,1024]{2,1,0:T(8,128)} %get-tuple-element.112.wide_ref, ...), custom_call_target="tpu_custom_call" | custom-call | flops 42949672960 | bytes 16777216 | tf_op jit(solution)/shard_map/attend_back/pallas_call | solution.py:220
  442.1 4.7 all-to-all-start.5
  449.3 2.8 collective-permute-start.23
  457.3 7.0 %collective-permute-done.23 = bf16[320,240]{1,0:T(8,128)(2,1)S(1)} collective-permute-done((bf16[320,240]{1,0:T(8,128)(2,1)S(1)}, bf16[320,240]{1,0:T(8,128)(2,1)S(1)}, u32[]{:S(2)}, u32[]{:S(2)}) %collective-permute-start.23) | collective-permute-done | bytes 153632 | tf_op jit(solution)/shard_map/ppermute | solution.py:704
  464.4 10.3 %input_grad.2.other_ref = f32[1024,1280]{1,0:T(8,128)} custom-call(bf16[1920,1024]{1,0:T(8,128)(2,1)} %bitcast.55.back_ref, bf16[1280,3840]{1,0:T(8,128)(2,1)} %all-gather.7.cloned.1.call-done.w_ref), custom_call_target="tpu_custom_call" | custom-call | flops 1 | bytes 1 | tf_op jit(solution)/shard_map/input_grad/pallas_call | solution.py:375
  474.8 12.5 %weight_grad.3 = (bf16[240,1280]{1,0:T(8,128)(2,1)}, f32[1,1280]{1,0:T(1,128)}) custom-call(s32[1]{0:T(128)} %bitcast.32.me_ref, bf16[512,1280]{1,0:T(8,128)(2,1)} %get-tuple-element.76.refs_0_, bf16[512,1280]{1,0:T(8,128)(2,1)} %get-tuple-element.77.refs_1_, bf16[512,1280]{1,0:T(8,128)(2,1)} %collective-permute-done.11.refs_0_.refs_2_, ...), custom_call_target="tpu_custom_call" | custom-call | flops 1 | bytes 1 | tf_op jit(solution)/shard_map/weight_grad/pallas_call | solution.py:335
  488.0 10.6 %collective-permute-done.21 = bf16[3,80,640]{2,1,0:T(8,128)(2,1)S(1)} collective-permute-done((bf16[3,80,640]{2,1,0:T(8,128)(2,1)S(1)}, bf16[3,80,640]{2,1,0:T(8,128)(2,1)S(1)}, u32[]{:S(2)}, u32[]{:S(2)}) %collective-permute-start.21) | collective-permute-done | bytes 307232 | tf_op jit(solution)/shard_map/ppermute | solution.py:476
  501.4 2.8 collective-permute-start.29
  505.5 3.7 collective-permute-start.26
  509.2 13.6 %input_grad.3 = bf16[1024,1280]{1,0:T(8,128)(2,1)} custom-call(bf16[1920,1024]{1,0:T(8,128)(2,1)} %bitcast.58.back_ref, bf16[1280,3840]{1,0:T(8,128)(2,1)} %all-gather.7.cloned.1.call-done.w_ref, f32[1024,1280]{1,0:T(8,128)} %input_grad.2.other_ref, bf16[1024,1280]{1,0:T(8,128)(2,1)} %bitcast.209, f32[1,1280]{1,0:T(1,128)} %broadcast_in_dim.66.gain_ref, ...), custom_call_target="tpu_custom_call" | custom-call | flops 5033164800 | bytes 20971520 | tf_op jit(solution)/shard_map/input_grad/pallas_call | solution.py:375
  523.0 7.2 %collective-permute-done.27 = bf16[320,240]{1,0:T(8,128)(2,1)S(1)} collective-permute-done((bf16[320,240]{1,0:T(8,128)(2,1)S(1)}, bf16[320,240]{1,0:T(8,128)(2,1)S(1)}, u32[]{:S(2)}, u32[]{:S(2)}) %collective-permute-start.27) | collective-permute-done | bytes 153632 | tf_op jit(solution)/shard_map/ppermute | solution.py:704
  535.3 2.7 collective-permute-done.35
  (266 shorter events, 93.6 us)
Async XLA Ops:
  7.2 58.0 %all-gather.9.cloned.1.call-start = ((), (), s32[]{:S(2)}) async-start(), calls=%async_computation.10 | async-start | bytes 1638400 | tf_op jit(solution)/shard_map/all_gather | solution.py:505
  7.2 20.8 %collective-permute-start.3 = (bf16[3,80,640]{2,1,0:T(8,128)(2,1)}, bf16[3,80,640]{2,1,0:T(8,128)(2,1)}, u32[]{:S(2)}, u32[]{:S(2)}) collective-permute-start(bf16[3,80,640]{2,1,0:T(8,128)(2,1)} %param.16), channel_id=1, source_target_pairs={{0,1},{1,0},{2,3},{3,2},{4,5},{5,4},{6,7},{7,6},{8,9},{9,8},{10,11... | collective-permute-start | bytes 921608 | tf_op jit(solution)/shard_map/ppermute | solution.py:463
  14.3 6.5 %collective-permute-start.2 = (bf16[80,480]{1,0:T(8,128)(2,1)S(1)}, bf16[80,480]{1,0:T(8,128)(2,1)S(1)}, u32[]{:S(2)}, u32[]{:S(2)}) collective-permute-start(bf16[80,480]{1,0:T(8,128)(2,1)S(1)} %bitcast.245), channel_id=1, source_target_pairs={{0,6},{2,4},{4,2},{6,0},{1,7},{3,5},{5,3},{7,1},{8,14},{10,12},{12... | collective-permute-start | bytes 230408 | tf_op jit(solution)/shard_map/ppermute | solution.py:492
  15.2 7.6 %collective-permute-start = (bf16[80,480]{1,0:T(8,128)(2,1)S(1)}, bf16[80,480]{1,0:T(8,128)(2,1)S(1)}, u32[]{:S(2)}, u32[]{:S(2)}) collective-permute-start(bf16[80,480]{1,0:T(8,128)(2,1)S(1)} %bitcast.244), channel_id=1, source_target_pairs={{0,2},{2,0},{4,6},{6,4},{1,3},{3,1},{5,7},{7,5},{8,10},{10,8},{12,... | collective-permute-start | bytes 230408 | tf_op jit(solution)/shard_map/ppermute | solution.py:492
  16.3 6.6 %collective-permute-start.1 = (bf16[80,480]{1,0:T(8,128)(2,1)S(1)}, bf16[80,480]{1,0:T(8,128)(2,1)S(1)}, u32[]{:S(2)}, u32[]{:S(2)}) collective-permute-start(bf16[80,480]{1,0:T(8,128)(2,1)S(1)} %bitcast.243), channel_id=1, source_target_pairs={{0,4},{2,6},{4,0},{6,2},{1,5},{3,7},{5,1},{7,3},{8,12},{10,14},{12... | collective-permute-start | bytes 230408 | tf_op jit(solution)/shard_map/ppermute | solution.py:492
  16.9 8.1 %collective-permute-start.4 = (bf16[640,80]{0,1:T(8,128)(2,1)}, bf16[640,80]{0,1:T(8,128)(2,1)}, u32[]{:S(2)}, u32[]{:S(2)}) collective-permute-start(bf16[640,80]{0,1:T(8,128)(2,1)} %param.17), channel_id=1, source_target_pairs={{0,1},{1,0},{2,3},{3,2},{4,5},{5,4},{6,7},{7,6},{8,9},{9,8},{10,11... | collective-permute-start | bytes 307208 | tf_op jit(solution)/shard_map/ppermute | solution.py:463
  20.8 6.1 %collective-permute-start.5 = (bf16[80,640]{1,0:T(8,128)(2,1)}, bf16[80,640]{1,0:T(8,128)(2,1)}, u32[]{:S(2)}, u32[]{:S(2)}) collective-permute-start(bf16[80,640]{1,0:T(8,128)(2,1)} %param.19), channel_id=1, source_target_pairs={{0,1},{1,0},{2,3},{3,2},{4,5},{5,4},{6,7},{7,6},{8,9},{9,8},{10,11... | collective-permute-start | bytes 307208 | tf_op jit(solution)/shard_map/ppermute | solution.py:463
  22.7 5.3 collective-permute-start.6
  28.1 13.6 %collective-permute-start.11 = (bf16[512,1280]{1,0:T(8,128)(2,1)}, bf16[512,1280]{1,0:T(8,128)(2,1)}, u32[]{:S(2)}, u32[]{:S(2)}) collective-permute-start(bf16[512,1280]{1,0:T(8,128)(2,1)} %get-tuple-element.76.refs_0_), channel_id=1, source_target_pairs={{0,2},{1,3},{2,0},{3,1},{4,6},{5,7},{6,4},{7,5},{8,10},{9,11},{10,... | collective-permute-start | bytes 3932168 | tf_op jit(solution)/shard_map/ppermute | solution.py:539
  31.0 184.3 %all-gather.5.cloned.1.call-start = ((), (), s32[]{:S(2)}) async-start(), calls=%async_computation.7 | async-start | bytes 10444800 | tf_op jit(solution)/shard_map/all_gather | solution.py:575
  33.7 45.6 %collective-permute-start.7 = (bf16[512,1280]{1,0:T(8,128)(2,1)}, bf16[512,1280]{1,0:T(8,128)(2,1)}, u32[]{:S(2)}, u32[]{:S(2)}) collective-permute-start(bf16[512,1280]{1,0:T(8,128)(2,1)} %get-tuple-element.76.refs_0_), channel_id=1, source_target_pairs={{0,1},{1,0},{2,3},{3,2},{4,5},{5,4},{6,7},{7,6},{8,9},{9,8},{10,11... | collective-permute-start | bytes 3932168 | tf_op jit(solution)/shard_map/ppermute | solution.py:539
  35.1 38.4 %collective-permute-start.12 = (bf16[512,1280]{1,0:T(8,128)(2,1)}, bf16[512,1280]{1,0:T(8,128)(2,1)}, u32[]{:S(2)}, u32[]{:S(2)}) collective-permute-start(bf16[512,1280]{1,0:T(8,128)(2,1)} %get-tuple-element.77.refs_1_), channel_id=1, source_target_pairs={{0,2},{1,3},{2,0},{3,1},{4,6},{5,7},{6,4},{7,5},{8,10},{9,11},{10,... | collective-permute-start | bytes 3932168 | tf_op jit(solution)/shard_map/ppermute | solution.py:539
  35.3 43.9 %collective-permute-start.9 = (bf16[512,1280]{1,0:T(8,128)(2,1)}, bf16[512,1280]{1,0:T(8,128)(2,1)}, u32[]{:S(2)}, u32[]{:S(2)}) collective-permute-start(bf16[512,1280]{1,0:T(8,128)(2,1)} %get-tuple-element.77.refs_1_), channel_id=1, source_target_pairs={{0,4},{1,5},{2,6},{3,7},{4,0},{5,1},{6,2},{7,3},{8,12},{9,13},{10,... | collective-permute-start | bytes 3932168 | tf_op jit(solution)/shard_map/ppermute | solution.py:539
  36.9 57.9 %collective-permute-start.10 = (bf16[512,1280]{1,0:T(8,128)(2,1)}, bf16[512,1280]{1,0:T(8,128)(2,1)}, u32[]{:S(2)}, u32[]{:S(2)}) collective-permute-start(bf16[512,1280]{1,0:T(8,128)(2,1)} %get-tuple-element.76.refs_0_), channel_id=1, source_target_pairs={{0,4},{1,5},{2,6},{3,7},{4,0},{5,1},{6,2},{7,3},{8,12},{9,13},{10,... | collective-permute-start | bytes 3932168 | tf_op jit(solution)/shard_map/ppermute | solution.py:539
  41.7 53.1 %collective-permute-start.8 = (bf16[512,1280]{1,0:T(8,128)(2,1)}, bf16[512,1280]{1,0:T(8,128)(2,1)}, u32[]{:S(2)}, u32[]{:S(2)}) collective-permute-start(bf16[512,1280]{1,0:T(8,128)(2,1)} %get-tuple-element.77.refs_1_), channel_id=1, source_target_pairs={{0,1},{1,0},{2,3},{3,2},{4,5},{5,4},{6,7},{7,6},{8,9},{9,8},{10,11... | collective-permute-start | bytes 3932168 | tf_op jit(solution)/shard_map/ppermute | solution.py:539
  94.7 196.9 %all-gather.7.cloned.1.call-start = ((), (), s32[]{:S(2)}) async-start(), calls=%async_computation.8 | async-start | bytes 10444800 | tf_op jit(solution)/shard_map/all_gather | solution.py:577
  95.0 3.4 collective-permute-start.17
  95.0 5.2 collective-permute-start.18
  95.5 12.3 %collective-permute-start.15 = (bf16[512,1280]{1,0:T(8,128)(2,1)}, bf16[512,1280]{1,0:T(8,128)(2,1)}, u32[]{:S(2)}, u32[]{:S(2)}) collective-permute-start(bf16[512,1280]{1,0:T(8,128)(2,1)} %collective-permute-done.10.refs_0_.refs_8_), channel_id=1, source_target_pairs={{0,2},{1,3},{2,0},{3,1},{4,6},{5,7},{6,4},{7,5},{8,10},{9,11},{10,... | collective-permute-start | bytes 3932168 | tf_op jit(solution)/shard_map/ppermute | solution.py:539
  95.6 12.2 %collective-permute-start.16 = (bf16[512,1280]{1,0:T(8,128)(2,1)}, bf16[512,1280]{1,0:T(8,128)(2,1)}, u32[]{:S(2)}, u32[]{:S(2)}) collective-permute-start(bf16[512,1280]{1,0:T(8,128)(2,1)} %collective-permute-done.9.refs_1_.refs_9_), channel_id=1, source_target_pairs={{0,2},{1,3},{2,0},{3,1},{4,6},{5,7},{6,4},{7,5},{8,10},{9,11},{10,... | collective-permute-start | bytes 3932168 | tf_op jit(solution)/shard_map/ppermute | solution.py:539
  96.1 37.7 %collective-permute-start.13 = (bf16[512,1280]{1,0:T(8,128)(2,1)}, bf16[512,1280]{1,0:T(8,128)(2,1)}, u32[]{:S(2)}, u32[]{:S(2)}) collective-permute-start(bf16[512,1280]{1,0:T(8,128)(2,1)} %collective-permute-done.7.refs_0_.refs_4_), channel_id=1, source_target_pairs={{0,4},{1,5},{2,6},{3,7},{4,0},{5,1},{6,2},{7,3},{8,12},{9,13},{10,... | collective-permute-start | bytes 3932168 | tf_op jit(solution)/shard_map/ppermute | solution.py:539
  98.4 35.3 %collective-permute-start.14 = (bf16[512,1280]{1,0:T(8,128)(2,1)}, bf16[512,1280]{1,0:T(8,128)(2,1)}, u32[]{:S(2)}, u32[]{:S(2)}) collective-permute-start(bf16[512,1280]{1,0:T(8,128)(2,1)} %collective-permute-done.9.refs_1_.refs_9_), channel_id=1, source_target_pairs={{0,1},{1,0},{2,3},{3,2},{4,5},{5,4},{6,7},{7,6},{8,9},{9,8},{10,11... | collective-permute-start | bytes 3932168 | tf_op jit(solution)/shard_map/ppermute | solution.py:539
  133.7 3.4 collective-permute-start.19
  133.7 7.1 %collective-permute-start.20 = (bf16[512,1280]{1,0:T(8,128)(2,1)}, bf16[512,1280]{1,0:T(8,128)(2,1)}, u32[]{:S(2)}, u32[]{:S(2)}) collective-permute-start(bf16[512,1280]{1,0:T(8,128)(2,1)} %collective-permute-done.14.refs_1_.refs_13_), channel_id=1, source_target_pairs={{0,2},{1,3},{2,0},{3,1},{4,6},{5,7},{6,4},{7,5},{8,10},{9,11},{10,... | collective-permute-start | bytes 3932168 | tf_op jit(solution)/shard_map/ppermute | solution.py:539
  177.4 33.6 %all-to-all-start = ((bf16[8,80,1024]{2,1,0:T(8,128)(2,1)}), bf16[8,80,1024]{2,1,0:T(8,128)(2,1)}, u32[]{:S(2)}, u32[]{:S(2)}) async-start(bf16[8,80,1024]{2,1,0:T(8,128)(2,1)} %get-tuple-element.102), calls=%async_computation | async-start | bytes 2621440 | tf_op jit(solution)/shard_map/all_to_all | solution.py:599
  211.0 24.4 %all-to-all-start.1 = ((bf16[8,80,1024]{2,1,0:T(8,128)(2,1)}), bf16[8,80,1024]{2,1,0:T(8,128)(2,1)}, u32[]{:S(2)}, u32[]{:S(2)}) async-start(bf16[8,80,1024]{2,1,0:T(8,128)(2,1)} %get-tuple-element.103), calls=%async_computation.1 | async-start | bytes 2621440 | tf_op jit(solution)/shard_map/all_to_all | solution.py:599
  215.3 236.8 %reduce-scatter.2.cloned.1.call-start = ((), (), s32[]{:S(2)}) async-start(), calls=%async_computation.9 | async-start | bytes 10444800 | tf_op jit(solution)/shard_map/reduce_scatter | solution.py:650
  291.7 22.6 %all-to-all-start.3 = ((bf16[8,80,1024]{2,1,0:T(8,128)(2,1)}), bf16[8,80,1024]{2,1,0:T(8,128)(2,1)S(1)}, u32[]{:S(2)}, u32[]{:S(2)}) async-start(bf16[8,80,1024]{2,1,0:T(8,128)(2,1)} %bitcast.47), calls=%async_computation.3 | async-start | bytes 2621440 | tf_op jit(solution)/shard_map/all_to_all | solution.py:602
  315.4 69.8 %all-to-all-start.2 = ((bf16[8,80,1024]{2,1,0:T(8,128)(2,1)}), bf16[8,80,1024]{2,1,0:T(8,128)(2,1)S(1)}, u32[]{:S(2)}, u32[]{:S(2)}) async-start(bf16[8,80,1024]{2,1,0:T(8,128)(2,1)} %bitcast.226), calls=%async_computation.2 | async-start | bytes 2621440 | tf_op jit(solution)/shard_map/all_to_all | solution.py:602
  386.3 55.8 %all-to-all-start.4 = ((bf16[8,3,80,1024]{3,2,1,0:T(8,128)(2,1)}), bf16[8,3,80,1024]{3,2,1,0:T(8,128)(2,1)}, u32[]{:S(2)}, u32[]{:S(2)}) async-start(bf16[8,3,80,1024]{3,2,1,0:T(8,128)(2,1)} %get-tuple-element.108.refs_17_), calls=%async_computation.4 | async-start | bytes 7864320 | tf_op jit(solution)/shard_map/all_to_all | solution.py:599
  442.1 57.5 %all-to-all-start.5 = ((bf16[8,3,80,1024]{3,2,1,0:T(8,128)(2,1)}), bf16[8,3,80,1024]{3,2,1,0:T(8,128)(2,1)}, u32[]{:S(2)}, u32[]{:S(2)}) async-start(bf16[8,3,80,1024]{3,2,1,0:T(8,128)(2,1)} %get-tuple-element.122.refs_17_), calls=%async_computation.5 | async-start | bytes 7864320 | tf_op jit(solution)/shard_map/all_to_all | solution.py:599
  447.6 9.6 %collective-permute-start.22 = (bf16[320,240]{1,0:T(8,128)(2,1)S(1)}, bf16[320,240]{1,0:T(8,128)(2,1)S(1)}, u32[]{:S(2)}, u32[]{:S(2)}) collective-permute-start(bf16[320,240]{1,0:T(8,128)(2,1)S(1)} %get-tuple-element.150), channel_id=1, source_target_pairs={{0,8},{8,0},{16,24},{24,16},{1,9},{9,1},{17,25},{25,17},{2,10},{10... | collective-permute-start | bytes 460808 | tf_op jit(solution)/shard_map/ppermute | solution.py:704
  449.3 15.0 %collective-permute-start.23 = (bf16[320,240]{1,0:T(8,128)(2,1)S(1)}, bf16[320,240]{1,0:T(8,128)(2,1)S(1)}, u32[]{:S(2)}, u32[]{:S(2)}) collective-permute-start(bf16[320,240]{1,0:T(8,128)(2,1)S(1)} %get-tuple-element.152), channel_id=1, source_target_pairs={{0,16},{8,24},{16,0},{24,8},{1,17},{9,25},{17,1},{25,9},{2,18},{10... | collective-permute-start | bytes 460808 | tf_op jit(solution)/shard_map/ppermute | solution.py:704
  452.1 12.2 %collective-permute-start.24 = (bf16[320,240]{1,0:T(8,128)(2,1)S(1)}, bf16[320,240]{1,0:T(8,128)(2,1)S(1)}, u32[]{:S(2)}, u32[]{:S(2)}) collective-permute-start(bf16[320,240]{1,0:T(8,128)(2,1)S(1)} %get-tuple-element.151), channel_id=1, source_target_pairs={{0,24},{8,16},{16,8},{24,0},{1,25},{9,17},{17,9},{25,1},{2,26},{10... | collective-permute-start | bytes 460808 | tf_op jit(solution)/shard_map/ppermute | solution.py:704
  454.5 44.2 %collective-permute-start.21 = (bf16[3,80,640]{2,1,0:T(8,128)(2,1)S(1)}, bf16[3,80,640]{2,1,0:T(8,128)(2,1)S(1)}, u32[]{:S(2)}, u32[]{:S(2)}) collective-permute-start(bf16[3,80,640]{2,1,0:T(8,128)(2,1)S(1)} %select_bitcast_fusion), channel_id=1, source_target_pairs={{0,1},{1,0},{2,3},{3,2},{4,5},{5,4},{6,7},{7,6},{8,9},{9,8},{10,11... | collective-permute-start | bytes 921608 | tf_op jit(solution)/shard_map/ppermute | solution.py:476
  499.7 23.1 %collective-permute-start.28 = (f32[5200]{0:T(1024)S(1)}, f32[5200]{0:T(1024)S(1)}, u32[]{:S(2)}, u32[]{:S(2)}) collective-permute-start(f32[5200]{0:T(1024)S(1)} %constant_dynamic-update-slice_fusion), channel_id=1, source_target_pairs={{0,8},{8,0},{16,24},{24,16},{1,9},{9,1},{17,25},{25,17},{2,10},{10... | collective-permute-start | bytes 62408 | tf_op jit(solution)/shard_map/ppermute | solution.py:712
  501.4 21.6 %collective-permute-start.29 = (f32[5200]{0:T(1024)S(1)}, f32[5200]{0:T(1024)S(1)}, u32[]{:S(2)}, u32[]{:S(2)}) collective-permute-start(f32[5200]{0:T(1024)S(1)} %constant_dynamic-update-slice_fusion), channel_id=1, source_target_pairs={{0,16},{8,24},{16,0},{24,8},{1,17},{9,25},{17,1},{25,9},{2,18},{10... | collective-permute-start | bytes 62408 | tf_op jit(solution)/shard_map/ppermute | solution.py:712
  504.2 18.8 %collective-permute-start.30 = (f32[5200]{0:T(1024)S(1)}, f32[5200]{0:T(1024)S(1)}, u32[]{:S(2)}, u32[]{:S(2)}) collective-permute-start(f32[5200]{0:T(1024)S(1)} %constant_dynamic-update-slice_fusion), channel_id=1, source_target_pairs={{0,24},{8,16},{16,8},{24,0},{1,25},{9,17},{17,9},{25,1},{2,26},{10... | collective-permute-start | bytes 62408 | tf_op jit(solution)/shard_map/ppermute | solution.py:712
  504.7 18.2 %collective-permute-start.25 = (bf16[320,240]{1,0:T(8,128)(2,1)S(1)}, bf16[320,240]{1,0:T(8,128)(2,1)S(1)}, u32[]{:S(2)}, u32[]{:S(2)}) collective-permute-start(bf16[320,240]{1,0:T(8,128)(2,1)S(1)} %get-tuple-element.154), channel_id=1, source_target_pairs={{0,8},{8,0},{16,24},{24,16},{1,9},{9,1},{17,25},{25,17},{2,10},{10... | collective-permute-start | bytes 460808 | tf_op jit(solution)/shard_map/ppermute | solution.py:704
  505.5 17.5 %collective-permute-start.26 = (bf16[320,240]{1,0:T(8,128)(2,1)S(1)}, bf16[320,240]{1,0:T(8,128)(2,1)S(1)}, u32[]{:S(2)}, u32[]{:S(2)}) collective-permute-start(bf16[320,240]{1,0:T(8,128)(2,1)S(1)} %get-tuple-element.156), channel_id=1, source_target_pairs={{0,16},{8,24},{16,0},{24,8},{1,17},{9,25},{17,1},{25,9},{2,18},{10... | collective-permute-start | bytes 460808 | tf_op jit(solution)/shard_map/ppermute | solution.py:704
  522.8 7.3 %collective-permute-start.27 = (bf16[320,240]{1,0:T(8,128)(2,1)S(1)}, bf16[320,240]{1,0:T(8,128)(2,1)S(1)}, u32[]{:S(2)}, u32[]{:S(2)}) collective-permute-start(bf16[320,240]{1,0:T(8,128)(2,1)S(1)} %get-tuple-element.155), channel_id=1, source_target_pairs={{0,24},{8,16},{16,8},{24,0},{1,25},{9,17},{17,9},{25,1},{2,26},{10... | collective-permute-start | bytes 460808 | tf_op jit(solution)/shard_map/ppermute | solution.py:704
  530.4 4.8 collective-permute-start.31
  530.4 4.9 collective-permute-start.32
  532.0 3.3 collective-permute-start.33
  532.9 2.4 collective-permute-start.34
  533.4 4.6 collective-permute-start.35
  535.2 4.7 collective-permute-start.36
  540.5 3.9 collective-permute-start.37
  (33 other events, 284.9 us)
Sparse Core Ops, SparseCore 0:
  31.2 34.0 all-gather.8
  94.9 87.7 all-gather.4
  184.9 93.0 all-gather.6
  291.8 117.7 reduce-scatter.1

commit v3 on v2

--- a/solution.py
+++ b/solution.py
@@ -392,6 +392,53 @@
     )(back, w, *others)
 
 
+def head_grad_body(low_ref, w_ref, out_ref):
+    out_ref[...] = nn(low_ref[...], w_ref[0]).T.astype(bf16)
+
+
+def head_grad(low, whole, p, features):
+    rows, width = low.shape
+    block = math.gcd(rows, 256)
+    return pl.pallas_call(
+        head_grad_body,
+        grid=(rows // block,),
+        in_specs=[
+            pl.BlockSpec((block, width), lambda t: (t, 0)),
+            pl.BlockSpec((1, width, features), lambda t: (0, 0, p)),
+        ],
+        out_specs=pl.BlockSpec((features, block), lambda t: (0, t)),
+        out_shape=jax.ShapeDtypeStruct((features, rows), bf16),
+        compiler_params=pltpu.CompilerParams(vmem_limit_bytes=VMEM_BYTES),
+        cost_estimate=pl.CostEstimate(flops=1, bytes_accessed=1, transcendentals=0),
+        name="head_grad",
+    )(low, whole)
+
+
+def outputs_body(act_ref, w_ref, hidden_ref, bias_ref, out_ref):
+    out_ref[...] = (hidden_ref[...] + (nt(act_ref[...], w_ref[0]) + bias_ref[...])).astype(bf16)
+
+
+def down_outputs(act, whole, hidden, bias):
+    rows, width = hidden.shape
+    block = math.gcd(rows, 256)
+    by_tokens = lambda n: pl.BlockSpec((block, n), lambda t: (t, 0))
+    return pl.pallas_call(
+        outputs_body,
+        grid=(rows // block,),
+        in_specs=[
+            by_tokens(act.shape[1]),
+            pl.BlockSpec((1, width, act.shape[1]), lambda t: (2, 0, 0)),
+            by_tokens(width),
+            pl.BlockSpec((1, width), lambda t: (0, 0)),
+        ],
+        out_specs=by_tokens(width),
+        out_shape=jax.ShapeDtypeStruct((rows, width), bf16),
+        compiler_params=pltpu.CompilerParams(vmem_limit_bytes=VMEM_BYTES),
+        cost_estimate=pl.CostEstimate(flops=1, bytes_accessed=1, transcendentals=0),
+        name="outputs",
+    )(act, whole, hidden, bias[None])
+
+
 def tile_list(segments):
     length = segments.shape[0]
     n_q, n_k = length // BLOCK_Q, length // BLOCK_K
@@ -626,21 +673,20 @@
     pre_act = nn(normed_two, up_all) + b_up
     sigma = jax.nn.sigmoid(pre_act)
     activation = (pre_act * sigma).astype(bf16)
-    outputs = (hidden + (nt(activation, down_t) + b_down)).astype(bf16)
-
     top_low = cotangent[:, 0]
     grad_top = top_low.astype(f32)
     grad_pre = (nn(top_low, down_t) * (sigma * (1 + pre_act * (1 - sigma)))).astype(bf16)
     grad_normed_two = nt(grad_pre, up_all)
     grad_hidden = grad_top + norm_back(grad_normed_two, unit_two, inverse_two, gain_mlp)
     grad_hidden_low = grad_hidden.astype(bf16)
-    grad_heads = [
-        nt(out_t[:, p * part : (p + 1) * part].T, grad_hidden_low).astype(bf16).reshape(n_owners, HD, rows)
-        for p in range(own)
-    ]
-    grad_heads[0], low, act, normed, outputs = lax.optimization_barrier(
-        (grad_heads[0], grad_hidden_low, activation, normed_two, outputs)
+    grad_heads = [nt(out_t[:, :part].T, grad_hidden_low).astype(bf16)]
+    grad_heads += [head_grad(grad_hidden_low, whole, p, part) for p in range(1, own)]
+    grad_heads = [g.reshape(n_owners, HD, rows) for g in grad_heads]
+    grad_heads[0], low, act, normed = lax.optimization_barrier(
+        (grad_heads[0], grad_hidden_low, activation, normed_two)
     )
+    outputs = down_outputs(act, whole, hidden, b_down)
+    grad_heads[-1], outputs = lax.optimization_barrier((grad_heads[-1], outputs))
     grad_heads = [to_heads(g) for g in grad_heads]
     grad_out_t = [dot(low, m, (0,), (1,)) for m in mixed]
     grad_up = dot(normed, grad_pre, (0,), (0,))
@@ -655,10 +701,8 @@
     scale_tile = jnp.broadcast_to(scaling[:, None], (HD, 128))
     scale_sum = jnp.zeros((HD,), f32)
     gain_part = jnp.zeros((width,), f32)
-    backs, wgrads, travelled = [], [], []
+    dxs, backs, wgrads, travelled = [], [], [], []
     for p in range(own):
-        if p:
-            heads_x, grad_heads[p], wgrads[-1] = lax.optimization_barrier((heads_x, grad_heads[p], wgrads[-1]))
         dx, part_sum = attend_back(
             tiles, heads_x, grad_heads[p], wides[p], lses[p], seg_chunks, scale_tile, p
         )
@@ -666,9 +710,13 @@
             dx, backs[-1] = lax.optimization_barrier((dx, backs[-1]))
         scale_sum = scale_sum + jnp.sum(part_sum, axis=1)
         backs.append(to_tokens(dx).reshape(3 * part, rows))
+        dxs.append(dx)
+    dxs = lax.optimization_barrier(dxs)
+    for p, dx in enumerate(dxs):
         if p == own - 1:
             grad_normed_one = jnp.zeros((rows, width), f32)
             for n in range(own - 1):
+                backs[n], wgrads[n] = lax.optimization_barrier((backs[n], wgrads[n]))
                 grad_normed_one = grad_normed_one + input_grad(backs[n], qkv_all, n, ())
             dx, grad_normed_one = lax.optimization_barrier((dx, grad_normed_one))
         if spots is None:
@@ -691,12 +739,9 @@
             split_up, split_down = (
                 reduced[n].reshape(shard, n_tensor, columns).transpose(1, 0, 2) for n in (1, 2)
             )
-            mine = scatter_pair(
-                jnp.stack([split_out.reshape(n_tensor, shard, columns), split_up, split_down], axis=1)
-            )
-            out_grad, up_grad, down_grad = mine[0].T, mine[1], mine[2].T
-            wgrads[-1], gain_part, backs[-1], out_grad, up_grad, down_grad = lax.optimization_barrier(
-                (wgrads[-1], gain_part, backs[-1], out_grad, up_grad, down_grad)
+            halves_of = jnp.stack([split_out.reshape(n_tensor, shard, columns), split_up, split_down], axis=1)
+            wgrads[-1], gain_part, backs[-1], halves_of, travelled = lax.optimization_barrier(
+                (wgrads[-1], gain_part, backs[-1], halves_of, travelled)
             )
         rows_by = by_distance(wgrads[-1].reshape(n_dp, n_ctx * shard, 3 * HD), lax.axis_index("dp"))
         wgrads[-1] = rows_by[0]
@@ -707,36 +752,42 @@
     if not split:
         once = (ctx_rank == 0).astype(f32)
         gain_one, scale_sum = gain_one * once, scale_sum * once
-    def across(x, axis):
-        count = lax.axis_size(axis)
-        return [x] + [lax.ppermute(x, axis, [(i, i ^ k) for i in range(count)]) for k in range(1, count)]
+
+    def doubled(x, axis):
+        count, bit = lax.axis_size(axis), 1
+        while bit < count:
+            x = x + lax.ppermute(x, axis, [(i, i ^ bit) for i in range(count)])
+            bit *= 2
+        return x
 
     sums = jnp.concatenate([gain_one, gain_two, bias_up, bias_down, scale_sum])
     small = all(n & (n - 1) == 0 and n <= 4 for n in (n_dp, n_ctx, n_tensor))
     if small:
-        sums = sum(across(sums, "dp"))
+        sums = doubled(sums, "dp")
     piece = jnp.concatenate(
         [sum((g.astype(f32) for g in far), w.astype(f32)).astype(bf16) for w, far in zip(wgrads, travelled, strict=True)],
         axis=1,
     )
-    piece, sums = lax.optimization_barrier((piece, sums))
+    grad_inputs = input_grad(
+        backs[-1], qkv_all, own - 1, (grad_normed_one, tokens[:, 0], gain_attn[None], grad_hidden)
+    )
+    mine = scatter_pair(halves_of)
+    piece, sums, grad_inputs, mine = lax.optimization_barrier((piece, sums, grad_inputs, mine))
+    out_grad, up_grad, down_grad = mine[0].T, mine[1], mine[2].T
     piece = piece.reshape(n_ctx, shard, head_width)
     if split:
         piece = exchange(piece, "ctx", ctx_rank)
     else:
         piece = lax.dynamic_slice_in_dim(piece, ctx_rank, 1, 0)
     if small:
-        sums = sum(across(sums, "ctx"))
+        sums = doubled(sums, "ctx")
         sums, piece = lax.optimization_barrier((sums, piece))
-        sums = sum(across(sums, "tensor"))
+        sums = doubled(sums, "tensor")
     else:
         sums = lax.psum(sums, everyone)
     qkv_grad = piece.reshape(ctx_parts, shard, own, 3, HD).transpose(3, 1, 0, 2, 4)
     qkv_grad = qkv_grad.reshape(w_qkv.shape).astype(f32)
 
-    grad_inputs = input_grad(
-        backs[-1], qkv_all, own - 1, (grad_normed_one, tokens[:, 0], gain_attn[None], grad_hidden)
-    )
     gain_one, gain_two, bias_up, bias_down = (sums[n * width : (n + 1) * width] for n in range(4))
     grad_query_scale = sums[4 * width :] * (LOG_TWO_E / math.sqrt(HD)) * jax.nn.sigmoid(query_scale)
     return (

time: 557 us -> 532 us (0.955)
  waiting for transfers between devices: 100 us -> 62.3 us
  Pallas kernels: 243 us -> 258 us
  matrix products: 58.3 us -> 51.4 us
    pallas_call x0 -> x2, Pallas kernels: none -> 15.3 us  [the longest x1 9.33 us: down_outputs(): pl.pallas_call(outputs_body, grid=(rows // block,), in_specs=[by_tokens(a...]
    ppermute x6, waiting for transfers between devices: 15 us -> 0.02 us  [per_device(): lax.ppermute(rows_by[k], 'dp', [(i, i ^ k) for i in range(n_dp)])]
    ppermute x1, waiting for transfers between devices: 10.6 us -> 0.01 us  [scatter_pair(): lax.ppermute(send, 'tensor', [(0, 1), (1, 0)]).astype(f32)]
    all_to_all x2, waiting for transfers between devices: 11.3 us -> 1.85 us  [to_heads(): x = lax.all_to_all(x, owners, 0, 0)]
    dot_general x12 -> x10, matrix products: 58.3 us -> 51.4 us  [dot(): lax.dot_general(a, b, ((contract_a, contract_b), ((), ())), preferred_ele...]
  transfers between devices with their start and end apart: 48 -> 46, of which waited for: 18 -> 15; matrix products, arithmetic and copies ran while one was open for 22% -> 23% of each run, Pallas kernels for 44% -> 49%
where the time goes in v3:
time: 532 us; the launch traced here: 526 us
  Pallas kernels  258 us (48%)
  starting transfers between devices  63.7 us (12%)
  waiting for transfers between devices  62.3 us (12%)
  matrix products  51.4 us (10%)
  local copies, waits for them, and re-layouts  43.5 us (8%)
  other arithmetic  30.4 us (6%)
  between operations  15.9 us (3%)
    pallas_call x2, Pallas kernels, attend_back(): pl.pallas_call(functools.partial(attend_back_body, chunks=chunks, chunk=c...  102 us
    pallas_call x2, Pallas kernels, attend(): pl.pallas_call(functools.partial(attend_body, chunks=chunks, chunk=chunk)...  58.1 us
    dot_general x10, matrix products, dot(): lax.dot_general(a, b, ((contract_a, contract_b), ((), ())), preferred_ele...  51.4 us
    ppermute x14, waiting for transfers between devices, swap(): lax.ppermute(x, ('ctx', 'tensor'), [(i, i ^ bit) for i in range(group)])  39.3 us
    pallas_call x5, Pallas kernels, project_into(): pl.pallas_call(functools.partial(project_body, places=places), in_specs=[...  34 us
    pallas_call x2, Pallas kernels, weight_grad(): pl.pallas_call(functools.partial(weight_grad_body, spots=spots), in_specs...  25 us
    pallas_call x2, Pallas kernels, input_grad(): pl.pallas_call(finish_body if others else back_one_body, grid=(rows // bl...  24.1 us
    all_to_all x4, starting transfers between devices, to_tokens(): return lax.all_to_all(x, owners, 0, 0)  18.4 us
  transfers between devices with their start and end apart: 46, of which 15 were waited for; matrix products, arithmetic and copies ran while one was open for 23% of the time, Pallas kernels for 49%

profile of v3, /device:TPU:0, one launch (start us, length us, event | category | flops | bytes accessed | tf_op | source)
XLA Modules:
  0.0 525.5 jit_solution(2221870377064742643)
XLA Ops:
  7.2 3.0 collective-permute-start.3
  10.2 2.3 reshape.217
  54.6 2.3 pad_maximum_fusion.1
  57.0 2.5 copy.154
  63.2 2.0 all-gather.9.cloned.1.call-done
  65.3 2.5 copy.156
  67.7 5.7 %project.5 = (bf16[8,480,1024]{2,1,0:T(8,128)(2,1)}, f32[8,128]{1,0:T(8,128)}) custom-call(s32[2]{0:T(128)} %pad_add_fusion.1.slots_ref, bf16[480,1280]{1,0:T(8,128)(2,1)} %bitcast.202, f32[480,1]{1,0:T(8,128)} %broadcast_in_dim_tile.4.scale_ref, bf16[512,1280]{1,0:T(8,128)(2,1)} %get-tuple-element.81.refs_0_, bf16[512,1280]{1,0:T(8,128)(2,1)} %get-tuple-element.82.refs_1_), custom_call_target="tpu_custom_call" | custom-call | flops 1258291200 | bytes 5242880 | tf_op jit(solution)/shard_map/project/pallas_call | solution.py:290
  73.5 5.8 %project.6 = (bf16[8,480,1024]{2,1,0:T(8,128)(2,1)}, f32[8,128]{1,0:T(8,128)}) custom-call(s32[2]{0:T(128)} %pad_add_fusion.slots_ref, bf16[480,1280]{1,0:T(8,128)(2,1)} %bitcast.203, f32[480,1]{1,0:T(8,128)} %broadcast_in_dim_tile.4.scale_ref, bf16[512,1280]{1,0:T(8,128)(2,1)} %collective-permute-done.11.refs_0_.refs_2_, ...), custom_call_target="tpu_custom_call", output_to_operand_aliasing={{0}: (5, {})} | custom-call | flops 1258291200 | bytes 5242880 | tf_op jit(solution)/shard_map/project/pallas_call | solution.py:290
  79.3 13.8 %collective-permute-done.8.refs_1_.refs_5_ = bf16[512,1280]{1,0:T(8,128)(2,1)} collective-permute-done((bf16[512,1280]{1,0:T(8,128)(2,1)}, bf16[512,1280]{1,0:T(8,128)(2,1)}, u32[]{:S(2)}, u32[]{:S(2)}) %collective-permute-start.8) | collective-permute-done | bytes 1310752 | tf_op jit(solution)/shard_map/ppermute | solution.py:586
  100.9 7.5 %project.7 = (bf16[8,480,1024]{2,1,0:T(8,128)(2,1)}, f32[8,128]{1,0:T(8,128)}) custom-call(s32[4]{0:T(128)} %pad_add_fusion.4.slots_ref, bf16[480,1280]{1,0:T(8,128)(2,1)} %bitcast.204, f32[480,1]{1,0:T(8,128)} %broadcast_in_dim_tile.4.scale_ref, bf16[512,1280]{1,0:T(8,128)(2,1)} %collective-permute-done.7.refs_0_.refs_4_, ...), custom_call_target="tpu_custom_call", output_to_operand_aliasing={{0}: (7, {})} | custom-call | flops 2516582400 | bytes 10485760 | tf_op jit(solution)/shard_map/project/pallas_call | solution.py:290
  108.5 7.5 %project.8 = (bf16[8,480,1024]{2,1,0:T(8,128)(2,1)}, f32[8,128]{1,0:T(8,128)}) custom-call(s32[4]{0:T(128)} %pad_add_fusion.3.slots_ref, bf16[480,1280]{1,0:T(8,128)(2,1)} %bitcast.205, f32[480,1]{1,0:T(8,128)} %broadcast_in_dim_tile.4.scale_ref, bf16[512,1280]{1,0:T(8,128)(2,1)} %collective-permute-done.10.refs_0_.refs_8_, ...), custom_call_target="tpu_custom_call", output_to_operand_aliasing={{0}: (7, {})} | custom-call | flops 2516582400 | bytes 10485760 | tf_op jit(solution)/shard_map/project/pallas_call | solution.py:290
  116.0 17.6 %collective-permute-done.13.refs_0_.refs_12_ = bf16[512,1280]{1,0:T(8,128)(2,1)} collective-permute-done((bf16[512,1280]{1,0:T(8,128)(2,1)}, bf16[512,1280]{1,0:T(8,128)(2,1)}, u32[]{:S(2)}, u32[]{:S(2)}) %collective-permute-start.13) | collective-permute-done | bytes 1310752 | tf_op jit(solution)/shard_map/ppermute | solution.py:586
  137.0 3.7 collective-permute-done.20.refs_3_.refs_15_
  140.8 7.5 %project.9 = (bf16[8,480,1024]{2,1,0:T(8,128)(2,1)}, f32[8,128]{1,0:T(8,128)}) custom-call(s32[4]{0:T(128)} %pad_add_fusion.2.slots_ref, bf16[480,1280]{1,0:T(8,128)(2,1)} %bitcast.206, f32[480,1]{1,0:T(8,128)} %broadcast_in_dim_tile.4.scale_ref, bf16[512,1280]{1,0:T(8,128)(2,1)} %collective-permute-done.13.refs_0_.refs_12_, ...), custom_call_target="tpu_custom_call", output_to_operand_aliasing={{0}: (7, {})} | custom-call | flops 2516582400 | bytes 10485760 | tf_op jit(solution)/shard_map/project/pallas_call | solution.py:290
  148.2 29.0 %attend.2 = (bf16[8,80,1024]{2,1,0:T(8,128)(2,1)}, f32[8,80,1024]{2,1,0:T(8,128)}, f32[1,8,1024]{2,1,0:T(8,128)}) custom-call(s32[1]{0:T(128)} %bitcast.29.count, s32[258]{0:T(512)} %fusion.24.tiles, bf16[8,2,3,80,1024]{4,3,2,1,0:T(8,128)(2,1)} %bitcast.196, s32[1,8,1024]{2,1,0:T(8,128)} %bitcast.249), custom_call_target="tpu_custom_call" | custom-call | flops 17179869184 | bytes 16777216 | tf_op jit(solution)/shard_map/attend/pallas_call | solution.py:183
  177.3 4.8 all-to-all-start
  182.1 29.1 %attend.3 = (bf16[8,80,1024]{2,1,0:T(8,128)(2,1)}, f32[8,80,1024]{2,1,0:T(8,128)}, f32[1,8,1024]{2,1,0:T(8,128)}) custom-call(s32[1]{0:T(128)} %bitcast.29.count, s32[258]{0:T(512)} %fusion.24.tiles, bf16[8,2,3,80,1024]{4,3,2,1,0:T(8,128)(2,1)} %bitcast.197, s32[1,8,1024]{2,1,0:T(8,128)} %bitcast.250), custom_call_target="tpu_custom_call" | custom-call | flops 17179869184 | bytes 16777216 | tf_op jit(solution)/shard_map/attend/pallas_call | solution.py:183
  211.1 4.3 all-to-all-start.1
  215.5 2.1 slice_bitcast_fusion.3
  219.3 5.9 %fusion.12 = f32[1024,1280]{1,0:T(8,128)} fusion(bf16[640,1024]{1,0:T(8,128)(2,1)} %bitcast.41, bf16[1280,1280]{1,0:T(8,128)(2,1)S(1)} %slice_bitcast_fusion.3), kind=kOutput, calls=%fused_computation.34 | convolution fusion | flops 1677721600 | bytes 8192000 | tf_op jit(solution)/shard_map/dot_general | solution.py:27
  225.2 10.3 %all-to-all-done.1 = bf16[8,80,1024]{2,1,0:T(8,128)(2,1)} async-done(((bf16[8,80,1024]{2,1,0:T(8,128)(2,1)}), bf16[8,80,1024]{2,1,0:T(8,128)(2,1)}, u32[]{:S(2)}, u32[]{:S(2)}) %all-to-all-start.1) | async-done | bytes 1310752 | tf_op jit(solution)/shard_map/all_to_all | solution.py:646
  235.5 5.9 %multiply_reduce_fusion.2 = (f32[1024]{0:T(1024)S(1)}, f32[1024,1280]{1,0:T(8,128)S(1)}) fusion(bf16[640,1024]{1,0:T(8,128)(2,1)} %bitcast.43, bf16[1280,1280]{1,0:T(8,128)(2,1)} %copy-done.4, f32[1024,1280]{1,0:T(8,128)} %fusion.12, bf16[1024,1,1280]{2,0,1:T(8,128)(2,1)S(1)} %copy-done.2), kind=kOutput, calls=%fused_computation.21 | convolution fusion | flops 1684274176 | bytes 16060416 | tf_op jit(solution)/shard_map/dot_general | solution.py:27
  242.2 8.1 %multiply_convert_fusion = (bf16[1024,1280]{1,0:T(8,128)(2,1)S(1)}, f32[1024,1280]{1,0:T(8,128)S(1)}) fusion(f32[1280]{0:T(1024)S(1)} %copy-done.28, bf16[1024,1280]{1,0:T(8,128)(2,1)S(1)} %multiply_convert_fusion.1, bf16[3,1280,1280]{2,1,0:T(8,128)(2,1)} %all-gather.5.cloned.1.call-done.w_ref), kind=kOutput, calls=%fused_computation.17 | convolution fusion | flops 3363307520 | bytes 13767680 | tf_op jit(solution)/shard_map/dot_general | solution.py:27
  250.4 6.5 %convert_reduce_fusion.1 = (f32[1280]{0:T(1024)}, bf16[1024,1280]{1,0:T(8,128)(2,1)}) fusion(f32[1024,1280]{1,0:T(8,128)S(1)} %get-tuple-element.199, f32[1280]{0:T(1024)S(1)} %copy-done.28, bf16[3,1280,1280]{2,1,0:T(8,128)(2,1)S(1)} %bitcast.201, bf16[1024,1,1280]{2,0,1:T(8,128)(2,1)S(1)} %copy-done.6), kind=kOutput, calls=%fused_computation.15 | convolution fusion | flops 3371170560 | bytes 13775872 | tf_op jit(solution)/shard_map/dot_general | solution.py:27
  256.9 6.4 %multiply_reduce_fusion = (f32[1280]{0:T(1024)}, f32[1024]{0:T(1024)S(1)}, f32[1024,1280]{1,0:T(8,128)S(1)}) fusion(f32[1024,1280]{1,0:T(8,128)S(1)} %get-tuple-element.196.hidden_ref, f32[1024]{0:T(1024)S(1)} %add_rsqrt_fusion, f32[1280]{0:T(1024)S(1)} %copy-done.19, bf16[1024,1280]{1,0:T(8,128)(2,1)} %get-tuple-element.201, ...), kind=kOutput, calls=%fused_computation.16 | convolution fusion | flops 3363305216 | bytes 16405504 | tf_op jit(solution)/shard_map/dot_general | solution.py:27
  263.3 3.9 fusion.26
  267.2 3.0 convolution_convert_fusion.4
  270.2 3.7 convolution_convert_fusion.2
  273.9 3.6 convolution_convert_fusion.3
  277.5 4.5 fusion
  282.0 3.9 convolution_convert_fusion.1
  285.9 4.3 pad_maximum_fusion
  290.2 5.1 all-to-all-start.3
  295.9 6.0 %head_grad.1 = bf16[640,1024]{1,0:T(8,128)(2,1)} custom-call(bf16[1024,1280]{1,0:T(8,128)(2,1)} %copy-done.3, bf16[3,1280,1280]{2,1,0:T(8,128)(2,1)} %all-gather.5.cloned.1.call-done.w_ref), custom_call_target="tpu_custom_call" | custom-call | flops 1 | bytes 1 | tf_op jit(solution)/shard_map/head_grad/pallas_call | solution.py:402
  301.8 9.3 %outputs.1 = bf16[1024,1280]{1,0:T(8,128)(2,1)} custom-call(bf16[1024,1280]{1,0:T(8,128)(2,1)} %copy-done.7, bf16[3,1280,1280]{2,1,0:T(8,128)(2,1)} %all-gather.5.cloned.1.call-done.w_ref, f32[1024,1280]{1,0:T(8,128)} %copy-done, f32[1,1280]{1,0:T(1,128)} %broadcast_in_dim.66.bias_ref), custom_call_target="tpu_custom_call" | custom-call | flops 1 | bytes 1 | tf_op jit(solution)/shard_map/outputs/pallas_call | solution.py:425
  313.0 3.6 all-to-all-start.2
  317.3 50.9 %attend_back.3 = (bf16[8,3,80,1024]{3,2,1,0:T(8,128)(2,1)}, f32[80,128]{1,0:T(8,128)}) custom-call(s32[1]{0:T(128)} %bitcast.29.count, s32[258]{0:T(512)} %fusion.24.tiles, bf16[8,2,3,80,1024]{4,3,2,1,0:T(8,128)(2,1)} %bitcast.198, bf16[8,80,1024]{2,1,0:T(8,128)(2,1)} %copy-done.9, f32[8,80,1024]{2,1,0:T(8,128)} %get-tuple-element.116.wide_ref, ...), custom_call_target="tpu_custom_call" | custom-call | flops 42949672960 | bytes 16777216 | tf_op jit(solution)/shard_map/attend_back/pallas_call | solution.py:220
  369.4 4.7 all-to-all-start.4
  374.1 51.1 %attend_back.2 = (bf16[8,3,80,1024]{3,2,1,0:T(8,128)(2,1)}, f32[80,128]{1,0:T(8,128)}) custom-call(s32[1]{0:T(128)} %bitcast.29.count, s32[258]{0:T(512)} %fusion.24.tiles, bf16[8,2,3,80,1024]{4,3,2,1,0:T(8,128)(2,1)} %bitcast.199, bf16[8,80,1024]{2,1,0:T(8,128)(2,1)} %copy-done.8, f32[8,80,1024]{2,1,0:T(8,128)} %get-tuple-element.112.wide_ref, ...), custom_call_target="tpu_custom_call" | custom-call | flops 42949672960 | bytes 16777216 | tf_op jit(solution)/shard_map/attend_back/pallas_call | solution.py:220
  426.1 4.7 all-to-all-start.5
  432.7 12.5 %weight_grad.2 = (bf16[240,1280]{1,0:T(8,128)(2,1)}, f32[1,1280]{1,0:T(1,128)}) custom-call(s32[1]{0:T(128)} %bitcast.33.me_ref, bf16[512,1280]{1,0:T(8,128)(2,1)} %get-tuple-element.81.refs_0_, bf16[512,1280]{1,0:T(8,128)(2,1)} %get-tuple-element.82.refs_1_, bf16[512,1280]{1,0:T(8,128)(2,1)} %collective-permute-done.11.refs_0_.refs_2_, ...), custom_call_target="tpu_custom_call" | custom-call | flops 1 | bytes 1 | tf_op jit(solution)/shard_map/weight_grad/pallas_call | solution.py:335
  446.9 10.6 %input_grad.2.other_ref = f32[1024,1280]{1,0:T(8,128)} custom-call(bf16[1920,1024]{1,0:T(8,128)(2,1)} %bitcast.50.back_ref, bf16[1280,3840]{1,0:T(8,128)(2,1)} %all-gather.7.cloned.1.call-done.w_ref), custom_call_target="tpu_custom_call" | custom-call | flops 1 | bytes 1 | tf_op jit(solution)/shard_map/input_grad/pallas_call | solution.py:375
  457.6 4.6 collective-permute-start.22
  462.1 12.4 %weight_grad.3 = (bf16[240,1280]{1,0:T(8,128)(2,1)}, f32[1,1280]{1,0:T(1,128)}) custom-call(s32[1]{0:T(128)} %bitcast.33.me_ref, bf16[512,1280]{1,0:T(8,128)(2,1)} %get-tuple-element.81.refs_0_, bf16[512,1280]{1,0:T(8,128)(2,1)} %get-tuple-element.82.refs_1_, bf16[512,1280]{1,0:T(8,128)(2,1)} %collective-permute-done.11.refs_0_.refs_2_, ...), custom_call_target="tpu_custom_call" | custom-call | flops 1 | bytes 1 | tf_op jit(solution)/shard_map/weight_grad/pallas_call | solution.py:335
  478.4 3.9 collective-permute-start.26
  486.4 13.5 %input_grad.3 = bf16[1024,1280]{1,0:T(8,128)(2,1)} custom-call(bf16[1920,1024]{1,0:T(8,128)(2,1)} %bitcast.58.back_ref, bf16[1280,3840]{1,0:T(8,128)(2,1)} %all-gather.7.cloned.1.call-done.w_ref, f32[1024,1280]{1,0:T(8,128)} %input_grad.2.other_ref, bf16[1024,1280]{1,0:T(8,128)(2,1)} %bitcast.208, f32[1,1280]{1,0:T(1,128)} %broadcast_in_dim.69.gain_ref, ...), custom_call_target="tpu_custom_call" | custom-call | flops 5033164800 | bytes 20971520 | tf_op jit(solution)/shard_map/input_grad/pallas_call | solution.py:375
  499.9 3.0 collective-permute-start.28
  515.0 2.1 reshape.244
  (264 shorter events, 88.7 us)
Async XLA Ops:
  7.2 58.1 %all-gather.9.cloned.1.call-start = ((), (), s32[]{:S(2)}) async-start(), calls=%async_computation.10 | async-start | bytes 1638400 | tf_op jit(solution)/shard_map/all_gather | solution.py:552
  7.2 21.0 %collective-permute-start.3 = (bf16[3,80,640]{2,1,0:T(8,128)(2,1)}, bf16[3,80,640]{2,1,0:T(8,128)(2,1)}, u32[]{:S(2)}, u32[]{:S(2)}) collective-permute-start(bf16[3,80,640]{2,1,0:T(8,128)(2,1)} %param.16), channel_id=1, source_target_pairs={{0,1},{1,0},{2,3},{3,2},{4,5},{5,4},{6,7},{7,6},{8,9},{9,8},{10,11... | collective-permute-start | bytes 921608 | tf_op jit(solution)/shard_map/ppermute | solution.py:510
  14.3 6.5 %collective-permute-start.2 = (bf16[80,480]{1,0:T(8,128)(2,1)S(1)}, bf16[80,480]{1,0:T(8,128)(2,1)S(1)}, u32[]{:S(2)}, u32[]{:S(2)}) collective-permute-start(bf16[80,480]{1,0:T(8,128)(2,1)S(1)} %bitcast.242), channel_id=1, source_target_pairs={{0,6},{2,4},{4,2},{6,0},{1,7},{3,5},{5,3},{7,1},{8,14},{10,12},{12... | collective-permute-start | bytes 230408 | tf_op jit(solution)/shard_map/ppermute | solution.py:539
  15.2 7.3 %collective-permute-start.1 = (bf16[80,480]{1,0:T(8,128)(2,1)S(1)}, bf16[80,480]{1,0:T(8,128)(2,1)S(1)}, u32[]{:S(2)}, u32[]{:S(2)}) collective-permute-start(bf16[80,480]{1,0:T(8,128)(2,1)S(1)} %bitcast.241), channel_id=1, source_target_pairs={{0,4},{2,6},{4,0},{6,2},{1,5},{3,7},{5,1},{7,3},{8,12},{10,14},{12... | collective-permute-start | bytes 230408 | tf_op jit(solution)/shard_map/ppermute | solution.py:539
  16.2 6.7 %collective-permute-start = (bf16[80,480]{1,0:T(8,128)(2,1)S(1)}, bf16[80,480]{1,0:T(8,128)(2,1)S(1)}, u32[]{:S(2)}, u32[]{:S(2)}) collective-permute-start(bf16[80,480]{1,0:T(8,128)(2,1)S(1)} %bitcast.240), channel_id=1, source_target_pairs={{0,2},{2,0},{4,6},{6,4},{1,3},{3,1},{5,7},{7,5},{8,10},{10,8},{12,... | collective-permute-start | bytes 230408 | tf_op jit(solution)/shard_map/ppermute | solution.py:539
  16.6 8.4 %collective-permute-start.4 = (bf16[640,80]{0,1:T(8,128)(2,1)}, bf16[640,80]{0,1:T(8,128)(2,1)}, u32[]{:S(2)}, u32[]{:S(2)}) collective-permute-start(bf16[640,80]{0,1:T(8,128)(2,1)} %param.17), channel_id=1, source_target_pairs={{0,1},{1,0},{2,3},{3,2},{4,5},{5,4},{6,7},{7,6},{8,9},{9,8},{10,11... | collective-permute-start | bytes 307208 | tf_op jit(solution)/shard_map/ppermute | solution.py:510
  20.8 6.1 %collective-permute-start.5 = (bf16[80,640]{1,0:T(8,128)(2,1)}, bf16[80,640]{1,0:T(8,128)(2,1)}, u32[]{:S(2)}, u32[]{:S(2)}) collective-permute-start(bf16[80,640]{1,0:T(8,128)(2,1)} %param.19), channel_id=1, source_target_pairs={{0,1},{1,0},{2,3},{3,2},{4,5},{5,4},{6,7},{7,6},{8,9},{9,8},{10,11... | collective-permute-start | bytes 307208 | tf_op jit(solution)/shard_map/ppermute | solution.py:510
  22.5 5.8 %collective-permute-start.6 = (bf16[640,80]{0,1:T(8,128)(2,1)}, bf16[640,80]{0,1:T(8,128)(2,1)}, u32[]{:S(2)}, u32[]{:S(2)}) collective-permute-start(bf16[640,80]{0,1:T(8,128)(2,1)} %param.21), channel_id=1, source_target_pairs={{0,1},{1,0},{2,3},{3,2},{4,5},{5,4},{6,7},{7,6},{8,9},{9,8},{10,11... | collective-permute-start | bytes 307208 | tf_op jit(solution)/shard_map/ppermute | solution.py:510
  28.3 11.7 %collective-permute-start.11 = (bf16[512,1280]{1,0:T(8,128)(2,1)}, bf16[512,1280]{1,0:T(8,128)(2,1)}, u32[]{:S(2)}, u32[]{:S(2)}) collective-permute-start(bf16[512,1280]{1,0:T(8,128)(2,1)} %get-tuple-element.81.refs_0_), channel_id=1, source_target_pairs={{0,2},{1,3},{2,0},{3,1},{4,6},{5,7},{6,4},{7,5},{8,10},{9,11},{10,... | collective-permute-start | bytes 3932168 | tf_op jit(solution)/shard_map/ppermute | solution.py:586
  31.2 184.2 %all-gather.5.cloned.1.call-start = ((), (), s32[]{:S(2)}) async-start(), calls=%async_computation.7 | async-start | bytes 10444800 | tf_op jit(solution)/shard_map/all_gather | solution.py:622
  33.5 45.7 %collective-permute-start.7 = (bf16[512,1280]{1,0:T(8,128)(2,1)}, bf16[512,1280]{1,0:T(8,128)(2,1)}, u32[]{:S(2)}, u32[]{:S(2)}) collective-permute-start(bf16[512,1280]{1,0:T(8,128)(2,1)} %get-tuple-element.81.refs_0_), channel_id=1, source_target_pairs={{0,1},{1,0},{2,3},{3,2},{4,5},{5,4},{6,7},{7,6},{8,9},{9,8},{10,11... | collective-permute-start | bytes 3932168 | tf_op jit(solution)/shard_map/ppermute | solution.py:586
  34.9 58.2 %collective-permute-start.8 = (bf16[512,1280]{1,0:T(8,128)(2,1)}, bf16[512,1280]{1,0:T(8,128)(2,1)}, u32[]{:S(2)}, u32[]{:S(2)}) collective-permute-start(bf16[512,1280]{1,0:T(8,128)(2,1)} %get-tuple-element.82.refs_1_), channel_id=1, source_target_pairs={{0,1},{1,0},{2,3},{3,2},{4,5},{5,4},{6,7},{7,6},{8,9},{9,8},{10,11... | collective-permute-start | bytes 3932168 | tf_op jit(solution)/shard_map/ppermute | solution.py:586
  35.6 57.6 %collective-permute-start.9 = (bf16[512,1280]{1,0:T(8,128)(2,1)}, bf16[512,1280]{1,0:T(8,128)(2,1)}, u32[]{:S(2)}, u32[]{:S(2)}) collective-permute-start(bf16[512,1280]{1,0:T(8,128)(2,1)} %get-tuple-element.82.refs_1_), channel_id=1, source_target_pairs={{0,4},{1,5},{2,6},{3,7},{4,0},{5,1},{6,2},{7,3},{8,12},{9,13},{10,... | collective-permute-start | bytes 3932168 | tf_op jit(solution)/shard_map/ppermute | solution.py:586
  37.0 36.5 %collective-permute-start.12 = (bf16[512,1280]{1,0:T(8,128)(2,1)}, bf16[512,1280]{1,0:T(8,128)(2,1)}, u32[]{:S(2)}, u32[]{:S(2)}) collective-permute-start(bf16[512,1280]{1,0:T(8,128)(2,1)} %get-tuple-element.82.refs_1_), channel_id=1, source_target_pairs={{0,2},{1,3},{2,0},{3,1},{4,6},{5,7},{6,4},{7,5},{8,10},{9,11},{10,... | collective-permute-start | bytes 3932168 | tf_op jit(solution)/shard_map/ppermute | solution.py:586
  39.9 54.7 %collective-permute-start.10 = (bf16[512,1280]{1,0:T(8,128)(2,1)}, bf16[512,1280]{1,0:T(8,128)(2,1)}, u32[]{:S(2)}, u32[]{:S(2)}) collective-permute-start(bf16[512,1280]{1,0:T(8,128)(2,1)} %get-tuple-element.81.refs_0_), channel_id=1, source_target_pairs={{0,4},{1,5},{2,6},{3,7},{4,0},{5,1},{6,2},{7,3},{8,12},{9,13},{10,... | collective-permute-start | bytes 3932168 | tf_op jit(solution)/shard_map/ppermute | solution.py:586
  94.6 195.6 %all-gather.7.cloned.1.call-start = ((), (), s32[]{:S(2)}) async-start(), calls=%async_computation.8 | async-start | bytes 10444800 | tf_op jit(solution)/shard_map/all_gather | solution.py:624
  94.9 3.4 collective-permute-start.17
  95.0 6.0 %collective-permute-start.18 = (bf16[512,1280]{1,0:T(8,128)(2,1)}, bf16[512,1280]{1,0:T(8,128)(2,1)}, u32[]{:S(2)}, u32[]{:S(2)}) collective-permute-start(bf16[512,1280]{1,0:T(8,128)(2,1)} %collective-permute-done.8.refs_1_.refs_5_), channel_id=1, source_target_pairs={{0,2},{1,3},{2,0},{3,1},{4,6},{5,7},{6,4},{7,5},{8,10},{9,11},{10,... | collective-permute-start | bytes 3932168 | tf_op jit(solution)/shard_map/ppermute | solution.py:586
  95.5 13.0 %collective-permute-start.15 = (bf16[512,1280]{1,0:T(8,128)(2,1)}, bf16[512,1280]{1,0:T(8,128)(2,1)}, u32[]{:S(2)}, u32[]{:S(2)}) collective-permute-start(bf16[512,1280]{1,0:T(8,128)(2,1)} %collective-permute-done.10.refs_0_.refs_8_), channel_id=1, source_target_pairs={{0,2},{1,3},{2,0},{3,1},{4,6},{5,7},{6,4},{7,5},{8,10},{9,11},{10,... | collective-permute-start | bytes 3932168 | tf_op jit(solution)/shard_map/ppermute | solution.py:586
  95.5 13.0 %collective-permute-start.16 = (bf16[512,1280]{1,0:T(8,128)(2,1)}, bf16[512,1280]{1,0:T(8,128)(2,1)}, u32[]{:S(2)}, u32[]{:S(2)}) collective-permute-start(bf16[512,1280]{1,0:T(8,128)(2,1)} %collective-permute-done.9.refs_1_.refs_9_), channel_id=1, source_target_pairs={{0,2},{1,3},{2,0},{3,1},{4,6},{5,7},{6,4},{7,5},{8,10},{9,11},{10,... | collective-permute-start | bytes 3932168 | tf_op jit(solution)/shard_map/ppermute | solution.py:586
  96.0 37.7 %collective-permute-start.13 = (bf16[512,1280]{1,0:T(8,128)(2,1)}, bf16[512,1280]{1,0:T(8,128)(2,1)}, u32[]{:S(2)}, u32[]{:S(2)}) collective-permute-start(bf16[512,1280]{1,0:T(8,128)(2,1)} %collective-permute-done.7.refs_0_.refs_4_), channel_id=1, source_target_pairs={{0,4},{1,5},{2,6},{3,7},{4,0},{5,1},{6,2},{7,3},{8,12},{9,13},{10,... | collective-permute-start | bytes 3932168 | tf_op jit(solution)/shard_map/ppermute | solution.py:586
  98.3 35.3 %collective-permute-start.14 = (bf16[512,1280]{1,0:T(8,128)(2,1)}, bf16[512,1280]{1,0:T(8,128)(2,1)}, u32[]{:S(2)}, u32[]{:S(2)}) collective-permute-start(bf16[512,1280]{1,0:T(8,128)(2,1)} %collective-permute-done.9.refs_1_.refs_9_), channel_id=1, source_target_pairs={{0,1},{1,0},{2,3},{3,2},{4,5},{5,4},{6,7},{7,6},{8,9},{9,8},{10,11... | collective-permute-start | bytes 3932168 | tf_op jit(solution)/shard_map/ppermute | solution.py:586
  133.6 3.4 collective-permute-start.19
  133.6 7.1 %collective-permute-start.20 = (bf16[512,1280]{1,0:T(8,128)(2,1)}, bf16[512,1280]{1,0:T(8,128)(2,1)}, u32[]{:S(2)}, u32[]{:S(2)}) collective-permute-start(bf16[512,1280]{1,0:T(8,128)(2,1)} %collective-permute-done.14.refs_1_.refs_13_), channel_id=1, source_target_pairs={{0,2},{1,3},{2,0},{3,1},{4,6},{5,7},{6,4},{7,5},{8,10},{9,11},{10,... | collective-permute-start | bytes 3932168 | tf_op jit(solution)/shard_map/ppermute | solution.py:586
  177.3 33.8 %all-to-all-start = ((bf16[8,80,1024]{2,1,0:T(8,128)(2,1)}), bf16[8,80,1024]{2,1,0:T(8,128)(2,1)}, u32[]{:S(2)}, u32[]{:S(2)}) async-start(bf16[8,80,1024]{2,1,0:T(8,128)(2,1)} %get-tuple-element.106), calls=%async_computation | async-start | bytes 2621440 | tf_op jit(solution)/shard_map/all_to_all | solution.py:646
  211.1 24.4 %all-to-all-start.1 = ((bf16[8,80,1024]{2,1,0:T(8,128)(2,1)}), bf16[8,80,1024]{2,1,0:T(8,128)(2,1)}, u32[]{:S(2)}, u32[]{:S(2)}) async-start(bf16[8,80,1024]{2,1,0:T(8,128)(2,1)} %get-tuple-element.108), calls=%async_computation.1 | async-start | bytes 2621440 | tf_op jit(solution)/shard_map/all_to_all | solution.py:646
  215.4 260.0 %reduce-scatter.2.cloned.1.call-start = ((), (), s32[]{:S(2)}) async-start(), calls=%async_computation.9 | async-start | bytes 10444800 | tf_op jit(solution)/shard_map/reduce_scatter | solution.py:696
  241.5 21.8 %copy-start = (f32[1024,1280]{1,0:T(8,128)}, f32[1024,1280]{1,0:T(8,128)S(1)}, u32[]{:S(2)}) copy-start(f32[1024,1280]{1,0:T(8,128)S(1)} %get-tuple-element.196.hidden_ref) | copy-start | bytes 15728644
  250.3 27.1 %copy-start.7 = (bf16[1024,1280]{1,0:T(8,128)(2,1)}, bf16[1024,1280]{1,0:T(8,128)(2,1)S(1)}, u32[]{:S(2)}) copy-start(bf16[1024,1280]{1,0:T(8,128)(2,1)S(1)} %get-tuple-element.109.act_ref) | copy-start | bytes 7864324
  290.2 22.8 %all-to-all-start.3 = ((bf16[8,80,1024]{2,1,0:T(8,128)(2,1)}), bf16[8,80,1024]{2,1,0:T(8,128)(2,1)S(1)}, u32[]{:S(2)}, u32[]{:S(2)}) async-start(bf16[8,80,1024]{2,1,0:T(8,128)(2,1)} %bitcast.48), calls=%async_computation.3 | async-start | bytes 2621440 | tf_op jit(solution)/shard_map/all_to_all | solution.py:649
  313.0 55.2 %all-to-all-start.2 = ((bf16[8,80,1024]{2,1,0:T(8,128)(2,1)}), bf16[8,80,1024]{2,1,0:T(8,128)(2,1)S(1)}, u32[]{:S(2)}, u32[]{:S(2)}) async-start(bf16[8,80,1024]{2,1,0:T(8,128)(2,1)} %bitcast.47), calls=%async_computation.2 | async-start | bytes 2621440 | tf_op jit(solution)/shard_map/all_to_all | solution.py:649
  369.4 56.7 %all-to-all-start.4 = ((bf16[8,3,80,1024]{3,2,1,0:T(8,128)(2,1)}), bf16[8,3,80,1024]{3,2,1,0:T(8,128)(2,1)}, u32[]{:S(2)}, u32[]{:S(2)}) async-start(bf16[8,3,80,1024]{3,2,1,0:T(8,128)(2,1)} %get-tuple-element.121.refs_17_), calls=%async_computation.4 | async-start | bytes 7864320 | tf_op jit(solution)/shard_map/all_to_all | solution.py:646
  426.1 51.7 %all-to-all-start.5 = ((bf16[8,3,80,1024]{3,2,1,0:T(8,128)(2,1)}), bf16[8,3,80,1024]{3,2,1,0:T(8,128)(2,1)}, u32[]{:S(2)}, u32[]{:S(2)}) async-start(bf16[8,3,80,1024]{3,2,1,0:T(8,128)(2,1)} %get-tuple-element.130.refs_17_), calls=%async_computation.5 | async-start | bytes 7864320 | tf_op jit(solution)/shard_map/all_to_all | solution.py:646
  457.5 20.3 %collective-permute-start.21 = (bf16[320,240]{1,0:T(8,128)(2,1)S(1)}, bf16[320,240]{1,0:T(8,128)(2,1)S(1)}, u32[]{:S(2)}, u32[]{:S(2)}) collective-permute-start(bf16[320,240]{1,0:T(8,128)(2,1)S(1)} %get-tuple-element.165), channel_id=1, source_target_pairs={{0,8},{8,0},{16,24},{24,16},{1,9},{9,1},{17,25},{25,17},{2,10},{10... | collective-permute-start | bytes 460808 | tf_op jit(solution)/shard_map/ppermute | solution.py:749
  457.6 20.2 %collective-permute-start.22 = (bf16[320,240]{1,0:T(8,128)(2,1)S(1)}, bf16[320,240]{1,0:T(8,128)(2,1)S(1)}, u32[]{:S(2)}, u32[]{:S(2)}) collective-permute-start(bf16[320,240]{1,0:T(8,128)(2,1)S(1)} %get-tuple-element.164), channel_id=1, source_target_pairs={{0,16},{8,24},{16,0},{24,8},{1,17},{9,25},{17,1},{25,9},{2,18},{10... | collective-permute-start | bytes 460808 | tf_op jit(solution)/shard_map/ppermute | solution.py:749
  462.1 15.7 %collective-permute-start.23 = (bf16[320,240]{1,0:T(8,128)(2,1)S(1)}, bf16[320,240]{1,0:T(8,128)(2,1)S(1)}, u32[]{:S(2)}, u32[]{:S(2)}) collective-permute-start(bf16[320,240]{1,0:T(8,128)(2,1)S(1)} %get-tuple-element.163), channel_id=1, source_target_pairs={{0,24},{8,16},{16,8},{24,0},{1,25},{9,17},{17,9},{25,1},{2,26},{10... | collective-permute-start | bytes 460808 | tf_op jit(solution)/shard_map/ppermute | solution.py:749
  478.4 26.6 %collective-permute-start.26 = (bf16[320,240]{1,0:T(8,128)(2,1)S(1)}, bf16[320,240]{1,0:T(8,128)(2,1)S(1)}, u32[]{:S(2)}, u32[]{:S(2)}) collective-permute-start(bf16[320,240]{1,0:T(8,128)(2,1)S(1)} %get-tuple-element.161), channel_id=1, source_target_pairs={{0,24},{8,16},{16,8},{24,0},{1,25},{9,17},{17,9},{25,1},{2,26},{10... | collective-permute-start | bytes 460808 | tf_op jit(solution)/shard_map/ppermute | solution.py:749
  482.3 22.7 %collective-permute-start.25 = (bf16[320,240]{1,0:T(8,128)(2,1)S(1)}, bf16[320,240]{1,0:T(8,128)(2,1)S(1)}, u32[]{:S(2)}, u32[]{:S(2)}) collective-permute-start(bf16[320,240]{1,0:T(8,128)(2,1)S(1)} %get-tuple-element.162), channel_id=1, source_target_pairs={{0,16},{8,24},{16,0},{24,8},{1,17},{9,25},{17,1},{25,9},{2,18},{10... | collective-permute-start | bytes 460808 | tf_op jit(solution)/shard_map/ppermute | solution.py:749
  482.3 22.7 %collective-permute-start.24 = (bf16[320,240]{1,0:T(8,128)(2,1)S(1)}, bf16[320,240]{1,0:T(8,128)(2,1)S(1)}, u32[]{:S(2)}, u32[]{:S(2)}) collective-permute-start(bf16[320,240]{1,0:T(8,128)(2,1)S(1)} %get-tuple-element.160), channel_id=1, source_target_pairs={{0,8},{8,0},{16,24},{24,16},{1,9},{9,1},{17,25},{25,17},{2,10},{10... | collective-permute-start | bytes 460808 | tf_op jit(solution)/shard_map/ppermute | solution.py:749
  483.0 16.9 %collective-permute-start.27 = (f32[5200]{0:T(1024)S(1)}, f32[5200]{0:T(1024)S(1)}, u32[]{:S(2)}, u32[]{:S(2)}) collective-permute-start(f32[5200]{0:T(1024)S(1)} %constant_dynamic-update-slice_fusion), channel_id=1, source_target_pairs={{0,8},{8,0},{16,24},{24,16},{1,9},{9,1},{17,25},{25,17},{2,10},{10... | collective-permute-start | bytes 62408 | tf_op jit(solution)/shard_map/ppermute | solution.py:759
  484.5 20.7 %collective-permute-start.29 = (bf16[3,80,640]{2,1,0:T(8,128)(2,1)S(1)}, bf16[3,80,640]{2,1,0:T(8,128)(2,1)S(1)}, u32[]{:S(2)}, u32[]{:S(2)}) collective-permute-start(bf16[3,80,640]{2,1,0:T(8,128)(2,1)S(1)} %select_bitcast_fusion), channel_id=1, source_target_pairs={{0,1},{1,0},{2,3},{3,2},{4,5},{5,4},{6,7},{7,6},{8,9},{9,8},{10,11... | collective-permute-start | bytes 921608 | tf_op jit(solution)/shard_map/ppermute | solution.py:523
  499.9 5.1 collective-permute-start.28
  505.4 3.3 collective-permute-start.30
  506.1 7.1 %collective-permute-start.34 = (bf16[80,480]{1,0:T(8,128)(2,1)S(1)}, bf16[80,480]{1,0:T(8,128)(2,1)S(1)}, u32[]{:S(2)}, u32[]{:S(2)}) collective-permute-start(bf16[80,480]{1,0:T(8,128)(2,1)S(1)} %bitcast.245), channel_id=1, source_target_pairs={{0,6},{2,4},{4,2},{6,0},{1,7},{3,5},{5,3},{7,1},{8,14},{10,12},{12... | collective-permute-start | bytes 230408 | tf_op jit(solution)/shard_map/ppermute | solution.py:539
  507.8 5.3 %collective-permute-start.33 = (bf16[80,480]{1,0:T(8,128)(2,1)S(1)}, bf16[80,480]{1,0:T(8,128)(2,1)S(1)}, u32[]{:S(2)}, u32[]{:S(2)}) collective-permute-start(bf16[80,480]{1,0:T(8,128)(2,1)S(1)} %bitcast.246), channel_id=1, source_target_pairs={{0,4},{2,6},{4,0},{6,2},{1,5},{3,7},{5,1},{7,3},{8,12},{10,14},{12... | collective-permute-start | bytes 230408 | tf_op jit(solution)/shard_map/ppermute | solution.py:539
  508.5 4.6 collective-permute-start.32
  508.6 4.5 collective-permute-start.31
  513.7 3.9 collective-permute-start.35
  (31 other events, 188.5 us)
Sparse Core Ops, SparseCore 0:
  31.3 33.8 all-gather.8
  94.7 88.2 all-gather.4
  185.4 92.7 all-gather.6
  290.3 143.2 reduce-scatter.1

commit v4 on v3

--- a/solution.py
+++ b/solution.py
@@ -414,6 +414,54 @@
     )(low, whole)
 
 
+def grad_act_body(top_ref, w_ref, out_ref):
+    out_ref[...] = nn(top_ref[...], w_ref[0])
+
+
+def grad_act_of(top, whole):
+    rows, width = top.shape
+    units = whole.shape[2]
+    block = math.gcd(rows, 256)
+    return pl.pallas_call(
+        grad_act_body,
+        grid=(rows // block,),
+        in_specs=[
+            pl.BlockSpec((block, width), lambda t: (t, 0)),
+            pl.BlockSpec((1, width, units), lambda t: (2, 0, 0)),
+        ],
+        out_specs=pl.BlockSpec((block, units), lambda t: (t, 0)),
+        out_shape=jax.ShapeDtypeStruct((rows, units), f32),
+        compiler_params=pltpu.CompilerParams(vmem_limit_bytes=VMEM_BYTES),
+        cost_estimate=pl.CostEstimate(flops=1, bytes_accessed=1, transcendentals=0),
+        name="grad_act",
+    )(top, whole)
+
+
+def first_out_body(mixed_ref, w_ref, tokens_ref, out_ref):
+    out_ref[...] = tokens_ref[...].astype(f32) + nn(w_ref[0], mixed_ref[...]).T
+
+
+def first_out(mixed, whole, tokens):
+    features, rows = mixed.shape
+    width = tokens.shape[1]
+    block = math.gcd(rows, 256)
+    by_tokens = pl.BlockSpec((block, width), lambda t: (t, 0))
+    return pl.pallas_call(
+        first_out_body,
+        grid=(rows // block,),
+        in_specs=[
+            pl.BlockSpec((features, block), lambda t: (0, t)),
+            pl.BlockSpec((1, width, features), lambda t: (0, 0, 0)),
+            by_tokens,
+        ],
+        out_specs=by_tokens,
+        out_shape=jax.ShapeDtypeStruct((rows, width), f32),
+        compiler_params=pltpu.CompilerParams(vmem_limit_bytes=VMEM_BYTES),
+        cost_estimate=pl.CostEstimate(flops=1, bytes_accessed=1, transcendentals=0),
+        name="first_out",
+    )(mixed, whole, tokens)
+
+
 def outputs_body(act_ref, w_ref, hidden_ref, bias_ref, out_ref):
     out_ref[...] = (hidden_ref[...] + (nt(act_ref[...], w_ref[0]) + bias_ref[...])).astype(bf16)
 
@@ -662,10 +710,16 @@
         o, wide, lse = attend(tiles, heads_x, seg_chunks, p)
         wides.append(wide)
         lses.append(lse)
+        if p == own - 1:
+            o, top_low = lax.optimization_barrier((o, cotangent[:, 0]))
         mixed.append(to_tokens(o).reshape(part, rows))
-
+    grad_act = grad_act_of(top_low, whole)
     hidden = inputs
-    for p in range(own):
+    if own > 1:
+        hidden = first_out(mixed[0], whole, tokens[:, 0])
+    mixed[-1], grad_act, hidden = lax.optimization_barrier((mixed[-1], grad_act, hidden))
+
+    for p in range(1 if own > 1 else 0, own):
         hidden = hidden + dot(mixed[p], out_t[:, p * part : (p + 1) * part], (0,), (1,))
     inverse_two = inverse_rms(hidden)
     unit_two = hidden * inverse_two
@@ -673,9 +727,8 @@
     pre_act = nn(normed_two, up_all) + b_up
     sigma = jax.nn.sigmoid(pre_act)
     activation = (pre_act * sigma).astype(bf16)
-    top_low = cotangent[:, 0]
     grad_top = top_low.astype(f32)
-    grad_pre = (nn(top_low, down_t) * (sigma * (1 + pre_act * (1 - sigma)))).astype(bf16)
+    grad_pre = (grad_act * (sigma * (1 + pre_act * (1 - sigma)))).astype(bf16)
     grad_normed_two = nt(grad_pre, up_all)
     grad_hidden = grad_top + norm_back(grad_normed_two, unit_two, inverse_two, gain_mlp)
     grad_hidden_low = grad_hidden.astype(bf16)

time: 532 us -> 523 us (0.983)
  matrix products: 51.4 us -> 35 us
  Pallas kernels: 258 us -> 274 us
  waiting for transfers between devices: 62.3 us -> 51.7 us
    dot_general x10 -> x8, matrix products: 51.4 us -> 35 us  [dot(): lax.dot_general(a, b, ((contract_a, contract_b), ((), ())), preferred_ele...]
    pallas_call x0 -> x2, Pallas kernels: none -> 14.9 us  [the longest x1 7.98 us: grad_act_of(): pl.pallas_call(grad_act_body, grid=(rows // block,), in_specs=[pl.BlockSp...]
    all_to_all x4, waiting for transfers between devices: 11.2 us -> 5.67 us  [to_tokens(): return lax.all_to_all(x, owners, 0, 0)]
  transfers between devices with their start and end apart: 46 -> 46, of which waited for: 15 -> 15; matrix products, arithmetic and copies ran while one was open for 23% -> 20% of each run, Pallas kernels for 49% -> 53%
where the time goes in v4:
time: 523 us; the launch traced here: 516 us
  Pallas kernels  274 us (52%)
  starting transfers between devices  62.6 us (12%)
  waiting for transfers between devices  51.7 us (10%)
  local copies, waits for them, and re-layouts  46.6 us (9%)
  matrix products  35 us (7%)
  other arithmetic  30.6 us (6%)
  between operations  15.9 us (3%)
    pallas_call x2, Pallas kernels, attend_back(): pl.pallas_call(functools.partial(attend_back_body, chunks=chunks, chunk=c...  102 us
    pallas_call x2, Pallas kernels, attend(): pl.pallas_call(functools.partial(attend_body, chunks=chunks, chunk=chunk)...  58.2 us
    ppermute x14, waiting for transfers between devices, swap(): lax.ppermute(x, ('ctx', 'tensor'), [(i, i ^ bit) for i in range(group)])  36.5 us
    dot_general x8, matrix products, dot(): lax.dot_general(a, b, ((contract_a, contract_b), ((), ())), preferred_ele...  35 us
    pallas_call x5, Pallas kernels, project_into(): pl.pallas_call(functools.partial(project_body, places=places), in_specs=[...  34.2 us
    pallas_call x2, Pallas kernels, weight_grad(): pl.pallas_call(functools.partial(weight_grad_body, spots=spots), in_specs...  24.9 us
    pallas_call x2, Pallas kernels, input_grad(): pl.pallas_call(finish_body if others else back_one_body, grid=(rows // bl...  24 us
    all_to_all x4, starting transfers between devices, to_tokens(): return lax.all_to_all(x, owners, 0, 0)  17.2 us
  transfers between devices with their start and end apart: 46, of which 15 were waited for; matrix products, arithmetic and copies ran while one was open for 20% of the time, Pallas kernels for 53%

profile of v4, /device:TPU:0, one launch (start us, length us, event | category | flops | bytes accessed | tf_op | source)
XLA Modules:
  0.0 516.2 jit_solution(5777953419779875050)
XLA Ops:
  7.2 3.0 collective-permute-start.3
  10.2 2.3 reshape.217
  57.0 2.3 pad_maximum_fusion.1
  59.3 2.5 copy.154
  65.6 2.5 copy.156
  68.1 5.8 %project.5 = (bf16[8,480,1024]{2,1,0:T(8,128)(2,1)}, f32[8,128]{1,0:T(8,128)}) custom-call(s32[2]{0:T(128)} %pad_add_fusion.1.slots_ref, bf16[480,1280]{1,0:T(8,128)(2,1)} %bitcast.181, f32[480,1]{1,0:T(8,128)} %broadcast_in_dim_tile.4.scale_ref, bf16[512,1280]{1,0:T(8,128)(2,1)} %copy-done.4, bf16[512,1280]{1,0:T(8,128)(2,1)} %copy-done.3), custom_call_target="tpu_custom_call" | custom-call | flops 1258291200 | bytes 5242880 | tf_op jit(solution)/shard_map/project/pallas_call | solution.py:290
  73.9 5.8 %project.6 = (bf16[8,480,1024]{2,1,0:T(8,128)(2,1)}, f32[8,128]{1,0:T(8,128)}) custom-call(s32[2]{0:T(128)} %pad_add_fusion.slots_ref, bf16[480,1280]{1,0:T(8,128)(2,1)} %bitcast.182, f32[480,1]{1,0:T(8,128)} %broadcast_in_dim_tile.4.scale_ref, bf16[512,1280]{1,0:T(8,128)(2,1)} %collective-permute-done.11.refs_0_.refs_2_, ...), custom_call_target="tpu_custom_call", output_to_operand_aliasing={{0}: (5, {})} | custom-call | flops 1258291200 | bytes 5242880 | tf_op jit(solution)/shard_map/project/pallas_call | solution.py:290
  79.7 12.3 %collective-permute-done.8.refs_1_.refs_5_ = bf16[512,1280]{1,0:T(8,128)(2,1)} collective-permute-done((bf16[512,1280]{1,0:T(8,128)(2,1)S(1)}, bf16[512,1280]{1,0:T(8,128)(2,1)}, u32[]{:S(2)}, u32[]{:S(2)}) %collective-permute-start.8) | collective-permute-done | bytes 1310752 | tf_op jit(solution)/shard_map/ppermute | solution.py:634
  102.1 7.6 %project.7 = (bf16[8,480,1024]{2,1,0:T(8,128)(2,1)}, f32[8,128]{1,0:T(8,128)}) custom-call(s32[4]{0:T(128)} %pad_add_fusion.4.slots_ref, bf16[480,1280]{1,0:T(8,128)(2,1)} %bitcast.183, f32[480,1]{1,0:T(8,128)} %broadcast_in_dim_tile.4.scale_ref, bf16[512,1280]{1,0:T(8,128)(2,1)} %collective-permute-done.7.refs_0_.refs_4_, ...), custom_call_target="tpu_custom_call", output_to_operand_aliasing={{0}: (7, {})} | custom-call | flops 2516582400 | bytes 10485760 | tf_op jit(solution)/shard_map/project/pallas_call | solution.py:290
  109.8 7.5 %project.8 = (bf16[8,480,1024]{2,1,0:T(8,128)(2,1)}, f32[8,128]{1,0:T(8,128)}) custom-call(s32[4]{0:T(128)} %pad_add_fusion.3.slots_ref, bf16[480,1280]{1,0:T(8,128)(2,1)} %bitcast.184, f32[480,1]{1,0:T(8,128)} %broadcast_in_dim_tile.4.scale_ref, bf16[512,1280]{1,0:T(8,128)(2,1)} %collective-permute-done.10.refs_0_.refs_8_, ...), custom_call_target="tpu_custom_call", output_to_operand_aliasing={{0}: (7, {})} | custom-call | flops 2516582400 | bytes 10485760 | tf_op jit(solution)/shard_map/project/pallas_call | solution.py:290
  117.3 15.5 %collective-permute-done.13.refs_0_.refs_12_ = bf16[512,1280]{1,0:T(8,128)(2,1)} collective-permute-done((bf16[512,1280]{1,0:T(8,128)(2,1)}, bf16[512,1280]{1,0:T(8,128)(2,1)}, u32[]{:S(2)}, u32[]{:S(2)}) %collective-permute-start.13) | collective-permute-done | bytes 1310752 | tf_op jit(solution)/shard_map/ppermute | solution.py:634
  136.1 3.7 collective-permute-done.20.refs_3_.refs_15_
  140.9 7.5 %project.9 = (bf16[8,480,1024]{2,1,0:T(8,128)(2,1)}, f32[8,128]{1,0:T(8,128)}) custom-call(s32[4]{0:T(128)} %pad_add_fusion.2.slots_ref, bf16[480,1280]{1,0:T(8,128)(2,1)} %bitcast.185, f32[480,1]{1,0:T(8,128)} %broadcast_in_dim_tile.4.scale_ref, bf16[512,1280]{1,0:T(8,128)(2,1)} %collective-permute-done.13.refs_0_.refs_12_, ...), custom_call_target="tpu_custom_call", output_to_operand_aliasing={{0}: (7, {})} | custom-call | flops 2516582400 | bytes 10485760 | tf_op jit(solution)/shard_map/project/pallas_call | solution.py:290
  148.4 29.1 %attend.3 = (bf16[8,80,1024]{2,1,0:T(8,128)(2,1)}, f32[8,80,1024]{2,1,0:T(8,128)}, f32[1,8,1024]{2,1,0:T(8,128)}) custom-call(s32[1]{0:T(128)} %bitcast.28.count, s32[258]{0:T(512)} %fusion.21.tiles, bf16[8,2,3,80,1024]{4,3,2,1,0:T(8,128)(2,1)} %bitcast.177, s32[1,8,1024]{2,1,0:T(8,128)} %bitcast.238), custom_call_target="tpu_custom_call" | custom-call | flops 17179869184 | bytes 16777216 | tf_op jit(solution)/shard_map/attend/pallas_call | solution.py:183
  177.5 3.6 all-to-all-start.1
  181.1 29.1 %attend.2 = (bf16[8,80,1024]{2,1,0:T(8,128)(2,1)}, f32[8,80,1024]{2,1,0:T(8,128)}, f32[1,8,1024]{2,1,0:T(8,128)}) custom-call(s32[1]{0:T(128)} %bitcast.28.count, s32[258]{0:T(512)} %fusion.21.tiles, bf16[8,2,3,80,1024]{4,3,2,1,0:T(8,128)(2,1)} %bitcast.178, s32[1,8,1024]{2,1,0:T(8,128)} %bitcast.239), custom_call_target="tpu_custom_call" | custom-call | flops 17179869184 | bytes 16777216 | tf_op jit(solution)/shard_map/attend/pallas_call | solution.py:183
  210.2 4.2 all-to-all-start
  214.6 8.0 %grad_act.1 = f32[1024,1280]{1,0:T(8,128)} custom-call(bf16[1024,1280]{1,0:T(8,128)(2,1)} %bitcast.189, bf16[3,1280,1280]{2,1,0:T(8,128)(2,1)} %all-gather.5.cloned.1.call-done.w_ref), custom_call_target="tpu_custom_call" | custom-call | flops 1 | bytes 1 | tf_op jit(solution)/shard_map/grad_act/pallas_call | solution.py:425
  222.6 6.9 %first_out.1 = f32[1024,1280]{1,0:T(8,128)} custom-call(bf16[640,1024]{1,0:T(8,128)(2,1)} %bitcast.194, bf16[3,1280,1280]{2,1,0:T(8,128)(2,1)} %all-gather.5.cloned.1.call-done.w_ref, bf16[1024,1280]{1,0:T(8,128)(2,1)} %bitcast.187), custom_call_target="tpu_custom_call" | custom-call | flops 1 | bytes 1 | tf_op jit(solution)/shard_map/first_out/pallas_call | solution.py:449
  229.5 5.0 all-to-all-done
  234.5 2.7 slice_bitcast_fusion.1
  237.3 5.8 %multiply_reduce_fusion.2 = (f32[1024]{0:T(1024)S(1)}, f32[1024,1280]{1,0:T(8,128)S(1)}) fusion(f32[1024,1280]{1,0:T(8,128)} %first_out.1, bf16[640,1024]{1,0:T(8,128)(2,1)S(1)} %bitcast.192, bf16[1280,1280]{1,0:T(8,128)(2,1)S(1)} %slice_bitcast_fusion.1), kind=kOutput, calls=%fused_computation.17 | convolution fusion | flops 1681652736 | bytes 13438976 | tf_op jit(solution)/shard_map/dot_general | solution.py:27
  243.8 7.3 %convert_reduce_fusion.1 = (f32[1280]{0:T(1024)}, bf16[1024,1280]{1,0:T(8,128)(2,1)}, bf16[1024,1280]{1,0:T(8,128)(2,1)}) fusion(f32[1024,1280]{1,0:T(8,128)S(1)} %bitcast.197, f32[1280]{0:T(1024)S(1)} %copy-done.36, bf16[1024,1280]{1,0:T(8,128)(2,1)S(1)} %multiply_convert_fusion.2, bf16[3,1280,1280]{2,1,0:T(8,128)(2,1)S(1)} %bitcast.176), kind=kOutput, calls=%fused_computation.10 | convolution fusion | flops 3373792000 | bytes 16397312 | tf_op jit(solution)/shard_map/dot_general | solution.py:27
  251.2 6.6 %multiply_reduce_fusion = (f32[1280]{0:T(1024)}, f32[1024]{0:T(1024)S(1)}, f32[1024,1280]{1,0:T(8,128)S(1)}) fusion(f32[1024,1280]{1,0:T(8,128)S(1)} %get-tuple-element.209.hidden_ref, f32[1024]{0:T(1024)S(1)} %add_rsqrt_fusion, f32[1280]{0:T(1024)S(1)} %copy-done.27, bf16[1024,1280]{1,0:T(8,128)(2,1)} %get-tuple-element.164, ...), kind=kOutput, calls=%fused_computation.11 | convolution fusion | flops 3363305216 | bytes 16405504 | tf_op jit(solution)/shard_map/dot_general | solution.py:27
  257.7 4.1 fusion.23
  261.8 3.0 fusion.8
  264.9 2.3 convolution_convert_fusion.2
  267.2 2.3 convolution_convert_fusion.3
  269.4 3.9 convolution_convert_fusion
  273.4 3.9 convolution_convert_fusion.1
  277.3 4.3 pad_maximum_fusion
  281.6 4.6 all-to-all-start.3
  286.8 6.0 %head_grad.1 = bf16[640,1024]{1,0:T(8,128)(2,1)} custom-call(bf16[1024,1280]{1,0:T(8,128)(2,1)} %copy-done.9, bf16[3,1280,1280]{2,1,0:T(8,128)(2,1)} %all-gather.5.cloned.1.call-done.w_ref), custom_call_target="tpu_custom_call" | custom-call | flops 1 | bytes 1 | tf_op jit(solution)/shard_map/head_grad/pallas_call | solution.py:402
  292.8 9.3 %outputs.1 = bf16[1024,1280]{1,0:T(8,128)(2,1)} custom-call(bf16[1024,1280]{1,0:T(8,128)(2,1)} %get-tuple-element.119.act_ref, bf16[3,1280,1280]{2,1,0:T(8,128)(2,1)} %all-gather.5.cloned.1.call-done.w_ref, f32[1024,1280]{1,0:T(8,128)} %copy-done, f32[1,1280]{1,0:T(1,128)} %broadcast_in_dim.66.bias_ref), custom_call_target="tpu_custom_call" | custom-call | flops 1 | bytes 1 | tf_op jit(solution)/shard_map/outputs/pallas_call | solution.py:473
  304.0 4.0 all-to-all-start.2
  308.7 51.0 %attend_back.3 = (bf16[8,3,80,1024]{3,2,1,0:T(8,128)(2,1)}, f32[80,128]{1,0:T(8,128)}) custom-call(s32[1]{0:T(128)} %bitcast.28.count, s32[258]{0:T(512)} %fusion.21.tiles, bf16[8,2,3,80,1024]{4,3,2,1,0:T(8,128)(2,1)} %bitcast.179, bf16[8,80,1024]{2,1,0:T(8,128)(2,1)} %copy-done.17, f32[8,80,1024]{2,1,0:T(8,128)} %get-tuple-element.126.wide_ref, ...), custom_call_target="tpu_custom_call" | custom-call | flops 42949672960 | bytes 16777216 | tf_op jit(solution)/shard_map/attend_back/pallas_call | solution.py:220
  360.7 4.5 all-to-all-start.4
  365.3 51.3 %attend_back.2 = (bf16[8,3,80,1024]{3,2,1,0:T(8,128)(2,1)}, f32[80,128]{1,0:T(8,128)}) custom-call(s32[1]{0:T(128)} %bitcast.28.count, s32[258]{0:T(512)} %fusion.21.tiles, bf16[8,2,3,80,1024]{4,3,2,1,0:T(8,128)(2,1)} %bitcast.180, bf16[8,80,1024]{2,1,0:T(8,128)(2,1)} %copy-done.16, f32[8,80,1024]{2,1,0:T(8,128)} %get-tuple-element.122.wide_ref, ...), custom_call_target="tpu_custom_call" | custom-call | flops 42949672960 | bytes 16777216 | tf_op jit(solution)/shard_map/attend_back/pallas_call | solution.py:220
  417.2 4.8 all-to-all-start.5
  424.0 12.5 %weight_grad.2 = (bf16[240,1280]{1,0:T(8,128)(2,1)}, f32[1,1280]{1,0:T(1,128)}) custom-call(s32[1]{0:T(128)} %bitcast.32.me_ref, bf16[512,1280]{1,0:T(8,128)(2,1)} %copy-done.4, bf16[512,1280]{1,0:T(8,128)(2,1)} %copy-done.3, bf16[512,1280]{1,0:T(8,128)(2,1)} %collective-permute-done.11.refs_0_.refs_2_, ...), custom_call_target="tpu_custom_call" | custom-call | flops 1 | bytes 1 | tf_op jit(solution)/shard_map/weight_grad/pallas_call | solution.py:335
  438.2 10.6 %input_grad.2.other_ref = f32[1024,1280]{1,0:T(8,128)} custom-call(bf16[1920,1024]{1,0:T(8,128)(2,1)} %bitcast.48.back_ref, bf16[1280,3840]{1,0:T(8,128)(2,1)} %all-gather.7.cloned.1.call-done.w_ref), custom_call_target="tpu_custom_call" | custom-call | flops 1 | bytes 1 | tf_op jit(solution)/shard_map/input_grad/pallas_call | solution.py:375
  450.3 2.7 collective-permute-start.22
  453.2 12.4 %weight_grad.3 = (bf16[240,1280]{1,0:T(8,128)(2,1)}, f32[1,1280]{1,0:T(1,128)}) custom-call(s32[1]{0:T(128)} %bitcast.32.me_ref, bf16[512,1280]{1,0:T(8,128)(2,1)} %copy-done.4, bf16[512,1280]{1,0:T(8,128)(2,1)} %copy-done.3, bf16[512,1280]{1,0:T(8,128)(2,1)} %collective-permute-done.11.refs_0_.refs_2_, ...), custom_call_target="tpu_custom_call" | custom-call | flops 1 | bytes 1 | tf_op jit(solution)/shard_map/weight_grad/pallas_call | solution.py:335
  469.4 3.7 collective-permute-start.26
  477.4 13.5 %input_grad.3 = bf16[1024,1280]{1,0:T(8,128)(2,1)} custom-call(bf16[1920,1024]{1,0:T(8,128)(2,1)} %bitcast.55.back_ref, bf16[1280,3840]{1,0:T(8,128)(2,1)} %all-gather.7.cloned.1.call-done.w_ref, f32[1024,1280]{1,0:T(8,128)} %input_grad.2.other_ref, bf16[1024,1280]{1,0:T(8,128)(2,1)} %bitcast.188, f32[1,1280]{1,0:T(1,128)} %broadcast_in_dim.69.gain_ref, ...), custom_call_target="tpu_custom_call" | custom-call | flops 5033164800 | bytes 20971520 | tf_op jit(solution)/shard_map/input_grad/pallas_call | solution.py:375
  490.8 3.0 collective-permute-start.28
  501.8 2.0 collective-permute-done.31
  505.7 2.1 reshape.244
  (285 shorter events, 92.0 us)
Async XLA Ops:
  7.2 58.4 %all-gather.9.cloned.1.call-start = ((), (), s32[]{:S(2)}) async-start(), calls=%async_computation.10 | async-start | bytes 1638400 | tf_op jit(solution)/shard_map/all_gather | solution.py:600
  7.2 20.1 %collective-permute-start.3 = (bf16[3,80,640]{2,1,0:T(8,128)(2,1)}, bf16[3,80,640]{2,1,0:T(8,128)(2,1)}, u32[]{:S(2)}, u32[]{:S(2)}) collective-permute-start(bf16[3,80,640]{2,1,0:T(8,128)(2,1)} %param.16), channel_id=1, source_target_pairs={{0,1},{1,0},{2,3},{3,2},{4,5},{5,4},{6,7},{7,6},{8,9},{9,8},{10,11... | collective-permute-start | bytes 921608 | tf_op jit(solution)/shard_map/ppermute | solution.py:558
  14.3 5.6 %collective-permute-start.2 = (bf16[80,480]{1,0:T(8,128)(2,1)S(1)}, bf16[80,480]{1,0:T(8,128)(2,1)S(1)}, u32[]{:S(2)}, u32[]{:S(2)}) collective-permute-start(bf16[80,480]{1,0:T(8,128)(2,1)S(1)} %bitcast.231), channel_id=1, source_target_pairs={{0,6},{2,4},{4,2},{6,0},{1,7},{3,5},{5,3},{7,1},{8,14},{10,12},{12... | collective-permute-start | bytes 230408 | tf_op jit(solution)/shard_map/ppermute | solution.py:587
  15.2 6.4 %collective-permute-start.1 = (bf16[80,480]{1,0:T(8,128)(2,1)S(1)}, bf16[80,480]{1,0:T(8,128)(2,1)S(1)}, u32[]{:S(2)}, u32[]{:S(2)}) collective-permute-start(bf16[80,480]{1,0:T(8,128)(2,1)S(1)} %bitcast.230), channel_id=1, source_target_pairs={{0,4},{2,6},{4,0},{6,2},{1,5},{3,7},{5,1},{7,3},{8,12},{10,14},{12... | collective-permute-start | bytes 230408 | tf_op jit(solution)/shard_map/ppermute | solution.py:587
  16.2 5.8 %collective-permute-start = (bf16[80,480]{1,0:T(8,128)(2,1)S(1)}, bf16[80,480]{1,0:T(8,128)(2,1)S(1)}, u32[]{:S(2)}, u32[]{:S(2)}) collective-permute-start(bf16[80,480]{1,0:T(8,128)(2,1)S(1)} %bitcast.229), channel_id=1, source_target_pairs={{0,2},{2,0},{4,6},{6,4},{1,3},{3,1},{5,7},{7,5},{8,10},{10,8},{12,... | collective-permute-start | bytes 230408 | tf_op jit(solution)/shard_map/ppermute | solution.py:587
  16.6 7.5 %collective-permute-start.4 = (bf16[640,80]{0,1:T(8,128)(2,1)}, bf16[640,80]{0,1:T(8,128)(2,1)}, u32[]{:S(2)}, u32[]{:S(2)}) collective-permute-start(bf16[640,80]{0,1:T(8,128)(2,1)} %param.17), channel_id=1, source_target_pairs={{0,1},{1,0},{2,3},{3,2},{4,5},{5,4},{6,7},{7,6},{8,9},{9,8},{10,11... | collective-permute-start | bytes 307208 | tf_op jit(solution)/shard_map/ppermute | solution.py:558
  18.5 21.1 %copy-start.3 = (bf16[512,1280]{1,0:T(8,128)(2,1)}, bf16[512,1280]{1,0:T(8,128)(2,1)S(1)}, u32[]{:S(2)}) copy-start(bf16[512,1280]{1,0:T(8,128)(2,1)S(1)} %get-tuple-element.87.refs_1_) | copy-start | bytes 3932164
  18.5 22.2 %copy-start.4 = (bf16[512,1280]{1,0:T(8,128)(2,1)}, bf16[512,1280]{1,0:T(8,128)(2,1)S(1)}, u32[]{:S(2)}) copy-start(bf16[512,1280]{1,0:T(8,128)(2,1)S(1)} %get-tuple-element.86.refs_0_) | copy-start | bytes 3932164
  19.9 6.1 %collective-permute-start.5 = (bf16[80,640]{1,0:T(8,128)(2,1)}, bf16[80,640]{1,0:T(8,128)(2,1)}, u32[]{:S(2)}, u32[]{:S(2)}) collective-permute-start(bf16[80,640]{1,0:T(8,128)(2,1)} %param.19), channel_id=1, source_target_pairs={{0,1},{1,0},{2,3},{3,2},{4,5},{5,4},{6,7},{7,6},{8,9},{9,8},{10,11... | collective-permute-start | bytes 307208 | tf_op jit(solution)/shard_map/ppermute | solution.py:558
  21.5 5.8 %collective-permute-start.6 = (bf16[640,80]{0,1:T(8,128)(2,1)}, bf16[640,80]{0,1:T(8,128)(2,1)}, u32[]{:S(2)}, u32[]{:S(2)}) collective-permute-start(bf16[640,80]{0,1:T(8,128)(2,1)} %param.21), channel_id=1, source_target_pairs={{0,1},{1,0},{2,3},{3,2},{4,5},{5,4},{6,7},{7,6},{8,9},{9,8},{10,11... | collective-permute-start | bytes 307208 | tf_op jit(solution)/shard_map/ppermute | solution.py:558
  27.3 13.4 %collective-permute-start.11 = (bf16[512,1280]{1,0:T(8,128)(2,1)S(1)}, bf16[512,1280]{1,0:T(8,128)(2,1)}, u32[]{:S(2)}, u32[]{:S(2)}) collective-permute-start(bf16[512,1280]{1,0:T(8,128)(2,1)S(1)} %get-tuple-element.86.refs_0_), channel_id=1, source_target_pairs={{0,2},{1,3},{2,0},{3,1},{4,6},{5,7},{6,4},{7,5},{8,10},{9,11},{10,... | collective-permute-start | bytes 3932168 | tf_op jit(solution)/shard_map/ppermute | solution.py:634
  30.3 184.3 %all-gather.5.cloned.1.call-start = ((), (), s32[]{:S(2)}) async-start(), calls=%async_computation.7 | async-start | bytes 10444800 | tf_op jit(solution)/shard_map/all_gather | solution.py:670
  32.7 47.0 %collective-permute-start.7 = (bf16[512,1280]{1,0:T(8,128)(2,1)S(1)}, bf16[512,1280]{1,0:T(8,128)(2,1)}, u32[]{:S(2)}, u32[]{:S(2)}) collective-permute-start(bf16[512,1280]{1,0:T(8,128)(2,1)S(1)} %get-tuple-element.86.refs_0_), channel_id=1, source_target_pairs={{0,1},{1,0},{2,3},{3,2},{4,5},{5,4},{6,7},{7,6},{8,9},{9,8},{10,11... | collective-permute-start | bytes 3932168 | tf_op jit(solution)/shard_map/ppermute | solution.py:634
  34.1 58.0 %collective-permute-start.8 = (bf16[512,1280]{1,0:T(8,128)(2,1)S(1)}, bf16[512,1280]{1,0:T(8,128)(2,1)}, u32[]{:S(2)}, u32[]{:S(2)}) collective-permute-start(bf16[512,1280]{1,0:T(8,128)(2,1)S(1)} %get-tuple-element.87.refs_1_), channel_id=1, source_target_pairs={{0,1},{1,0},{2,3},{3,2},{4,5},{5,4},{6,7},{7,6},{8,9},{9,8},{10,11... | collective-permute-start | bytes 3932168 | tf_op jit(solution)/shard_map/ppermute | solution.py:634
  34.7 57.4 %collective-permute-start.9 = (bf16[512,1280]{1,0:T(8,128)(2,1)S(1)}, bf16[512,1280]{1,0:T(8,128)(2,1)}, u32[]{:S(2)}, u32[]{:S(2)}) collective-permute-start(bf16[512,1280]{1,0:T(8,128)(2,1)S(1)} %get-tuple-element.87.refs_1_), channel_id=1, source_target_pairs={{0,4},{1,5},{2,6},{3,7},{4,0},{5,1},{6,2},{7,3},{8,12},{9,13},{10,... | collective-permute-start | bytes 3932168 | tf_op jit(solution)/shard_map/ppermute | solution.py:634
  36.1 37.7 %collective-permute-start.12 = (bf16[512,1280]{1,0:T(8,128)(2,1)S(1)}, bf16[512,1280]{1,0:T(8,128)(2,1)}, u32[]{:S(2)}, u32[]{:S(2)}) collective-permute-start(bf16[512,1280]{1,0:T(8,128)(2,1)S(1)} %get-tuple-element.87.refs_1_), channel_id=1, source_target_pairs={{0,2},{1,3},{2,0},{3,1},{4,6},{5,7},{6,4},{7,5},{8,10},{9,11},{10,... | collective-permute-start | bytes 3932168 | tf_op jit(solution)/shard_map/ppermute | solution.py:634
  40.7 52.8 %collective-permute-start.10 = (bf16[512,1280]{1,0:T(8,128)(2,1)S(1)}, bf16[512,1280]{1,0:T(8,128)(2,1)}, u32[]{:S(2)}, u32[]{:S(2)}) collective-permute-start(bf16[512,1280]{1,0:T(8,128)(2,1)S(1)} %get-tuple-element.86.refs_0_), channel_id=1, source_target_pairs={{0,4},{1,5},{2,6},{3,7},{4,0},{5,1},{6,2},{7,3},{8,12},{9,13},{10,... | collective-permute-start | bytes 3932168 | tf_op jit(solution)/shard_map/ppermute | solution.py:634
  93.5 188.1 %all-gather.7.cloned.1.call-start = ((), (), s32[]{:S(2)}) async-start(), calls=%async_computation.8 | async-start | bytes 10444800 | tf_op jit(solution)/shard_map/all_gather | solution.py:672
  94.0 3.3 collective-permute-start.17
  94.1 7.0 %collective-permute-start.18 = (bf16[512,1280]{1,0:T(8,128)(2,1)}, bf16[512,1280]{1,0:T(8,128)(2,1)S(1)}, u32[]{:S(2)}, u32[]{:S(2)}) collective-permute-start(bf16[512,1280]{1,0:T(8,128)(2,1)} %collective-permute-done.8.refs_1_.refs_5_), channel_id=1, source_target_pairs={{0,2},{1,3},{2,0},{3,1},{4,6},{5,7},{6,4},{7,5},{8,10},{9,11},{10,... | collective-permute-start | bytes 3932168 | tf_op jit(solution)/shard_map/ppermute | solution.py:634
  94.6 15.2 %collective-permute-start.15 = (bf16[512,1280]{1,0:T(8,128)(2,1)}, bf16[512,1280]{1,0:T(8,128)(2,1)}, u32[]{:S(2)}, u32[]{:S(2)}) collective-permute-start(bf16[512,1280]{1,0:T(8,128)(2,1)} %collective-permute-done.10.refs_0_.refs_8_), channel_id=1, source_target_pairs={{0,2},{1,3},{2,0},{3,1},{4,6},{5,7},{6,4},{7,5},{8,10},{9,11},{10,... | collective-permute-start | bytes 3932168 | tf_op jit(solution)/shard_map/ppermute | solution.py:634
  94.6 15.1 %collective-permute-start.16 = (bf16[512,1280]{1,0:T(8,128)(2,1)}, bf16[512,1280]{1,0:T(8,128)(2,1)}, u32[]{:S(2)}, u32[]{:S(2)}) collective-permute-start(bf16[512,1280]{1,0:T(8,128)(2,1)} %collective-permute-done.9.refs_1_.refs_9_), channel_id=1, source_target_pairs={{0,2},{1,3},{2,0},{3,1},{4,6},{5,7},{6,4},{7,5},{8,10},{9,11},{10,... | collective-permute-start | bytes 3932168 | tf_op jit(solution)/shard_map/ppermute | solution.py:634
  95.1 37.7 %collective-permute-start.13 = (bf16[512,1280]{1,0:T(8,128)(2,1)}, bf16[512,1280]{1,0:T(8,128)(2,1)}, u32[]{:S(2)}, u32[]{:S(2)}) collective-permute-start(bf16[512,1280]{1,0:T(8,128)(2,1)} %collective-permute-done.7.refs_0_.refs_4_), channel_id=1, source_target_pairs={{0,4},{1,5},{2,6},{3,7},{4,0},{5,1},{6,2},{7,3},{8,12},{9,13},{10,... | collective-permute-start | bytes 3932168 | tf_op jit(solution)/shard_map/ppermute | solution.py:634
  97.3 35.5 %collective-permute-start.14 = (bf16[512,1280]{1,0:T(8,128)(2,1)}, bf16[512,1280]{1,0:T(8,128)(2,1)}, u32[]{:S(2)}, u32[]{:S(2)}) collective-permute-start(bf16[512,1280]{1,0:T(8,128)(2,1)} %collective-permute-done.9.refs_1_.refs_9_), channel_id=1, source_target_pairs={{0,1},{1,0},{2,3},{3,2},{4,5},{5,4},{6,7},{7,6},{8,9},{9,8},{10,11... | collective-permute-start | bytes 3932168 | tf_op jit(solution)/shard_map/ppermute | solution.py:634
  132.8 3.2 collective-permute-start.19
  132.8 7.0 %collective-permute-start.20 = (bf16[512,1280]{1,0:T(8,128)(2,1)}, bf16[512,1280]{1,0:T(8,128)(2,1)S(1)}, u32[]{:S(2)}, u32[]{:S(2)}) collective-permute-start(bf16[512,1280]{1,0:T(8,128)(2,1)} %collective-permute-done.14.refs_1_.refs_13_), channel_id=1, source_target_pairs={{0,2},{1,3},{2,0},{3,1},{4,6},{5,7},{6,4},{7,5},{8,10},{9,11},{10,... | collective-permute-start | bytes 3932168 | tf_op jit(solution)/shard_map/ppermute | solution.py:634
  177.5 32.7 %all-to-all-start.1 = ((bf16[8,80,1024]{2,1,0:T(8,128)(2,1)}), bf16[8,80,1024]{2,1,0:T(8,128)(2,1)S(1)}, u32[]{:S(2)}, u32[]{:S(2)}) async-start(bf16[8,80,1024]{2,1,0:T(8,128)(2,1)} %get-tuple-element.115), calls=%async_computation.1 | async-start | bytes 2621440 | tf_op jit(solution)/shard_map/all_to_all | solution.py:694
  210.2 24.3 %all-to-all-start = ((bf16[8,80,1024]{2,1,0:T(8,128)(2,1)}), bf16[8,80,1024]{2,1,0:T(8,128)(2,1)S(1)}, u32[]{:S(2)}, u32[]{:S(2)}) async-start(bf16[8,80,1024]{2,1,0:T(8,128)(2,1)} %get-tuple-element.113), calls=%async_computation | async-start | bytes 2621440 | tf_op jit(solution)/shard_map/all_to_all | solution.py:694
  214.4 252.0 %reduce-scatter.2.cloned.1.call-start = ((), (), s32[]{:S(2)}) async-start(), calls=%async_computation.9 | async-start | bytes 10444800 | tf_op jit(solution)/shard_map/reduce_scatter | solution.py:749
  281.6 22.3 %all-to-all-start.3 = ((bf16[8,80,1024]{2,1,0:T(8,128)(2,1)}), bf16[8,80,1024]{2,1,0:T(8,128)(2,1)S(1)}, u32[]{:S(2)}, u32[]{:S(2)}) async-start(bf16[8,80,1024]{2,1,0:T(8,128)(2,1)} %bitcast.46), calls=%async_computation.3 | async-start | bytes 2621440 | tf_op jit(solution)/shard_map/all_to_all | solution.py:697
  304.0 55.7 %all-to-all-start.2 = ((bf16[8,80,1024]{2,1,0:T(8,128)(2,1)}), bf16[8,80,1024]{2,1,0:T(8,128)(2,1)S(1)}, u32[]{:S(2)}, u32[]{:S(2)}) async-start(bf16[8,80,1024]{2,1,0:T(8,128)(2,1)} %bitcast.45), calls=%async_computation.2 | async-start | bytes 2621440 | tf_op jit(solution)/shard_map/all_to_all | solution.py:697
  360.7 56.5 %all-to-all-start.4 = ((bf16[8,3,80,1024]{3,2,1,0:T(8,128)(2,1)}), bf16[8,3,80,1024]{3,2,1,0:T(8,128)(2,1)}, u32[]{:S(2)}, u32[]{:S(2)}) async-start(bf16[8,3,80,1024]{3,2,1,0:T(8,128)(2,1)} %get-tuple-element.131.refs_17_), calls=%async_computation.4 | async-start | bytes 7864320 | tf_op jit(solution)/shard_map/all_to_all | solution.py:694
  417.2 51.6 %all-to-all-start.5 = ((bf16[8,3,80,1024]{3,2,1,0:T(8,128)(2,1)}), bf16[8,3,80,1024]{3,2,1,0:T(8,128)(2,1)}, u32[]{:S(2)}, u32[]{:S(2)}) async-start(bf16[8,3,80,1024]{3,2,1,0:T(8,128)(2,1)} %get-tuple-element.140.refs_17_), calls=%async_computation.5 | async-start | bytes 7864320 | tf_op jit(solution)/shard_map/all_to_all | solution.py:694
  448.7 20.1 %collective-permute-start.21 = (bf16[320,240]{1,0:T(8,128)(2,1)S(1)}, bf16[320,240]{1,0:T(8,128)(2,1)S(1)}, u32[]{:S(2)}, u32[]{:S(2)}) collective-permute-start(bf16[320,240]{1,0:T(8,128)(2,1)S(1)} %get-tuple-element.178), channel_id=1, source_target_pairs={{0,8},{8,0},{16,24},{24,16},{1,9},{9,1},{17,25},{25,17},{2,10},{10... | collective-permute-start | bytes 460808 | tf_op jit(solution)/shard_map/ppermute | solution.py:802
  450.3 18.5 %collective-permute-start.22 = (bf16[320,240]{1,0:T(8,128)(2,1)S(1)}, bf16[320,240]{1,0:T(8,128)(2,1)S(1)}, u32[]{:S(2)}, u32[]{:S(2)}) collective-permute-start(bf16[320,240]{1,0:T(8,128)(2,1)S(1)} %get-tuple-element.177), channel_id=1, source_target_pairs={{0,16},{8,24},{16,0},{24,8},{1,17},{9,25},{17,1},{25,9},{2,18},{10... | collective-permute-start | bytes 460808 | tf_op jit(solution)/shard_map/ppermute | solution.py:802
  453.0 15.9 %collective-permute-start.23 = (bf16[320,240]{1,0:T(8,128)(2,1)S(1)}, bf16[320,240]{1,0:T(8,128)(2,1)S(1)}, u32[]{:S(2)}, u32[]{:S(2)}) collective-permute-start(bf16[320,240]{1,0:T(8,128)(2,1)S(1)} %get-tuple-element.176), channel_id=1, source_target_pairs={{0,24},{8,16},{16,8},{24,0},{1,25},{9,17},{17,9},{25,1},{2,26},{10... | collective-permute-start | bytes 460808 | tf_op jit(solution)/shard_map/ppermute | solution.py:802
  469.4 26.2 %collective-permute-start.26 = (bf16[320,240]{1,0:T(8,128)(2,1)S(1)}, bf16[320,240]{1,0:T(8,128)(2,1)S(1)}, u32[]{:S(2)}, u32[]{:S(2)}) collective-permute-start(bf16[320,240]{1,0:T(8,128)(2,1)S(1)} %get-tuple-element.174), channel_id=1, source_target_pairs={{0,24},{8,16},{16,8},{24,0},{1,25},{9,17},{17,9},{25,1},{2,26},{10... | collective-permute-start | bytes 460808 | tf_op jit(solution)/shard_map/ppermute | solution.py:802
  473.1 22.6 %collective-permute-start.25 = (bf16[320,240]{1,0:T(8,128)(2,1)S(1)}, bf16[320,240]{1,0:T(8,128)(2,1)S(1)}, u32[]{:S(2)}, u32[]{:S(2)}) collective-permute-start(bf16[320,240]{1,0:T(8,128)(2,1)S(1)} %get-tuple-element.175), channel_id=1, source_target_pairs={{0,16},{8,24},{16,0},{24,8},{1,17},{9,25},{17,1},{25,9},{2,18},{10... | collective-permute-start | bytes 460808 | tf_op jit(solution)/shard_map/ppermute | solution.py:802
  473.1 22.6 %collective-permute-start.24 = (bf16[320,240]{1,0:T(8,128)(2,1)S(1)}, bf16[320,240]{1,0:T(8,128)(2,1)S(1)}, u32[]{:S(2)}, u32[]{:S(2)}) collective-permute-start(bf16[320,240]{1,0:T(8,128)(2,1)S(1)} %get-tuple-element.173), channel_id=1, source_target_pairs={{0,8},{8,0},{16,24},{24,16},{1,9},{9,1},{17,25},{25,17},{2,10},{10... | collective-permute-start | bytes 460808 | tf_op jit(solution)/shard_map/ppermute | solution.py:802
  474.0 16.8 %collective-permute-start.27 = (f32[5200]{0:T(1024)S(1)}, f32[5200]{0:T(1024)S(1)}, u32[]{:S(2)}, u32[]{:S(2)}) collective-permute-start(f32[5200]{0:T(1024)S(1)} %constant_dynamic-update-slice_fusion), channel_id=1, source_target_pairs={{0,8},{8,0},{16,24},{24,16},{1,9},{9,1},{17,25},{25,17},{2,10},{10... | collective-permute-start | bytes 62408 | tf_op jit(solution)/shard_map/ppermute | solution.py:812
  475.3 20.6 %collective-permute-start.29 = (bf16[3,80,640]{2,1,0:T(8,128)(2,1)S(1)}, bf16[3,80,640]{2,1,0:T(8,128)(2,1)S(1)}, u32[]{:S(2)}, u32[]{:S(2)}) collective-permute-start(bf16[3,80,640]{2,1,0:T(8,128)(2,1)S(1)} %select_bitcast_fusion), channel_id=1, source_target_pairs={{0,1},{1,0},{2,3},{3,2},{4,5},{5,4},{6,7},{7,6},{8,9},{9,8},{10,11... | collective-permute-start | bytes 921608 | tf_op jit(solution)/shard_map/ppermute | solution.py:571
  490.8 4.8 collective-permute-start.28
  496.0 3.3 collective-permute-start.30
  496.7 7.1 %collective-permute-start.34 = (bf16[80,480]{1,0:T(8,128)(2,1)S(1)}, bf16[80,480]{1,0:T(8,128)(2,1)S(1)}, u32[]{:S(2)}, u32[]{:S(2)}) collective-permute-start(bf16[80,480]{1,0:T(8,128)(2,1)S(1)} %bitcast.234), channel_id=1, source_target_pairs={{0,6},{2,4},{4,2},{6,0},{1,7},{3,5},{5,3},{7,1},{8,14},{10,12},{12... | collective-permute-start | bytes 230408 | tf_op jit(solution)/shard_map/ppermute | solution.py:587
  498.5 5.3 %collective-permute-start.33 = (bf16[80,480]{1,0:T(8,128)(2,1)S(1)}, bf16[80,480]{1,0:T(8,128)(2,1)S(1)}, u32[]{:S(2)}, u32[]{:S(2)}) collective-permute-start(bf16[80,480]{1,0:T(8,128)(2,1)S(1)} %bitcast.235), channel_id=1, source_target_pairs={{0,4},{2,6},{4,0},{6,2},{1,5},{3,7},{5,1},{7,3},{8,12},{10,14},{12... | collective-permute-start | bytes 230408 | tf_op jit(solution)/shard_map/ppermute | solution.py:587
  499.2 4.6 collective-permute-start.32
  499.3 4.5 collective-permute-start.31
  504.4 3.9 collective-permute-start.35
  (41 other events, 240.4 us)
Sparse Core Ops, SparseCore 0:
  30.4 33.8 all-gather.8
  93.7 88.3 all-gather.4
  184.3 92.8 all-gather.6
  281.7 142.6 reduce-scatter.1

commit v5 on v4

--- a/solution.py
+++ b/solution.py
@@ -64,7 +64,7 @@
     turns(count[0] // 2, lambda t: tiles[t], False)
 
 
-def attend_body(count, tiles, x_ref, segment_ref, o_ref, wide_ref, lse_ref, key_rows, query_cols, acc, top, total, scores, *, chunks, chunk):
+def attend_body(count, tiles, x_ref, segment_ref, o_ref, lse_ref, key_rows, query_cols, acc, top, total, scores, *, chunks, chunk):
     nk = chunks * chunk // BLOCK_K
     per_q, per_k = chunk // BLOCK_Q, chunk // BLOCK_K
     lanes = BLOCK_Q // PARTS
@@ -108,12 +108,11 @@
     for c in range(chunks):
         t = total[c : c + 1, :]
         o = acc[c] / t
-        wide_ref[c] = o
         o_ref[c] = o.astype(bf16)
         lse_ref[0, c : c + 1, :] = top[c : c + 1, :] + jnp.log2(t)
 
 
-def attend_back_body(count, tiles, x_ref, g_ref, wide_ref, lse_ref, segment_ref, scale_ref, dx_ref, part_ref, key_rows, query_cols, value_rows, dq, dk, dv, delta, scores, grads, *, chunks, chunk):
+def attend_back_body(count, tiles, x_ref, g_ref, mixed_ref, lse_ref, segment_ref, scale_ref, dx_ref, part_ref, key_rows, query_cols, value_rows, dq, dk, dv, delta, scores, grads, *, chunks, chunk):
     nk = chunks * chunk // BLOCK_K
     per_q, per_k = chunk // BLOCK_Q, chunk // BLOCK_K
     lanes = BLOCK_Q // PARTS
@@ -123,7 +122,7 @@
         key_rows[pl.ds(c * chunk, chunk), :] = keys.T
         query_cols[c] = jnp.concatenate([x_ref[c, 0, 0], jnp.where(hot, 0.0, NEGATIVE).astype(bf16)], axis=0)
         value_rows[pl.ds(c * chunk, chunk), :] = x_ref[c, 0, 2].T
-        delta[c : c + 1, :] = jnp.sum(g_ref[c].astype(f32) * wide_ref[c], axis=0, keepdims=True)
+        delta[c : c + 1, :] = jnp.sum(g_ref[c].astype(f32) * mixed_ref[c].astype(f32), axis=0, keepdims=True)
         for ref in (dq, dk, dv):
             ref[c] = jnp.zeros((HD, chunk), f32)
     key_iota = lax.broadcasted_iota(jnp.int32, (BLOCK_K, lanes), 0)
@@ -191,7 +190,6 @@
             ],
             out_specs=[
                 pl.BlockSpec((chunks, HD, chunk), flat),
-                pl.BlockSpec((chunks, HD, chunk), flat),
                 pl.BlockSpec((1, chunks, chunk), flat),
             ],
             scratch_shapes=[
@@ -205,7 +203,6 @@
         ),
         out_shape=[
             jax.ShapeDtypeStruct((chunks, HD, chunk), bf16),
-            jax.ShapeDtypeStruct((chunks, HD, chunk), f32),
             jax.ShapeDtypeStruct((1, chunks, chunk), f32),
         ],
         compiler_params=pltpu.CompilerParams(vmem_limit_bytes=VMEM_BYTES),
@@ -214,7 +211,7 @@
     )(*tables, x, segments)
 
 
-def attend_back(tables, x, grad, wide, lse, segments, scale, p):
+def attend_back(tables, x, grad, mixed, lse, segments, scale, p):
     chunks, _, _, _, chunk = x.shape
     flat = lambda g, *_: (0, 0, 0)
     return pl.pallas_call(
@@ -253,7 +250,7 @@
         compiler_params=pltpu.CompilerParams(vmem_limit_bytes=VMEM_BYTES),
         cost_estimate=kernel_cost(chunks * chunk, 5),
         name="attend_back",
-    )(*tables, x, grad, wide, lse, segments, scale)
+    )(*tables, x, grad, mixed, lse, segments, scale)
 
 
 def project_body(slots_ref, w_ref, scale_ref, *refs, places):
@@ -705,10 +702,10 @@
 
     part = n_owners * HD
 
-    mixed, wides, lses = [], [], []
+    mixed, head_outs, lses = [], [], []
     for p in range(own):
-        o, wide, lse = attend(tiles, heads_x, seg_chunks, p)
-        wides.append(wide)
+        o, lse = attend(tiles, heads_x, seg_chunks, p)
+        head_outs.append(o)
         lses.append(lse)
         if p == own - 1:
             o, top_low = lax.optimization_barrier((o, cotangent[:, 0]))
@@ -757,7 +754,7 @@
     dxs, backs, wgrads, travelled = [], [], [], []
     for p in range(own):
         dx, part_sum = attend_back(
-            tiles, heads_x, grad_heads[p], wides[p], lses[p], seg_chunks, scale_tile, p
+            tiles, heads_x, grad_heads[p], head_outs[p], lses[p], seg_chunks, scale_tile, p
         )
         if p:
             dx, backs[-1] = lax.optimization_barrier((dx, backs[-1]))

time: 523 us -> 519 us (level)
  no operation moved by 1% of the time
where the time goes in v5:
time: 519 us; the launch traced here: 514 us
  Pallas kernels  271 us (52%)
  starting transfers between devices  62.1 us (12%)
  waiting for transfers between devices  53.2 us (10%)
  local copies, waits for them, and re-layouts  46.6 us (9%)
  matrix products  35 us (7%)
  other arithmetic  30.6 us (6%)
  between operations  15.8 us (3%)
    pallas_call x2, Pallas kernels, attend_back(): pl.pallas_call(functools.partial(attend_back_body, chunks=chunks, chunk=c...  101 us
    pallas_call x2, Pallas kernels, attend(): pl.pallas_call(functools.partial(attend_body, chunks=chunks, chunk=chunk)...  56.7 us
    ppermute x14, waiting for transfers between devices, swap(): lax.ppermute(x, ('ctx', 'tensor'), [(i, i ^ bit) for i in range(group)])  36.5 us
    dot_general x8, matrix products, dot(): lax.dot_general(a, b, ((contract_a, contract_b), ((), ())), preferred_ele...  35 us
    pallas_call x5, Pallas kernels, project_into(): pl.pallas_call(functools.partial(project_body, places=places), in_specs=[...  34.2 us
    pallas_call x2, Pallas kernels, weight_grad(): pl.pallas_call(functools.partial(weight_grad_body, spots=spots), in_specs...  25 us
    pallas_call x2, Pallas kernels, input_grad(): pl.pallas_call(finish_body if others else back_one_body, grid=(rows // bl...  24 us
    all_to_all x4, starting transfers between devices, to_tokens(): return lax.all_to_all(x, owners, 0, 0)  17.4 us
  transfers between devices with their start and end apart: 46, of which 15 were waited for; matrix products, arithmetic and copies ran while one was open for 20% of the time, Pallas kernels for 53%

profile of v5, /device:TPU:0, one launch (start us, length us, event | category | flops | bytes accessed | tf_op | source)
XLA Modules:
  0.0 513.9 jit_solution(4118203299504961543)
XLA Ops:
  7.2 3.0 collective-permute-start.3
  10.2 2.3 reshape.217
  56.9 2.3 pad_maximum_fusion.1
  59.3 2.5 copy.154
  65.6 2.5 copy.156
  68.1 5.8 %project.5 = (bf16[8,480,1024]{2,1,0:T(8,128)(2,1)}, f32[8,128]{1,0:T(8,128)}) custom-call(s32[2]{0:T(128)} %pad_add_fusion.1.slots_ref, bf16[480,1280]{1,0:T(8,128)(2,1)} %bitcast.181, f32[480,1]{1,0:T(8,128)} %broadcast_in_dim_tile.4.scale_ref, bf16[512,1280]{1,0:T(8,128)(2,1)} %copy-done.4, bf16[512,1280]{1,0:T(8,128)(2,1)} %copy-done.3), custom_call_target="tpu_custom_call" | custom-call | flops 1258291200 | bytes 5242880 | tf_op jit(solution)/shard_map/project/pallas_call | solution.py:287
  73.9 5.8 %project.6 = (bf16[8,480,1024]{2,1,0:T(8,128)(2,1)}, f32[8,128]{1,0:T(8,128)}) custom-call(s32[2]{0:T(128)} %pad_add_fusion.slots_ref, bf16[480,1280]{1,0:T(8,128)(2,1)} %bitcast.182, f32[480,1]{1,0:T(8,128)} %broadcast_in_dim_tile.4.scale_ref, bf16[512,1280]{1,0:T(8,128)(2,1)} %collective-permute-done.11.refs_0_.refs_2_, ...), custom_call_target="tpu_custom_call", output_to_operand_aliasing={{0}: (5, {})} | custom-call | flops 1258291200 | bytes 5242880 | tf_op jit(solution)/shard_map/project/pallas_call | solution.py:287
  79.7 12.3 %collective-permute-done.8.refs_1_.refs_5_ = bf16[512,1280]{1,0:T(8,128)(2,1)} collective-permute-done((bf16[512,1280]{1,0:T(8,128)(2,1)S(1)}, bf16[512,1280]{1,0:T(8,128)(2,1)}, u32[]{:S(2)}, u32[]{:S(2)}) %collective-permute-start.8) | collective-permute-done | bytes 1310752 | tf_op jit(solution)/shard_map/ppermute | solution.py:631
  102.0 7.7 %project.7 = (bf16[8,480,1024]{2,1,0:T(8,128)(2,1)}, f32[8,128]{1,0:T(8,128)}) custom-call(s32[4]{0:T(128)} %pad_add_fusion.4.slots_ref, bf16[480,1280]{1,0:T(8,128)(2,1)} %bitcast.183, f32[480,1]{1,0:T(8,128)} %broadcast_in_dim_tile.4.scale_ref, bf16[512,1280]{1,0:T(8,128)(2,1)} %collective-permute-done.7.refs_0_.refs_4_, ...), custom_call_target="tpu_custom_call", output_to_operand_aliasing={{0}: (7, {})} | custom-call | flops 2516582400 | bytes 10485760 | tf_op jit(solution)/shard_map/project/pallas_call | solution.py:287
  109.7 7.5 %project.8 = (bf16[8,480,1024]{2,1,0:T(8,128)(2,1)}, f32[8,128]{1,0:T(8,128)}) custom-call(s32[4]{0:T(128)} %pad_add_fusion.3.slots_ref, bf16[480,1280]{1,0:T(8,128)(2,1)} %bitcast.184, f32[480,1]{1,0:T(8,128)} %broadcast_in_dim_tile.4.scale_ref, bf16[512,1280]{1,0:T(8,128)(2,1)} %collective-permute-done.10.refs_0_.refs_8_, ...), custom_call_target="tpu_custom_call", output_to_operand_aliasing={{0}: (7, {})} | custom-call | flops 2516582400 | bytes 10485760 | tf_op jit(solution)/shard_map/project/pallas_call | solution.py:287
  117.2 15.5 %collective-permute-done.13.refs_0_.refs_12_ = bf16[512,1280]{1,0:T(8,128)(2,1)} collective-permute-done((bf16[512,1280]{1,0:T(8,128)(2,1)}, bf16[512,1280]{1,0:T(8,128)(2,1)}, u32[]{:S(2)}, u32[]{:S(2)}) %collective-permute-start.13) | collective-permute-done | bytes 1310752 | tf_op jit(solution)/shard_map/ppermute | solution.py:631
  135.9 3.7 collective-permute-done.20.refs_3_.refs_15_
  140.7 7.5 %project.9 = (bf16[8,480,1024]{2,1,0:T(8,128)(2,1)}, f32[8,128]{1,0:T(8,128)}) custom-call(s32[4]{0:T(128)} %pad_add_fusion.2.slots_ref, bf16[480,1280]{1,0:T(8,128)(2,1)} %bitcast.185, f32[480,1]{1,0:T(8,128)} %broadcast_in_dim_tile.4.scale_ref, bf16[512,1280]{1,0:T(8,128)(2,1)} %collective-permute-done.13.refs_0_.refs_12_, ...), custom_call_target="tpu_custom_call", output_to_operand_aliasing={{0}: (7, {})} | custom-call | flops 2516582400 | bytes 10485760 | tf_op jit(solution)/shard_map/project/pallas_call | solution.py:287
  148.2 28.2 %attend.3 = (bf16[8,80,1024]{2,1,0:T(8,128)(2,1)}, f32[1,8,1024]{2,1,0:T(8,128)}) custom-call(s32[1]{0:T(128)} %bitcast.28.count, s32[258]{0:T(512)} %fusion.21.tiles, bf16[8,2,3,80,1024]{4,3,2,1,0:T(8,128)(2,1)} %bitcast.177, s32[1,8,1024]{2,1,0:T(8,128)} %bitcast.238), custom_call_target="tpu_custom_call" | custom-call | flops 17179869184 | bytes 16777216 | tf_op jit(solution)/shard_map/attend/pallas_call | solution.py:182
  176.4 3.6 all-to-all-start.1
  180.0 28.6 %attend.2 = (bf16[8,80,1024]{2,1,0:T(8,128)(2,1)}, f32[1,8,1024]{2,1,0:T(8,128)}) custom-call(s32[1]{0:T(128)} %bitcast.28.count, s32[258]{0:T(512)} %fusion.21.tiles, bf16[8,2,3,80,1024]{4,3,2,1,0:T(8,128)(2,1)} %bitcast.178, s32[1,8,1024]{2,1,0:T(8,128)} %bitcast.239), custom_call_target="tpu_custom_call" | custom-call | flops 17179869184 | bytes 16777216 | tf_op jit(solution)/shard_map/attend/pallas_call | solution.py:182
  208.6 4.2 all-to-all-start
  212.9 8.0 %grad_act.1 = f32[1024,1280]{1,0:T(8,128)} custom-call(bf16[1024,1280]{1,0:T(8,128)(2,1)} %bitcast.189, bf16[3,1280,1280]{2,1,0:T(8,128)(2,1)} %all-gather.5.cloned.1.call-done.w_ref), custom_call_target="tpu_custom_call" | custom-call | flops 1 | bytes 1 | tf_op jit(solution)/shard_map/grad_act/pallas_call | solution.py:422
  220.9 6.9 %first_out.1 = f32[1024,1280]{1,0:T(8,128)} custom-call(bf16[640,1024]{1,0:T(8,128)(2,1)} %bitcast.194, bf16[3,1280,1280]{2,1,0:T(8,128)(2,1)} %all-gather.5.cloned.1.call-done.w_ref, bf16[1024,1280]{1,0:T(8,128)(2,1)} %bitcast.187), custom_call_target="tpu_custom_call" | custom-call | flops 1 | bytes 1 | tf_op jit(solution)/shard_map/first_out/pallas_call | solution.py:446
  227.8 5.2 %all-to-all-done = bf16[8,80,1024]{2,1,0:T(8,128)(2,1)S(1)} async-done(((bf16[8,80,1024]{2,1,0:T(8,128)(2,1)}), bf16[8,80,1024]{2,1,0:T(8,128)(2,1)S(1)}, u32[]{:S(2)}, u32[]{:S(2)}) %all-to-all-start) | async-done | bytes 1310752 | tf_op jit(solution)/shard_map/all_to_all | solution.py:691
  233.0 2.7 slice_bitcast_fusion.1
  235.7 5.8 %multiply_reduce_fusion.2 = (f32[1024]{0:T(1024)S(1)}, f32[1024,1280]{1,0:T(8,128)S(1)}) fusion(f32[1024,1280]{1,0:T(8,128)} %first_out.1, bf16[640,1024]{1,0:T(8,128)(2,1)S(1)} %bitcast.192, bf16[1280,1280]{1,0:T(8,128)(2,1)S(1)} %slice_bitcast_fusion.1), kind=kOutput, calls=%fused_computation.17 | convolution fusion | flops 1681652736 | bytes 13438976 | tf_op jit(solution)/shard_map/dot_general | solution.py:27
  242.2 7.3 %convert_reduce_fusion.1 = (f32[1280]{0:T(1024)}, bf16[1024,1280]{1,0:T(8,128)(2,1)}, bf16[1024,1280]{1,0:T(8,128)(2,1)}) fusion(f32[1024,1280]{1,0:T(8,128)S(1)} %bitcast.197, f32[1280]{0:T(1024)S(1)} %copy-done.36, bf16[1024,1280]{1,0:T(8,128)(2,1)S(1)} %multiply_convert_fusion.2, bf16[3,1280,1280]{2,1,0:T(8,128)(2,1)S(1)} %bitcast.176), kind=kOutput, calls=%fused_computation.10 | convolution fusion | flops 3373792000 | bytes 16397312 | tf_op jit(solution)/shard_map/dot_general | solution.py:27
  249.6 6.6 %multiply_reduce_fusion = (f32[1280]{0:T(1024)}, f32[1024]{0:T(1024)S(1)}, f32[1024,1280]{1,0:T(8,128)S(1)}) fusion(f32[1024,1280]{1,0:T(8,128)S(1)} %get-tuple-element.205.hidden_ref, f32[1024]{0:T(1024)S(1)} %add_rsqrt_fusion, f32[1280]{0:T(1024)S(1)} %copy-done.27, bf16[1024,1280]{1,0:T(8,128)(2,1)} %get-tuple-element.160, ...), kind=kOutput, calls=%fused_computation.11 | convolution fusion | flops 3363305216 | bytes 16405504 | tf_op jit(solution)/shard_map/dot_general | solution.py:27
  256.1 4.1 fusion.23
  260.2 3.1 fusion.8
  263.3 2.3 convolution_convert_fusion.2
  265.6 2.3 convolution_convert_fusion.3
  267.9 3.9 convolution_convert_fusion
  271.8 3.9 convolution_convert_fusion.1
  275.7 4.3 pad_maximum_fusion
  280.0 4.4 all-to-all-start.3
  285.0 5.9 %head_grad.1 = bf16[640,1024]{1,0:T(8,128)(2,1)} custom-call(bf16[1024,1280]{1,0:T(8,128)(2,1)} %copy-done.9, bf16[3,1280,1280]{2,1,0:T(8,128)(2,1)} %all-gather.5.cloned.1.call-done.w_ref), custom_call_target="tpu_custom_call" | custom-call | flops 1 | bytes 1 | tf_op jit(solution)/shard_map/head_grad/pallas_call | solution.py:399
  290.9 9.3 %outputs.1 = bf16[1024,1280]{1,0:T(8,128)(2,1)} custom-call(bf16[1024,1280]{1,0:T(8,128)(2,1)} %get-tuple-element.117.act_ref, bf16[3,1280,1280]{2,1,0:T(8,128)(2,1)} %all-gather.5.cloned.1.call-done.w_ref, f32[1024,1280]{1,0:T(8,128)} %copy-done, f32[1,1280]{1,0:T(1,128)} %broadcast_in_dim.66.bias_ref), custom_call_target="tpu_custom_call" | custom-call | flops 1 | bytes 1 | tf_op jit(solution)/shard_map/outputs/pallas_call | solution.py:470
  302.1 3.8 all-to-all-start.2
  306.7 50.2 %attend_back.3 = (bf16[8,3,80,1024]{3,2,1,0:T(8,128)(2,1)}, f32[80,128]{1,0:T(8,128)}) custom-call(s32[1]{0:T(128)} %bitcast.28.count, s32[258]{0:T(512)} %fusion.21.tiles, bf16[8,2,3,80,1024]{4,3,2,1,0:T(8,128)(2,1)} %bitcast.179, bf16[8,80,1024]{2,1,0:T(8,128)(2,1)} %copy-done.17, bf16[8,80,1024]{2,1,0:T(8,128)(2,1)} %get-tuple-element.113.mixed_ref, ...), custom_call_target="tpu_custom_call" | custom-call | flops 42949672960 | bytes 16777216 | tf_op jit(solution)/shard_map/attend_back/pallas_call | solution.py:217
  357.9 4.5 all-to-all-start.4
  362.5 50.3 %attend_back.2 = (bf16[8,3,80,1024]{3,2,1,0:T(8,128)(2,1)}, f32[80,128]{1,0:T(8,128)}) custom-call(s32[1]{0:T(128)} %bitcast.28.count, s32[258]{0:T(512)} %fusion.21.tiles, bf16[8,2,3,80,1024]{4,3,2,1,0:T(8,128)(2,1)} %bitcast.180, bf16[8,80,1024]{2,1,0:T(8,128)(2,1)} %copy-done.16, bf16[8,80,1024]{2,1,0:T(8,128)(2,1)} %get-tuple-element.111.mixed_ref, ...), custom_call_target="tpu_custom_call" | custom-call | flops 42949672960 | bytes 16777216 | tf_op jit(solution)/shard_map/attend_back/pallas_call | solution.py:217
  414.4 5.1 all-to-all-start.5
  421.5 12.5 %weight_grad.2 = (bf16[240,1280]{1,0:T(8,128)(2,1)}, f32[1,1280]{1,0:T(1,128)}) custom-call(s32[1]{0:T(128)} %bitcast.32.me_ref, bf16[512,1280]{1,0:T(8,128)(2,1)} %copy-done.4, bf16[512,1280]{1,0:T(8,128)(2,1)} %copy-done.3, bf16[512,1280]{1,0:T(8,128)(2,1)} %collective-permute-done.11.refs_0_.refs_2_, ...), custom_call_target="tpu_custom_call" | custom-call | flops 1 | bytes 1 | tf_op jit(solution)/shard_map/weight_grad/pallas_call | solution.py:332
  435.6 10.5 %input_grad.2.other_ref = f32[1024,1280]{1,0:T(8,128)} custom-call(bf16[1920,1024]{1,0:T(8,128)(2,1)} %bitcast.48.back_ref, bf16[1280,3840]{1,0:T(8,128)(2,1)} %all-gather.7.cloned.1.call-done.w_ref), custom_call_target="tpu_custom_call" | custom-call | flops 1 | bytes 1 | tf_op jit(solution)/shard_map/input_grad/pallas_call | solution.py:372
  447.9 2.5 collective-permute-start.22
  450.6 12.4 %weight_grad.3 = (bf16[240,1280]{1,0:T(8,128)(2,1)}, f32[1,1280]{1,0:T(1,128)}) custom-call(s32[1]{0:T(128)} %bitcast.32.me_ref, bf16[512,1280]{1,0:T(8,128)(2,1)} %copy-done.4, bf16[512,1280]{1,0:T(8,128)(2,1)} %copy-done.3, bf16[512,1280]{1,0:T(8,128)(2,1)} %collective-permute-done.11.refs_0_.refs_2_, ...), custom_call_target="tpu_custom_call" | custom-call | flops 1 | bytes 1 | tf_op jit(solution)/shard_map/weight_grad/pallas_call | solution.py:332
  466.9 3.7 collective-permute-start.26
  474.8 13.5 %input_grad.3 = bf16[1024,1280]{1,0:T(8,128)(2,1)} custom-call(bf16[1920,1024]{1,0:T(8,128)(2,1)} %bitcast.55.back_ref, bf16[1280,3840]{1,0:T(8,128)(2,1)} %all-gather.7.cloned.1.call-done.w_ref, f32[1024,1280]{1,0:T(8,128)} %input_grad.2.other_ref, bf16[1024,1280]{1,0:T(8,128)(2,1)} %bitcast.188, f32[1,1280]{1,0:T(1,128)} %broadcast_in_dim.69.gain_ref, ...), custom_call_target="tpu_custom_call" | custom-call | flops 5033164800 | bytes 20971520 | tf_op jit(solution)/shard_map/input_grad/pallas_call | solution.py:372
  488.3 3.0 collective-permute-start.28
  499.5 2.0 collective-permute-done.31
  503.4 2.1 reshape.244
  (285 shorter events, 93.1 us)
Async XLA Ops:
  7.2 58.4 %all-gather.9.cloned.1.call-start = ((), (), s32[]{:S(2)}) async-start(), calls=%async_computation.10 | async-start | bytes 1638400 | tf_op jit(solution)/shard_map/all_gather | solution.py:597
  7.2 20.1 %collective-permute-start.3 = (bf16[3,80,640]{2,1,0:T(8,128)(2,1)}, bf16[3,80,640]{2,1,0:T(8,128)(2,1)}, u32[]{:S(2)}, u32[]{:S(2)}) collective-permute-start(bf16[3,80,640]{2,1,0:T(8,128)(2,1)} %param.16), channel_id=1, source_target_pairs={{0,1},{1,0},{2,3},{3,2},{4,5},{5,4},{6,7},{7,6},{8,9},{9,8},{10,11... | collective-permute-start | bytes 921608 | tf_op jit(solution)/shard_map/ppermute | solution.py:555
  14.3 5.6 %collective-permute-start.2 = (bf16[80,480]{1,0:T(8,128)(2,1)S(1)}, bf16[80,480]{1,0:T(8,128)(2,1)S(1)}, u32[]{:S(2)}, u32[]{:S(2)}) collective-permute-start(bf16[80,480]{1,0:T(8,128)(2,1)S(1)} %bitcast.231), channel_id=1, source_target_pairs={{0,6},{2,4},{4,2},{6,0},{1,7},{3,5},{5,3},{7,1},{8,14},{10,12},{12... | collective-permute-start | bytes 230408 | tf_op jit(solution)/shard_map/ppermute | solution.py:584
  15.2 6.4 %collective-permute-start.1 = (bf16[80,480]{1,0:T(8,128)(2,1)S(1)}, bf16[80,480]{1,0:T(8,128)(2,1)S(1)}, u32[]{:S(2)}, u32[]{:S(2)}) collective-permute-start(bf16[80,480]{1,0:T(8,128)(2,1)S(1)} %bitcast.230), channel_id=1, source_target_pairs={{0,4},{2,6},{4,0},{6,2},{1,5},{3,7},{5,1},{7,3},{8,12},{10,14},{12... | collective-permute-start | bytes 230408 | tf_op jit(solution)/shard_map/ppermute | solution.py:584
  16.2 5.8 %collective-permute-start = (bf16[80,480]{1,0:T(8,128)(2,1)S(1)}, bf16[80,480]{1,0:T(8,128)(2,1)S(1)}, u32[]{:S(2)}, u32[]{:S(2)}) collective-permute-start(bf16[80,480]{1,0:T(8,128)(2,1)S(1)} %bitcast.229), channel_id=1, source_target_pairs={{0,2},{2,0},{4,6},{6,4},{1,3},{3,1},{5,7},{7,5},{8,10},{10,8},{12,... | collective-permute-start | bytes 230408 | tf_op jit(solution)/shard_map/ppermute | solution.py:584
  16.6 7.5 %collective-permute-start.4 = (bf16[640,80]{0,1:T(8,128)(2,1)}, bf16[640,80]{0,1:T(8,128)(2,1)}, u32[]{:S(2)}, u32[]{:S(2)}) collective-permute-start(bf16[640,80]{0,1:T(8,128)(2,1)} %param.17), channel_id=1, source_target_pairs={{0,1},{1,0},{2,3},{3,2},{4,5},{5,4},{6,7},{7,6},{8,9},{9,8},{10,11... | collective-permute-start | bytes 307208 | tf_op jit(solution)/shard_map/ppermute | solution.py:555
  18.5 21.1 %copy-start.3 = (bf16[512,1280]{1,0:T(8,128)(2,1)}, bf16[512,1280]{1,0:T(8,128)(2,1)S(1)}, u32[]{:S(2)}) copy-start(bf16[512,1280]{1,0:T(8,128)(2,1)S(1)} %get-tuple-element.85.refs_1_) | copy-start | bytes 3932164
  18.5 22.1 %copy-start.4 = (bf16[512,1280]{1,0:T(8,128)(2,1)}, bf16[512,1280]{1,0:T(8,128)(2,1)S(1)}, u32[]{:S(2)}) copy-start(bf16[512,1280]{1,0:T(8,128)(2,1)S(1)} %get-tuple-element.84.refs_0_) | copy-start | bytes 3932164
  19.9 6.1 %collective-permute-start.5 = (bf16[80,640]{1,0:T(8,128)(2,1)}, bf16[80,640]{1,0:T(8,128)(2,1)}, u32[]{:S(2)}, u32[]{:S(2)}) collective-permute-start(bf16[80,640]{1,0:T(8,128)(2,1)} %param.19), channel_id=1, source_target_pairs={{0,1},{1,0},{2,3},{3,2},{4,5},{5,4},{6,7},{7,6},{8,9},{9,8},{10,11... | collective-permute-start | bytes 307208 | tf_op jit(solution)/shard_map/ppermute | solution.py:555
  21.5 5.8 %collective-permute-start.6 = (bf16[640,80]{0,1:T(8,128)(2,1)}, bf16[640,80]{0,1:T(8,128)(2,1)}, u32[]{:S(2)}, u32[]{:S(2)}) collective-permute-start(bf16[640,80]{0,1:T(8,128)(2,1)} %param.21), channel_id=1, source_target_pairs={{0,1},{1,0},{2,3},{3,2},{4,5},{5,4},{6,7},{7,6},{8,9},{9,8},{10,11... | collective-permute-start | bytes 307208 | tf_op jit(solution)/shard_map/ppermute | solution.py:555
  27.3 13.3 %collective-permute-start.11 = (bf16[512,1280]{1,0:T(8,128)(2,1)S(1)}, bf16[512,1280]{1,0:T(8,128)(2,1)}, u32[]{:S(2)}, u32[]{:S(2)}) collective-permute-start(bf16[512,1280]{1,0:T(8,128)(2,1)S(1)} %get-tuple-element.84.refs_0_), channel_id=1, source_target_pairs={{0,2},{1,3},{2,0},{3,1},{4,6},{5,7},{6,4},{7,5},{8,10},{9,11},{10,... | collective-permute-start | bytes 3932168 | tf_op jit(solution)/shard_map/ppermute | solution.py:631
  30.3 182.6 %all-gather.5.cloned.1.call-start = ((), (), s32[]{:S(2)}) async-start(), calls=%async_computation.7 | async-start | bytes 10444800 | tf_op jit(solution)/shard_map/all_gather | solution.py:667
  32.6 47.0 %collective-permute-start.7 = (bf16[512,1280]{1,0:T(8,128)(2,1)S(1)}, bf16[512,1280]{1,0:T(8,128)(2,1)}, u32[]{:S(2)}, u32[]{:S(2)}) collective-permute-start(bf16[512,1280]{1,0:T(8,128)(2,1)S(1)} %get-tuple-element.84.refs_0_), channel_id=1, source_target_pairs={{0,1},{1,0},{2,3},{3,2},{4,5},{5,4},{6,7},{7,6},{8,9},{9,8},{10,11... | collective-permute-start | bytes 3932168 | tf_op jit(solution)/shard_map/ppermute | solution.py:631
  34.0 58.0 %collective-permute-start.8 = (bf16[512,1280]{1,0:T(8,128)(2,1)S(1)}, bf16[512,1280]{1,0:T(8,128)(2,1)}, u32[]{:S(2)}, u32[]{:S(2)}) collective-permute-start(bf16[512,1280]{1,0:T(8,128)(2,1)S(1)} %get-tuple-element.85.refs_1_), channel_id=1, source_target_pairs={{0,1},{1,0},{2,3},{3,2},{4,5},{5,4},{6,7},{7,6},{8,9},{9,8},{10,11... | collective-permute-start | bytes 3932168 | tf_op jit(solution)/shard_map/ppermute | solution.py:631
  34.7 57.4 %collective-permute-start.9 = (bf16[512,1280]{1,0:T(8,128)(2,1)S(1)}, bf16[512,1280]{1,0:T(8,128)(2,1)}, u32[]{:S(2)}, u32[]{:S(2)}) collective-permute-start(bf16[512,1280]{1,0:T(8,128)(2,1)S(1)} %get-tuple-element.85.refs_1_), channel_id=1, source_target_pairs={{0,4},{1,5},{2,6},{3,7},{4,0},{5,1},{6,2},{7,3},{8,12},{9,13},{10,... | collective-permute-start | bytes 3932168 | tf_op jit(solution)/shard_map/ppermute | solution.py:631
  36.1 37.7 %collective-permute-start.12 = (bf16[512,1280]{1,0:T(8,128)(2,1)S(1)}, bf16[512,1280]{1,0:T(8,128)(2,1)}, u32[]{:S(2)}, u32[]{:S(2)}) collective-permute-start(bf16[512,1280]{1,0:T(8,128)(2,1)S(1)} %get-tuple-element.85.refs_1_), channel_id=1, source_target_pairs={{0,2},{1,3},{2,0},{3,1},{4,6},{5,7},{6,4},{7,5},{8,10},{9,11},{10,... | collective-permute-start | bytes 3932168 | tf_op jit(solution)/shard_map/ppermute | solution.py:631
  40.7 52.8 %collective-permute-start.10 = (bf16[512,1280]{1,0:T(8,128)(2,1)S(1)}, bf16[512,1280]{1,0:T(8,128)(2,1)}, u32[]{:S(2)}, u32[]{:S(2)}) collective-permute-start(bf16[512,1280]{1,0:T(8,128)(2,1)S(1)} %get-tuple-element.84.refs_0_), channel_id=1, source_target_pairs={{0,4},{1,5},{2,6},{3,7},{4,0},{5,1},{6,2},{7,3},{8,12},{9,13},{10,... | collective-permute-start | bytes 3932168 | tf_op jit(solution)/shard_map/ppermute | solution.py:631
  93.5 186.5 %all-gather.7.cloned.1.call-start = ((), (), s32[]{:S(2)}) async-start(), calls=%async_computation.8 | async-start | bytes 10444800 | tf_op jit(solution)/shard_map/all_gather | solution.py:669
  93.8 3.3 collective-permute-start.17
  93.9 7.0 %collective-permute-start.18 = (bf16[512,1280]{1,0:T(8,128)(2,1)}, bf16[512,1280]{1,0:T(8,128)(2,1)S(1)}, u32[]{:S(2)}, u32[]{:S(2)}) collective-permute-start(bf16[512,1280]{1,0:T(8,128)(2,1)} %collective-permute-done.8.refs_1_.refs_5_), channel_id=1, source_target_pairs={{0,2},{1,3},{2,0},{3,1},{4,6},{5,7},{6,4},{7,5},{8,10},{9,11},{10,... | collective-permute-start | bytes 3932168 | tf_op jit(solution)/shard_map/ppermute | solution.py:631
  94.4 15.3 %collective-permute-start.15 = (bf16[512,1280]{1,0:T(8,128)(2,1)}, bf16[512,1280]{1,0:T(8,128)(2,1)}, u32[]{:S(2)}, u32[]{:S(2)}) collective-permute-start(bf16[512,1280]{1,0:T(8,128)(2,1)} %collective-permute-done.10.refs_0_.refs_8_), channel_id=1, source_target_pairs={{0,2},{1,3},{2,0},{3,1},{4,6},{5,7},{6,4},{7,5},{8,10},{9,11},{10,... | collective-permute-start | bytes 3932168 | tf_op jit(solution)/shard_map/ppermute | solution.py:631
  94.5 15.2 %collective-permute-start.16 = (bf16[512,1280]{1,0:T(8,128)(2,1)}, bf16[512,1280]{1,0:T(8,128)(2,1)}, u32[]{:S(2)}, u32[]{:S(2)}) collective-permute-start(bf16[512,1280]{1,0:T(8,128)(2,1)} %collective-permute-done.9.refs_1_.refs_9_), channel_id=1, source_target_pairs={{0,2},{1,3},{2,0},{3,1},{4,6},{5,7},{6,4},{7,5},{8,10},{9,11},{10,... | collective-permute-start | bytes 3932168 | tf_op jit(solution)/shard_map/ppermute | solution.py:631
  94.9 37.7 %collective-permute-start.13 = (bf16[512,1280]{1,0:T(8,128)(2,1)}, bf16[512,1280]{1,0:T(8,128)(2,1)}, u32[]{:S(2)}, u32[]{:S(2)}) collective-permute-start(bf16[512,1280]{1,0:T(8,128)(2,1)} %collective-permute-done.7.refs_0_.refs_4_), channel_id=1, source_target_pairs={{0,4},{1,5},{2,6},{3,7},{4,0},{5,1},{6,2},{7,3},{8,12},{9,13},{10,... | collective-permute-start | bytes 3932168 | tf_op jit(solution)/shard_map/ppermute | solution.py:631
  97.1 35.5 %collective-permute-start.14 = (bf16[512,1280]{1,0:T(8,128)(2,1)}, bf16[512,1280]{1,0:T(8,128)(2,1)}, u32[]{:S(2)}, u32[]{:S(2)}) collective-permute-start(bf16[512,1280]{1,0:T(8,128)(2,1)} %collective-permute-done.9.refs_1_.refs_9_), channel_id=1, source_target_pairs={{0,1},{1,0},{2,3},{3,2},{4,5},{5,4},{6,7},{7,6},{8,9},{9,8},{10,11... | collective-permute-start | bytes 3932168 | tf_op jit(solution)/shard_map/ppermute | solution.py:631
  132.7 3.2 collective-permute-start.19
  132.7 7.0 %collective-permute-start.20 = (bf16[512,1280]{1,0:T(8,128)(2,1)}, bf16[512,1280]{1,0:T(8,128)(2,1)S(1)}, u32[]{:S(2)}, u32[]{:S(2)}) collective-permute-start(bf16[512,1280]{1,0:T(8,128)(2,1)} %collective-permute-done.14.refs_1_.refs_13_), channel_id=1, source_target_pairs={{0,2},{1,3},{2,0},{3,1},{4,6},{5,7},{6,4},{7,5},{8,10},{9,11},{10,... | collective-permute-start | bytes 3932168 | tf_op jit(solution)/shard_map/ppermute | solution.py:631
  176.4 32.2 %all-to-all-start.1 = ((bf16[8,80,1024]{2,1,0:T(8,128)(2,1)}), bf16[8,80,1024]{2,1,0:T(8,128)(2,1)S(1)}, u32[]{:S(2)}, u32[]{:S(2)}) async-start(bf16[8,80,1024]{2,1,0:T(8,128)(2,1)} %get-tuple-element.113.mixed_ref), calls=%async_computation.1 | async-start | bytes 2621440 | tf_op jit(solution)/shard_map/all_to_all | solution.py:691
  208.6 24.3 %all-to-all-start = ((bf16[8,80,1024]{2,1,0:T(8,128)(2,1)}), bf16[8,80,1024]{2,1,0:T(8,128)(2,1)S(1)}, u32[]{:S(2)}, u32[]{:S(2)}) async-start(bf16[8,80,1024]{2,1,0:T(8,128)(2,1)} %get-tuple-element.111.mixed_ref), calls=%async_computation | async-start | bytes 2621440 | tf_op jit(solution)/shard_map/all_to_all | solution.py:691
  212.8 251.1 %reduce-scatter.2.cloned.1.call-start = ((), (), s32[]{:S(2)}) async-start(), calls=%async_computation.9 | async-start | bytes 10444800 | tf_op jit(solution)/shard_map/reduce_scatter | solution.py:746
  280.0 22.1 %all-to-all-start.3 = ((bf16[8,80,1024]{2,1,0:T(8,128)(2,1)}), bf16[8,80,1024]{2,1,0:T(8,128)(2,1)S(1)}, u32[]{:S(2)}, u32[]{:S(2)}) async-start(bf16[8,80,1024]{2,1,0:T(8,128)(2,1)} %bitcast.46), calls=%async_computation.3 | async-start | bytes 2621440 | tf_op jit(solution)/shard_map/all_to_all | solution.py:694
  302.1 54.7 %all-to-all-start.2 = ((bf16[8,80,1024]{2,1,0:T(8,128)(2,1)}), bf16[8,80,1024]{2,1,0:T(8,128)(2,1)S(1)}, u32[]{:S(2)}, u32[]{:S(2)}) async-start(bf16[8,80,1024]{2,1,0:T(8,128)(2,1)} %bitcast.45), calls=%async_computation.2 | async-start | bytes 2621440 | tf_op jit(solution)/shard_map/all_to_all | solution.py:694
  357.9 56.5 %all-to-all-start.4 = ((bf16[8,3,80,1024]{3,2,1,0:T(8,128)(2,1)}), bf16[8,3,80,1024]{3,2,1,0:T(8,128)(2,1)}, u32[]{:S(2)}, u32[]{:S(2)}) async-start(bf16[8,3,80,1024]{3,2,1,0:T(8,128)(2,1)} %get-tuple-element.127.refs_17_), calls=%async_computation.4 | async-start | bytes 7864320 | tf_op jit(solution)/shard_map/all_to_all | solution.py:691
  414.4 51.9 %all-to-all-start.5 = ((bf16[8,3,80,1024]{3,2,1,0:T(8,128)(2,1)}), bf16[8,3,80,1024]{3,2,1,0:T(8,128)(2,1)}, u32[]{:S(2)}, u32[]{:S(2)}) async-start(bf16[8,3,80,1024]{3,2,1,0:T(8,128)(2,1)} %get-tuple-element.136.refs_17_), calls=%async_computation.5 | async-start | bytes 7864320 | tf_op jit(solution)/shard_map/all_to_all | solution.py:691
  446.2 20.1 %collective-permute-start.21 = (bf16[320,240]{1,0:T(8,128)(2,1)S(1)}, bf16[320,240]{1,0:T(8,128)(2,1)S(1)}, u32[]{:S(2)}, u32[]{:S(2)}) collective-permute-start(bf16[320,240]{1,0:T(8,128)(2,1)S(1)} %get-tuple-element.174), channel_id=1, source_target_pairs={{0,8},{8,0},{16,24},{24,16},{1,9},{9,1},{17,25},{25,17},{2,10},{10... | collective-permute-start | bytes 460808 | tf_op jit(solution)/shard_map/ppermute | solution.py:799
  447.9 18.4 %collective-permute-start.22 = (bf16[320,240]{1,0:T(8,128)(2,1)S(1)}, bf16[320,240]{1,0:T(8,128)(2,1)S(1)}, u32[]{:S(2)}, u32[]{:S(2)}) collective-permute-start(bf16[320,240]{1,0:T(8,128)(2,1)S(1)} %get-tuple-element.173), channel_id=1, source_target_pairs={{0,16},{8,24},{16,0},{24,8},{1,17},{9,25},{17,1},{25,9},{2,18},{10... | collective-permute-start | bytes 460808 | tf_op jit(solution)/shard_map/ppermute | solution.py:799
  450.4 15.8 %collective-permute-start.23 = (bf16[320,240]{1,0:T(8,128)(2,1)S(1)}, bf16[320,240]{1,0:T(8,128)(2,1)S(1)}, u32[]{:S(2)}, u32[]{:S(2)}) collective-permute-start(bf16[320,240]{1,0:T(8,128)(2,1)S(1)} %get-tuple-element.172), channel_id=1, source_target_pairs={{0,24},{8,16},{16,8},{24,0},{1,25},{9,17},{17,9},{25,1},{2,26},{10... | collective-permute-start | bytes 460808 | tf_op jit(solution)/shard_map/ppermute | solution.py:799
  466.9 26.5 %collective-permute-start.26 = (bf16[320,240]{1,0:T(8,128)(2,1)S(1)}, bf16[320,240]{1,0:T(8,128)(2,1)S(1)}, u32[]{:S(2)}, u32[]{:S(2)}) collective-permute-start(bf16[320,240]{1,0:T(8,128)(2,1)S(1)} %get-tuple-element.170), channel_id=1, source_target_pairs={{0,24},{8,16},{16,8},{24,0},{1,25},{9,17},{17,9},{25,1},{2,26},{10... | collective-permute-start | bytes 460808 | tf_op jit(solution)/shard_map/ppermute | solution.py:799
  470.6 22.8 %collective-permute-start.25 = (bf16[320,240]{1,0:T(8,128)(2,1)S(1)}, bf16[320,240]{1,0:T(8,128)(2,1)S(1)}, u32[]{:S(2)}, u32[]{:S(2)}) collective-permute-start(bf16[320,240]{1,0:T(8,128)(2,1)S(1)} %get-tuple-element.171), channel_id=1, source_target_pairs={{0,16},{8,24},{16,0},{24,8},{1,17},{9,25},{17,1},{25,9},{2,18},{10... | collective-permute-start | bytes 460808 | tf_op jit(solution)/shard_map/ppermute | solution.py:799
  470.6 22.8 %collective-permute-start.24 = (bf16[320,240]{1,0:T(8,128)(2,1)S(1)}, bf16[320,240]{1,0:T(8,128)(2,1)S(1)}, u32[]{:S(2)}, u32[]{:S(2)}) collective-permute-start(bf16[320,240]{1,0:T(8,128)(2,1)S(1)} %get-tuple-element.169), channel_id=1, source_target_pairs={{0,8},{8,0},{16,24},{24,16},{1,9},{9,1},{17,25},{25,17},{2,10},{10... | collective-permute-start | bytes 460808 | tf_op jit(solution)/shard_map/ppermute | solution.py:799
  471.4 16.9 %collective-permute-start.27 = (f32[5200]{0:T(1024)S(1)}, f32[5200]{0:T(1024)S(1)}, u32[]{:S(2)}, u32[]{:S(2)}) collective-permute-start(f32[5200]{0:T(1024)S(1)} %constant_dynamic-update-slice_fusion), channel_id=1, source_target_pairs={{0,8},{8,0},{16,24},{24,16},{1,9},{9,1},{17,25},{25,17},{2,10},{10... | collective-permute-start | bytes 62408 | tf_op jit(solution)/shard_map/ppermute | solution.py:809
  472.8 20.8 %collective-permute-start.29 = (bf16[3,80,640]{2,1,0:T(8,128)(2,1)S(1)}, bf16[3,80,640]{2,1,0:T(8,128)(2,1)S(1)}, u32[]{:S(2)}, u32[]{:S(2)}) collective-permute-start(bf16[3,80,640]{2,1,0:T(8,128)(2,1)S(1)} %select_bitcast_fusion), channel_id=1, source_target_pairs={{0,1},{1,0},{2,3},{3,2},{4,5},{5,4},{6,7},{7,6},{8,9},{9,8},{10,11... | collective-permute-start | bytes 921608 | tf_op jit(solution)/shard_map/ppermute | solution.py:568
  488.3 5.1 collective-permute-start.28
  493.7 3.3 collective-permute-start.30
  494.4 7.1 %collective-permute-start.34 = (bf16[80,480]{1,0:T(8,128)(2,1)S(1)}, bf16[80,480]{1,0:T(8,128)(2,1)S(1)}, u32[]{:S(2)}, u32[]{:S(2)}) collective-permute-start(bf16[80,480]{1,0:T(8,128)(2,1)S(1)} %bitcast.234), channel_id=1, source_target_pairs={{0,6},{2,4},{4,2},{6,0},{1,7},{3,5},{5,3},{7,1},{8,14},{10,12},{12... | collective-permute-start | bytes 230408 | tf_op jit(solution)/shard_map/ppermute | solution.py:584
  496.2 5.3 %collective-permute-start.33 = (bf16[80,480]{1,0:T(8,128)(2,1)S(1)}, bf16[80,480]{1,0:T(8,128)(2,1)S(1)}, u32[]{:S(2)}, u32[]{:S(2)}) collective-permute-start(bf16[80,480]{1,0:T(8,128)(2,1)S(1)} %bitcast.235), channel_id=1, source_target_pairs={{0,4},{2,6},{4,0},{6,2},{1,5},{3,7},{5,1},{7,3},{8,12},{10,14},{12... | collective-permute-start | bytes 230408 | tf_op jit(solution)/shard_map/ppermute | solution.py:584
  496.9 4.6 collective-permute-start.32
  497.0 4.5 collective-permute-start.31
  502.1 3.9 collective-permute-start.35
  (41 other events, 240.7 us)
Sparse Core Ops, SparseCore 0:
  30.4 33.8 all-gather.8
  93.6 88.2 all-gather.4
  184.2 91.3 all-gather.6
  280.2 142.5 reduce-scatter.1
